TPU v7x, 32 devices: a whole 2x2x4 slice. The times are simulated.
32 devices in a mesh: parts: 2 (over x), ctx: 16 (over z, y, core).
Axes of the slice: x: 2, y: 2, z: 4, core: 2. Of those that a mesh axis runs over, the one named last changes fastest.
Arguments:
- queries: bfloat16 [8192, 2048], P(('parts', 'ctx')), parts along dimension 0, may hold values from -6 to 6
- key_vectors: bfloat16 [8192, 2048], P(('parts', 'ctx')), parts along dimension 0, may hold values from -6 to 6
- value_vectors: bfloat16 [8192, 2048], P(('parts', 'ctx')), parts along dimension 0, may hold values from -6 to 6
- out_grad: bfloat16 [8192, 2048], P(('parts', 'ctx')), parts along dimension 0, may hold values from -6 to 6
- norm_gain: float32 [2048], replicated, may hold values from 0.5 to 1.5
- doc_bounds: int32 [2, 64], P(None, ('parts', 'ctx')), parts along dimension 1, may hold values from 0 to 31, as said below
Outputs:
- query_grad: bfloat16 [8192, 2048], P(('parts', 'ctx')), parts along dimension 0
- key_grad: bfloat16 [8192, 2048], P(('parts', 'ctx')), parts along dimension 0
- value_grad: bfloat16 [8192, 2048], P(('parts', 'ctx')), parts along dimension 0
- gain_grad: float32 [4096], P('parts'), parts along dimension 0
There are 2 independent parts, one for each index of `parts`. A program takes and returns all parts, laid end to end along the dimension named above; an argument that names none is the same for every part. Nothing has to cross between parts.
Inputs may be any that keep to these rules, and one draw needn't show every extreme that they name: doc_bounds[0, b] and doc_bounds[1, b] are the first and last block of the document that holds block b; documents are runs of whole blocks of 128 tokens covering the sequence in order, and block 0 starts one.
All inputs are finite; a program needn't handle non-finite values.
Results may differ from a plain program's by a relative error of at most 0.011.
Values sent between devices are 32-bit elements; how exact they have to be, the bound alone decides.
No kernel may reach another device: no remote copies, remote signals or barrier semaphores. Data moves between devices by JAX's collectives and lax.ppermute only.
A program may use at most 64 MiB of HBM per device.

v0:
```python
import math

import jax
import jax.numpy as jnp
from jax import lax
from jax.sharding import PartitionSpec as P

E = 128
H = 16


epsilon = 1e-06


def from_behind(block, axis, distance):
    devices = range(lax.axis_size(axis))
    route = [(i - distance, i) for i in devices if i - distance in devices]
    return lax.ppermute(block, axis, route)


def combine_states(earlier, later):
    return (jnp.maximum(earlier[0], later[0]), later[1] + (1.0 - later[0]) * earlier[1])


def distances(count):
    result = [1]
    spread = 1
    while spread < count:
        result.append(spread)
        spread = spread * 2
    return result


def forward_doubling(pair):
    count = lax.axis_size("ctx")
    current = pair
    for order, spread in enumerate(distances(count)):
        moved = from_behind(current, "ctx", spread)
        current = moved if order == 0 else combine_states(moved, current)
    return current


def backward_doubling(pair):
    count = lax.axis_size("ctx")
    current = pair
    for order, spread in enumerate(distances(count)):
        moved = from_behind(current, "ctx", -spread)
        current = moved if order == 0 else combine_states(moved, current)
    return current


def shards(queries, key_vectors, value_vectors, out_grad, norm_gain, doc_bounds):
    tok_count = queries.shape[0]
    block_count = doc_bounds.shape[1]
    block_len = tok_count // block_count
    dev_first = lax.axis_index("ctx") * block_count
    doc_first = jnp.repeat(doc_bounds[0], block_len)
    doc_last = jnp.repeat(doc_bounds[1], block_len)
    positions = jnp.arange(tok_count, dtype=jnp.int32)
    causal_mask = (doc_first[:, None] == doc_first[None, :]) & (
        positions[None, :] <= positions[:, None]
    )
    use_carry = (doc_first < dev_first)[:, None, None]
    tail_rows = (doc_last >= dev_first + block_count - 1)[:, None, None]
    reset_flag = (doc_bounds[0, block_count - 1] >= dev_first).astype(jnp.float32)
    query_part = queries.reshape(tok_count, H, E)
    key_part = key_vectors.reshape(tok_count, H, E)
    value_part = value_vectors.reshape(tok_count, H, E)
    grad_float = out_grad.reshape(tok_count, H, E).astype(jnp.float32)
    gain_heads = norm_gain.reshape(H, E)
    key_tail = jnp.where(tail_rows, key_part, jnp.zeros_like(key_part))
    state_part = jnp.einsum(
        "jhe,jhf->hef", key_tail, value_part, preferred_element_type=jnp.float32
    )
    carried = forward_doubling((reset_flag, state_part))[1]
    raw_scores = jnp.einsum(
        "ihe,jhe->hij", query_part, key_part, preferred_element_type=jnp.float32
    )
    scores_b = jnp.where(causal_mask[None], raw_scores, 0.0).astype(jnp.bfloat16)
    local_out = jnp.einsum("hij,jhe->ihe", scores_b, value_part, preferred_element_type=jnp.float32)
    carried_b = carried.astype(jnp.bfloat16)
    from_carry = jnp.einsum(
        "ihe,hef->ihf", query_part, carried_b, preferred_element_type=jnp.float32
    )
    attended = local_out + jnp.where(use_carry, from_carry, 0.0)
    root = jnp.sqrt(jnp.mean(attended * attended, axis=-1, keepdims=True) + epsilon)
    normed = attended / root
    gain_local = jnp.sum(grad_float * normed, axis=0).reshape(H * E)
    dnormed = grad_float * gain_heads
    d_att = ((dnormed - normed * jnp.mean(dnormed * normed, axis=-1, keepdims=True)) / root).astype(
        jnp.bfloat16
    )
    query_used = jnp.where(use_carry, query_part, jnp.zeros_like(query_part))
    grad_state = jnp.einsum("ihe,ihf->hef", query_used, d_att, preferred_element_type=jnp.float32)
    later = backward_doubling((reset_flag, grad_state))[1]
    later_b = later.astype(jnp.bfloat16)
    raw_dscores = jnp.einsum("ihe,jhe->hij", d_att, value_part, preferred_element_type=jnp.float32)
    dscores_b = jnp.where(causal_mask[None], raw_dscores, 0.0).astype(jnp.bfloat16)
    query_grad = jnp.einsum(
        "hij,jhe->ihe", dscores_b, key_part, preferred_element_type=jnp.float32
    ) + jnp.where(
        use_carry,
        jnp.einsum("ihf,hef->ihe", d_att, carried_b, preferred_element_type=jnp.float32),
        0.0,
    )
    key_grad = jnp.einsum(
        "hij,ihe->jhe", dscores_b, query_part, preferred_element_type=jnp.float32
    ) + jnp.where(
        tail_rows,
        jnp.einsum("jhf,hef->jhe", value_part, later_b, preferred_element_type=jnp.float32),
        0.0,
    )
    value_grad = jnp.einsum(
        "hij,ihe->jhe", scores_b, d_att, preferred_element_type=jnp.float32
    ) + jnp.where(
        tail_rows,
        jnp.einsum("jhe,hef->jhf", key_part, later_b, preferred_element_type=jnp.float32),
        0.0,
    )
    gain_grad = lax.psum(gain_local, "ctx") / math.sqrt(tok_count * lax.axis_size("ctx"))
    width = H * E
    return (
        query_grad.reshape(tok_count, width).astype(jnp.bfloat16),
        key_grad.reshape(tok_count, width).astype(jnp.bfloat16),
        value_grad.reshape(tok_count, width).astype(jnp.bfloat16),
        gain_grad,
    )


def solution(mesh):
    return jax.shard_map(
        shards,
        mesh=mesh,
        in_specs=(
            P(("parts", "ctx"), None),
            P(("parts", "ctx"), None),
            P(("parts", "ctx"), None),
            P(("parts", "ctx"), None),
            P(),
            P(None, ("parts", "ctx")),
        ),
        out_specs=(
            P(("parts", "ctx"), None),
            P(("parts", "ctx"), None),
            P(("parts", "ctx"), None),
            P("parts"),
        ),
        check_vma=False,
    )
```

profile of v0, /device:TPU:16, one launch (start us, length us, event | category | flops | bytes accessed | tf_op | source)
XLA Modules:
  0.0 333.5 jit_solution(8816836569707186097)
XLA Ops:
  6.1 15.1 %collective-permute-done = f32[16,128,128]{2,1,0:T(8,128)S(1)} collective-permute-done((f32[16,128,128]{2,1,0:T(8,128)S(1)}, f32[16,128,128]{2,1,0:T(8,128)S(1)}, u32[]{:S(2)}, u32[]{:S(2)}) %collective-permute-start) | collective-permute-done | bytes 1048608 | tf_op jit(solution)/shard_map/ppermute | solution.py:18
  24.4 3.6 %collective-permute-start.1 = (f32[]{:T(128)}, f32[]{:T(128)}, u32[]{:S(2)}, u32[]{:S(2)}) collective-permute-start(f32[]{:T(128)} %convert_element_type.48), channel_id=1, source_target_pairs={{0,1},{1,2},{2,3},{3,4},{4,5},{5,6},{6,7},{7,8},{8,9},{9,10},{10,1... | collective-permute-start | bytes 20 | tf_op jit(solution)/shard_map/ppermute | solution.py:18
  28.0 10.4 %collective-permute-done.1 = f32[]{:T(128)} collective-permute-done((f32[]{:T(128)}, f32[]{:T(128)}, u32[]{:S(2)}, u32[]{:S(2)}) %collective-permute-start.1) | collective-permute-done | bytes 36 | tf_op jit(solution)/shard_map/ppermute | solution.py:18
  42.6 2.1 collective-permute-start.3
  44.7 17.4 %collective-permute-done.3 = f32[]{:T(128)} collective-permute-done((f32[]{:T(128)}, f32[]{:T(128)}, u32[]{:S(2)}, u32[]{:S(2)}) %collective-permute-start.3) | collective-permute-done | bytes 36 | tf_op jit(solution)/shard_map/ppermute | solution.py:18
  63.2 2.7 collective-permute-done.4
  65.9 2.3 multiply_add_fusion.4
  68.2 3.5 %collective-permute-start.6 = (f32[16,128,128]{2,1,0:T(8,128)}, f32[16,128,128]{2,1,0:T(8,128)}, u32[]{:S(2)}, u32[]{:S(2)}) collective-permute-start(f32[16,128,128]{2,1,0:T(8,128)} %multiply_add_fusion.4), channel_id=1, source_target_pairs={{0,4},{1,5},{2,6},{3,7},{4,8},{5,9},{6,10},{7,11},{8,12},{9,13},{1... | collective-permute-start | bytes 3145736 | tf_op jit(solution)/shard_map/ppermute | solution.py:18
  74.5 3.2 collective-permute-start.5
  77.7 17.4 %collective-permute-done.5 = f32[]{:T(128)} collective-permute-done((f32[]{:T(128)}, f32[]{:T(128)}, u32[]{:S(2)}, u32[]{:S(2)}) %collective-permute-start.5) | collective-permute-done | bytes 36 | tf_op jit(solution)/shard_map/ppermute | solution.py:18
  95.7 2.8 multiply_add_fusion.3
  100.8 2.2 fusion.2
  102.9 3.5 %collective-permute-start.7 = (f32[]{:T(128)}, f32[]{:T(128)}, u32[]{:S(2)}, u32[]{:S(2)}) collective-permute-start(f32[]{:T(128)} %max.19), channel_id=1, source_target_pairs={{0,4},{1,5},{2,6},{3,7},{4,8},{5,9},{6,10},{7,11},{8,12},{9,13},{1... | collective-permute-start | bytes 20 | tf_op jit(solution)/shard_map/ppermute | solution.py:18
  106.4 39.0 %collective-permute-done.7 = f32[]{:T(128)} collective-permute-done((f32[]{:T(128)}, f32[]{:T(128)}, u32[]{:S(2)}, u32[]{:S(2)}) %collective-permute-start.7) | collective-permute-done | bytes 36 | tf_op jit(solution)/shard_map/ppermute | solution.py:18
  147.9 2.4 multiply_reduce_fusion.2
  155.1 12.3 %collective-permute-done.9 = f32[16,128,128]{2,1,0:T(8,128)S(1)} collective-permute-done((f32[16,128,128]{2,1,0:T(8,128)S(1)}, f32[16,128,128]{2,1,0:T(8,128)S(1)}, u32[]{:S(2)}, u32[]{:S(2)}) %collective-permute-start.9) | collective-permute-done | bytes 1048608 | tf_op jit(solution)/shard_map/ppermute | solution.py:18
  167.4 4.7 %collective-permute-start.11 = (f32[16,128,128]{2,1,0:T(8,128)S(1)}, f32[16,128,128]{2,1,0:T(8,128)}, u32[]{:S(2)}, u32[]{:S(2)}) collective-permute-start(f32[16,128,128]{2,1,0:T(8,128)S(1)} %collective-permute-done.9), channel_id=1, source_target_pairs={{1,0},{2,1},{3,2},{4,3},{5,4},{6,5},{7,6},{8,7},{9,8},{10,9},{11,1... | collective-permute-start | bytes 3145736 | tf_op jit(solution)/shard_map/ppermute | solution.py:18
  172.1 12.3 %collective-permute-start.10 = (f32[]{:T(128)}, f32[]{:T(128)}, u32[]{:S(2)}, u32[]{:S(2)}) collective-permute-start(f32[]{:T(128)} %convert_element_type.48), channel_id=1, source_target_pairs={{1,0},{2,1},{3,2},{4,3},{5,4},{6,5},{7,6},{8,7},{9,8},{10,9},{11,1... | collective-permute-start | bytes 20 | tf_op jit(solution)/shard_map/ppermute | solution.py:18
  186.5 2.1 collective-permute-start.13
  188.6 4.8 %collective-permute-start.12 = (f32[]{:T(128)}, f32[]{:T(128)}, u32[]{:S(2)}, u32[]{:S(2)}) collective-permute-start(f32[]{:T(128)} %collective-permute-done.10), channel_id=1, source_target_pairs={{1,0},{2,1},{3,2},{4,3},{5,4},{6,5},{7,6},{8,7},{9,8},{10,9},{11,1... | collective-permute-start | bytes 20 | tf_op jit(solution)/shard_map/ppermute | solution.py:18
  193.4 16.3 %collective-permute-done.12 = f32[]{:T(128)} collective-permute-done((f32[]{:T(128)}, f32[]{:T(128)}, u32[]{:S(2)}, u32[]{:S(2)}) %collective-permute-start.12) | collective-permute-done | bytes 36 | tf_op jit(solution)/shard_map/ppermute | solution.py:18
  211.0 3.7 %collective-permute-done.13 = f32[16,128,128]{2,1,0:T(8,128)} collective-permute-done((f32[16,128,128]{2,1,0:T(8,128)S(1)}, f32[16,128,128]{2,1,0:T(8,128)}, u32[]{:S(2)}, u32[]{:S(2)}) %collective-permute-start.13) | collective-permute-done | bytes 1048608 | tf_op jit(solution)/shard_map/ppermute | solution.py:18
  218.2 22.9 %collective-permute-start.14 = (f32[]{:T(128)}, f32[]{:T(128)}, u32[]{:S(2)}, u32[]{:S(2)}) collective-permute-start(f32[]{:T(128)} %max.21), channel_id=1, source_target_pairs={{2,0},{3,1},{4,2},{5,3},{6,4},{7,5},{8,6},{9,7},{10,8},{11,9},{12,... | collective-permute-start | bytes 20 | tf_op jit(solution)/shard_map/ppermute | solution.py:18
  241.8 3.2 collective-permute-start.16
  245.0 2.3 collective-permute-done.16
  250.4 2.4 multiply_add_fusion
  252.8 2.3 collective-permute-start.17
  257.0 62.5 %psum.7 = f32[2048]{0:T(1024)S(1)} all-reduce(f32[2048]{0:T(1024)S(1)} %bitcast.101), channel_id=1, replica_groups=mesh['parts'=2,'ctx'=16] {'ctx'}, use_global_device_ids=true, to_apply=%region_3.4 | all-reduce | flops 2048 | bytes 16384 | tf_op jit(solution)/shard_map/psum | solution.py:120
  320.1 2.2 fusion.27
  326.5 2.3 copy.30
  328.7 2.5 fusion
  331.2 2.3 copy.29
  (86 shorter events, 37.3 us)
Async XLA Ops:
  0.6 3.1 copy-start
  3.8 36.9 %copy-start.14 = (bf16[256,16,128]{0,2,1:T(8,128)(2,1)}, bf16[256,16,128]{0,2,1:T(8,128)(2,1)S(1)}, u32[]{:S(2)}) copy-start(bf16[256,16,128]{0,2,1:T(8,128)(2,1)S(1)} %copy.14) | copy-start | bytes 3145732
  3.8 19.4 %copy-start.20 = (s32[2,2]{1,0:T(2,128)S(1)}, s32[2,2]{1,0:T(2,128)}, u32[]{:S(2)}) copy-start(s32[2,2]{1,0:T(2,128)} %param.11) | copy-start | bytes 52
  4.2 17.0 %collective-permute-start = (f32[16,128,128]{2,1,0:T(8,128)S(1)}, f32[16,128,128]{2,1,0:T(8,128)S(1)}, u32[]{:S(2)}, u32[]{:S(2)}) collective-permute-start(f32[16,128,128]{2,1,0:T(8,128)S(1)} %fusion.6), channel_id=1, source_target_pairs={{0,1},{1,2},{2,3},{3,4},{4,5},{5,6},{6,7},{7,8},{8,9},{9,10},{10,1... | collective-permute-start | bytes 3145736 | tf_op jit(solution)/shard_map/ppermute | solution.py:18
  21.2 17.7 %copy-start.18 = (f32[16,128,128]{2,1,0:T(8,128)}, f32[16,128,128]{2,1,0:T(8,128)S(1)}, u32[]{:S(2)}) copy-start(f32[16,128,128]{2,1,0:T(8,128)S(1)} %collective-permute-done) | copy-start | bytes 3145732
  21.2 17.7 %collective-permute-start.2 = (f32[16,128,128]{2,1,0:T(8,128)S(1)}, f32[16,128,128]{2,1,0:T(8,128)}, u32[]{:S(2)}, u32[]{:S(2)}) collective-permute-start(f32[16,128,128]{2,1,0:T(8,128)S(1)} %collective-permute-done), channel_id=1, source_target_pairs={{0,1},{1,2},{2,3},{3,4},{4,5},{5,6},{6,7},{7,8},{8,9},{9,10},{10,1... | collective-permute-start | bytes 3145736 | tf_op jit(solution)/shard_map/ppermute | solution.py:18
  24.4 14.0 %collective-permute-start.1 = (f32[]{:T(128)}, f32[]{:T(128)}, u32[]{:S(2)}, u32[]{:S(2)}) collective-permute-start(f32[]{:T(128)} %convert_element_type.48), channel_id=1, source_target_pairs={{0,1},{1,2},{2,3},{3,4},{4,5},{5,6},{6,7},{7,8},{8,9},{9,10},{10,1... | collective-permute-start | bytes 20 | tf_op jit(solution)/shard_map/ppermute | solution.py:18
  40.7 25.2 %collective-permute-start.4 = (f32[16,128,128]{2,1,0:T(8,128)S(1)}, f32[16,128,128]{2,1,0:T(8,128)}, u32[]{:S(2)}, u32[]{:S(2)}) collective-permute-start(f32[16,128,128]{2,1,0:T(8,128)S(1)} %multiply_add_fusion.5), channel_id=1, source_target_pairs={{0,2},{1,3},{2,4},{3,5},{4,6},{5,7},{6,8},{7,9},{8,10},{9,11},{10,... | collective-permute-start | bytes 3145736 | tf_op jit(solution)/shard_map/ppermute | solution.py:18
  42.6 29.1 %copy-start.17 = (bf16[256,2048]{1,0:T(8,128)(2,1)S(1)}, bf16[256,2048]{1,0:T(8,128)(2,1)}, u32[]{:S(2)}) copy-start(bf16[256,2048]{1,0:T(8,128)(2,1)} %param.6) | copy-start | bytes 3145732
  42.6 19.4 %collective-permute-start.3 = (f32[]{:T(128)}, f32[]{:T(128)}, u32[]{:S(2)}, u32[]{:S(2)}) collective-permute-start(f32[]{:T(128)} %collective-permute-done.1), channel_id=1, source_target_pairs={{0,1},{1,2},{2,3},{3,4},{4,5},{5,6},{6,7},{7,8},{8,9},{9,10},{10,1... | collective-permute-start | bytes 20 | tf_op jit(solution)/shard_map/ppermute | solution.py:18
  68.2 27.5 %collective-permute-start.6 = (f32[16,128,128]{2,1,0:T(8,128)}, f32[16,128,128]{2,1,0:T(8,128)}, u32[]{:S(2)}, u32[]{:S(2)}) collective-permute-start(f32[16,128,128]{2,1,0:T(8,128)} %multiply_add_fusion.4), channel_id=1, source_target_pairs={{0,4},{1,5},{2,6},{3,7},{4,8},{5,9},{6,10},{7,11},{8,12},{9,13},{1... | collective-permute-start | bytes 3145736 | tf_op jit(solution)/shard_map/ppermute | solution.py:18
  74.5 20.6 %collective-permute-start.5 = (f32[]{:T(128)}, f32[]{:T(128)}, u32[]{:S(2)}, u32[]{:S(2)}) collective-permute-start(f32[]{:T(128)} %max.18), channel_id=1, source_target_pairs={{0,2},{1,3},{2,4},{3,5},{4,6},{5,7},{6,8},{7,9},{8,10},{9,11},{10,... | collective-permute-start | bytes 20 | tf_op jit(solution)/shard_map/ppermute | solution.py:18
  95.7 4.3 %copy-start.3 = (bf16[256,2048]{0,1:T(8,128)(2,1)S(1)}, bf16[256,2048]{0,1:T(8,128)(2,1)}, u32[]{:S(2)}) copy-start(bf16[256,2048]{0,1:T(8,128)(2,1)} %copy.36) | copy-start | bytes 3145732
  95.7 4.3 %copy-start.12 = (bf16[256,2048]{1,0:T(8,128)(2,1)S(1)}, bf16[256,2048]{1,0:T(8,128)(2,1)}, u32[]{:S(2)}) copy-start(bf16[256,2048]{1,0:T(8,128)(2,1)} %param.7) | copy-start | bytes 3145732
  98.5 47.6 %collective-permute-start.8 = (f32[16,128,128]{2,1,0:T(8,128)}, f32[16,128,128]{2,1,0:T(8,128)}, u32[]{:S(2)}, u32[]{:S(2)}) collective-permute-start(f32[16,128,128]{2,1,0:T(8,128)} %multiply_add_fusion.3), channel_id=1, source_target_pairs={{0,8},{1,9},{2,10},{3,11},{4,12},{5,13},{6,14},{7,15},{16,24},{17,... | collective-permute-start | bytes 3145736 | tf_op jit(solution)/shard_map/ppermute | solution.py:18
  102.9 42.5 %collective-permute-start.7 = (f32[]{:T(128)}, f32[]{:T(128)}, u32[]{:S(2)}, u32[]{:S(2)}) collective-permute-start(f32[]{:T(128)} %max.19), channel_id=1, source_target_pairs={{0,4},{1,5},{2,6},{3,7},{4,8},{5,9},{6,10},{7,11},{8,12},{9,13},{1... | collective-permute-start | bytes 20 | tf_op jit(solution)/shard_map/ppermute | solution.py:18
  147.9 2.4 copy-start.9
  147.9 2.4 copy-start.19
  153.2 14.2 %collective-permute-start.9 = (f32[16,128,128]{2,1,0:T(8,128)S(1)}, f32[16,128,128]{2,1,0:T(8,128)S(1)}, u32[]{:S(2)}, u32[]{:S(2)}) collective-permute-start(f32[16,128,128]{2,1,0:T(8,128)S(1)} %fusion.10), channel_id=1, source_target_pairs={{1,0},{2,1},{3,2},{4,3},{5,4},{6,5},{7,6},{8,7},{9,8},{10,9},{11,1... | collective-permute-start | bytes 3145736 | tf_op jit(solution)/shard_map/ppermute | solution.py:18
  167.4 17.7 %collective-permute-start.11 = (f32[16,128,128]{2,1,0:T(8,128)S(1)}, f32[16,128,128]{2,1,0:T(8,128)}, u32[]{:S(2)}, u32[]{:S(2)}) collective-permute-start(f32[16,128,128]{2,1,0:T(8,128)S(1)} %collective-permute-done.9), channel_id=1, source_target_pairs={{1,0},{2,1},{3,2},{4,3},{5,4},{6,5},{7,6},{8,7},{9,8},{10,9},{11,1... | collective-permute-start | bytes 3145736 | tf_op jit(solution)/shard_map/ppermute | solution.py:18
  172.1 12.3 %collective-permute-start.10 = (f32[]{:T(128)}, f32[]{:T(128)}, u32[]{:S(2)}, u32[]{:S(2)}) collective-permute-start(f32[]{:T(128)} %convert_element_type.48), channel_id=1, source_target_pairs={{1,0},{2,1},{3,2},{4,3},{5,4},{6,5},{7,6},{8,7},{9,8},{10,9},{11,1... | collective-permute-start | bytes 20 | tf_op jit(solution)/shard_map/ppermute | solution.py:18
  186.5 24.5 %copy-start.16 = (f32[16,128,128]{2,1,0:T(8,128)}, f32[16,128,128]{2,1,0:T(8,128)S(1)}, u32[]{:S(2)}) copy-start(f32[16,128,128]{2,1,0:T(8,128)S(1)} %multiply_add_fusion.2) | copy-start | bytes 3145732
  186.5 61.4 %copy-start.2 = (bf16[256,16,128]{0,2,1:T(8,128)(2,1)S(1)}, bf16[256,16,128]{0,2,1:T(8,128)(2,1)}, u32[]{:S(2)}) copy-start(bf16[256,16,128]{0,2,1:T(8,128)(2,1)} %copy-done.1) | copy-start | bytes 3145732
  186.5 28.1 %collective-permute-start.13 = (f32[16,128,128]{2,1,0:T(8,128)S(1)}, f32[16,128,128]{2,1,0:T(8,128)}, u32[]{:S(2)}, u32[]{:S(2)}) collective-permute-start(f32[16,128,128]{2,1,0:T(8,128)S(1)} %multiply_add_fusion.2), channel_id=1, source_target_pairs={{2,0},{3,1},{4,2},{5,3},{6,4},{7,5},{8,6},{9,7},{10,8},{11,9},{12,... | collective-permute-start | bytes 3145736 | tf_op jit(solution)/shard_map/ppermute | solution.py:18
  188.6 21.2 %collective-permute-start.12 = (f32[]{:T(128)}, f32[]{:T(128)}, u32[]{:S(2)}, u32[]{:S(2)}) collective-permute-start(f32[]{:T(128)} %collective-permute-done.10), channel_id=1, source_target_pairs={{1,0},{2,1},{3,2},{4,3},{5,4},{6,5},{7,6},{8,7},{9,8},{10,9},{11,1... | collective-permute-start | bytes 20 | tf_op jit(solution)/shard_map/ppermute | solution.py:18
  216.3 34.1 %collective-permute-start.15 = (f32[16,128,128]{2,1,0:T(8,128)S(1)}, f32[16,128,128]{2,1,0:T(8,128)}, u32[]{:S(2)}, u32[]{:S(2)}) collective-permute-start(f32[16,128,128]{2,1,0:T(8,128)S(1)} %multiply_add_fusion.1), channel_id=1, source_target_pairs={{4,0},{5,1},{6,2},{7,3},{8,4},{9,5},{10,6},{11,7},{12,8},{13,9},{1... | collective-permute-start | bytes 3145736 | tf_op jit(solution)/shard_map/ppermute | solution.py:18
  218.2 23.0 %collective-permute-start.14 = (f32[]{:T(128)}, f32[]{:T(128)}, u32[]{:S(2)}, u32[]{:S(2)}) collective-permute-start(f32[]{:T(128)} %max.21), channel_id=1, source_target_pairs={{2,0},{3,1},{4,2},{5,3},{6,4},{7,5},{8,6},{9,7},{10,8},{11,9},{12,... | collective-permute-start | bytes 20 | tf_op jit(solution)/shard_map/ppermute | solution.py:18
  241.8 5.5 %collective-permute-start.16 = (f32[]{:T(128)}, f32[]{:T(128)}, u32[]{:S(2)}, u32[]{:S(2)}) collective-permute-start(f32[]{:T(128)} %max.22), channel_id=1, source_target_pairs={{4,0},{5,1},{6,2},{7,3},{8,4},{9,5},{10,6},{11,7},{12,8},{13,9},{1... | collective-permute-start | bytes 20 | tf_op jit(solution)/shard_map/ppermute | solution.py:18
  250.4 4.7 %copy-start.10 = (bf16[16,128,128]{2,1,0:T(8,128)(2,1)S(1)}, bf16[16,128,128]{2,1,0:T(8,128)(2,1)}, u32[]{:S(2)}) copy-start(bf16[16,128,128]{2,1,0:T(8,128)(2,1)} %copy-done.9) | copy-start | bytes 1572868
  252.8 70.3 %collective-permute-start.17 = (f32[16,128,128]{2,1,0:T(8,128)}, f32[16,128,128]{2,1,0:T(8,128)}, u32[]{:S(2)}, u32[]{:S(2)}) collective-permute-start(f32[16,128,128]{2,1,0:T(8,128)} %multiply_add_fusion), channel_id=1, source_target_pairs={{8,0},{9,1},{10,2},{11,3},{12,4},{13,5},{14,6},{15,7},{24,16},{25,... | collective-permute-start | bytes 3145736 | tf_op jit(solution)/shard_map/ppermute | solution.py:18
  320.1 2.2 copy-start.5
  320.1 2.5 copy-start.8
  (7 other events, 10.9 us)
where the time goes:
time: 335 us; the launch traced here: 333 us
  waiting for transfers between devices  137 us (41%)
  starting transfers between devices  79 us (24%)
  blocking collectives  62.5 us (19%)
  other arithmetic  18.6 us (6%)
  matrix products  14.8 us (4%)
  local copies, waits for them, and re-layouts  14.2 us (4%)
  between operations  7.73 us (2%)
    ppermute x18, waiting for transfers between devices, from_behind(): return lax.ppermute(block, axis, route)  137 us
    ppermute x18, starting transfers between devices, from_behind(): return lax.ppermute(block, axis, route)  79 us
    psum x1, blocking collectives, shards(): lax.psum(gain_local, 'ctx') / math.sqrt(tok_count * lax.axis_size('ctx'))  62.5 us
    add x6, other arithmetic, combine_states(): later[1] + (1.0 - later[0]) * earlier[1]  12.1 us
    unnamed x46, local copies, waits for them, and re-layouts  9.86 us
  transfers between devices with their start and end apart: 18, of which 10 were waited for; matrix products, arithmetic and copies ran while one was open for 4% of the time, Pallas kernels for 0%

commit v1 on v0

v1 whole, which is shorter than its diff:
```python
import functools
import math

import jax
import jax.numpy as jnp
from jax import lax
from jax.experimental import pallas as pl
from jax.experimental.pallas import tpu as pltpu
from jax.sharding import PartitionSpec as P

E = 128
PAIR = 2 * E
FLAG = 8
EPS = 1e-06
F32 = jnp.float32
BF16 = jnp.bfloat16


def dot(a, b, a_dim, b_dim):
    return lax.dot_general(a, b, (((a_dim,), (b_dim,)), ((), ())), preferred_element_type=F32)


def row_values(values, rows, block_len):
    position = lax.broadcasted_iota(jnp.int32, (rows, E), 0)
    result = jnp.full((rows, E), values[0], values[0].dtype)
    for block in range(1, len(values)):
        result = jnp.where(position >= block * block_len, values[block], result)
    return result


def flags(bounds, block_count):
    first = lax.axis_index("ctx") * block_count
    use = [(bounds[0, b] < first).astype(F32) for b in range(block_count)]
    tail = [(bounds[1, b] >= first + block_count - 1).astype(F32) for b in range(block_count)]
    reset = (bounds[0, block_count - 1] >= first).astype(F32)
    return use, tail, reset


def place(step, pairs):
    y_bit = (lax.axis_index("ctx") // 2) % 2
    slot = ((step % 2) ^ y_bit) * (pairs // 2) + step // 2
    return pl.ds(pl.multiple_of(slot * E, E), E)


def state_kernel(bounds, k_ref, v_ref, keep_ref, send_ref, tail_ref, *, block_count, pairs):
    step = pl.program_id(0)
    rows = k_ref.shape[0]
    core = lax.axis_index("ctx") % 2

    @pl.when(step == 0)
    def _():
        _, tail, reset = flags(bounds, block_count)
        tail_ref[...] = row_values(tail, rows, rows // block_count).astype(BF16)
        send_ref[pairs * E :, :] = jnp.full((FLAG, E), reset, F32)

    tail_rows = tail_ref[...]
    states = []
    for half in range(2):
        columns = slice(half * E, (half + 1) * E)
        states.append(dot(k_ref[:, columns] * tail_rows, v_ref[:, columns], 0, 0))
    where = place(step, pairs)
    keep_ref[where, :] = jnp.where(core == 0, states[0], states[1])
    send_ref[where, :] = jnp.where(core == 0, states[1], states[0])


def main_kernel(
    bounds, q_ref, k_ref, v_ref, g_ref, gain_ref, kept_ref, got_ref,
    qg_ref, kp_ref, vp_ref, keep_ref, send_ref, mask_ref, use_ref,
    *, block_count, pairs,
):
    step = pl.program_id(0)
    rows = q_ref.shape[0]
    core = lax.axis_index("ctx") % 2

    @pl.when(step == 0)
    def _():
        use, _, reset = flags(bounds, block_count)
        block_len = rows // block_count
        use_ref[...] = row_values(use, rows, block_len).astype(BF16)
        row = lax.broadcasted_iota(jnp.int32, (rows, rows), 0)
        column = lax.broadcasted_iota(jnp.int32, (rows, rows), 1)
        row_doc = jnp.full((rows, rows), bounds[0, 0], jnp.int32)
        column_doc = row_doc
        for block in range(1, block_count):
            row_doc = jnp.where(row >= block * block_len, bounds[0, block], row_doc)
            column_doc = jnp.where(column >= block * block_len, bounds[0, block], column_doc)
        seen = (row_doc == column_doc) & (column <= row)
        mask_ref[...] = jnp.where(seen, 1.0, 0.0).astype(BF16)
        send_ref[pairs * E : pairs * E + FLAG, :] = jnp.full((FLAG, E), reset, F32)

    where = place(step, pairs)
    kept, got = kept_ref[where, :], got_ref[where, :]
    carries = (
        jnp.where(core == 0, kept, got).astype(BF16),
        jnp.where(core == 0, got, kept).astype(BF16),
    )
    use_rows = use_ref[...]
    states = []
    for half in range(2):
        columns = slice(half * E, (half + 1) * E)
        query, key, value = q_ref[:, columns], k_ref[:, columns], v_ref[:, columns]
        carry = carries[half]
        query_used = query * use_rows
        scores = dot(query, key, 1, 1).astype(BF16) * mask_ref[...]
        attended = dot(scores, value, 1, 0) + dot(query_used, carry, 1, 0)
        inverse = 1.0 / jnp.sqrt(jnp.mean(attended * attended, axis=1, keepdims=True) + EPS)
        normed = attended * inverse
        grad = g_ref[:, columns].astype(F32)
        gained = grad * normed
        send_ref[pl.ds(pairs * E + FLAG + 2 * step + half, 1), :] = jnp.sum(gained, axis=0, keepdims=True)
        gain = gain_ref[:, columns]
        centre = jnp.mean(gained * gain, axis=1, keepdims=True)
        d_att = ((grad * gain - normed * centre) * inverse).astype(BF16)
        states.append(dot(query_used, d_att, 0, 0))
        dscores = dot(d_att, value, 1, 1).astype(BF16) * mask_ref[...]
        qg_ref[:, columns] = (dot(dscores, key, 1, 0) + dot(d_att * use_rows, carry, 1, 1)).astype(BF16)
        kp_ref[:, columns] = dot(dscores, query, 0, 0)
        vp_ref[:, columns] = dot(scores, d_att, 0, 0)
    keep_ref[where, :] = jnp.where(core == 0, states[0], states[1])
    send_ref[where, :] = jnp.where(core == 0, states[1], states[0])


def final_kernel(bounds, k_ref, v_ref, kp_ref, vp_ref, kept_ref, got_ref, kg_ref, vg_ref, tail_ref, *, block_count, pairs):
    step = pl.program_id(0)
    rows = k_ref.shape[0]
    core = lax.axis_index("ctx") % 2

    @pl.when(step == 0)
    def _():
        _, tail, _ = flags(bounds, block_count)
        tail_ref[...] = row_values(tail, rows, rows // block_count).astype(BF16)

    where = place(step, pairs)
    kept, got = kept_ref[where, :], got_ref[where, :]
    laters = (
        jnp.where(core == 0, kept, got).astype(BF16),
        jnp.where(core == 0, got, kept).astype(BF16),
    )
    tail_rows = tail_ref[...]
    for half in range(2):
        columns = slice(half * E, (half + 1) * E)
        later = laters[half]
        kg_ref[:, columns] = (kp_ref[:, columns] + dot(v_ref[:, columns] * tail_rows, later, 1, 1)).astype(BF16)
        vg_ref[:, columns] = (vp_ref[:, columns] + dot(k_ref[:, columns] * tail_rows, later, 1, 0)).astype(BF16)


def swap(block, distance):
    count = lax.axis_size("ctx")
    return lax.ppermute(block, "ctx", [(i, i ^ distance) for i in range(count)])


def scan(keep, send, backward):
    count = lax.axis_size("ctx")
    me = lax.axis_index("ctx")
    rows = keep.shape[0]
    half = rows // 2

    def last(distance):
        return ((me // distance) % 2 == 1) != backward

    got = swap(send, 1)
    flag, got_flag = send[rows : rows + 1], got[rows : rows + 1]
    extra = send[rows + FLAG :] + got[rows + FLAG :]
    second = last(1)
    first_core = jnp.where(second, got[:rows], keep)
    core_flag = jnp.where(second, got_flag, flag)
    late, late_flag = jnp.where(second, keep, got[:rows]), jnp.where(second, flag, got_flag)
    total = late + (1.0 - late_flag) * first_core
    flag = jnp.maximum(flag, got_flag)

    def packed(block, flag, extra):
        return jnp.concatenate([block, jnp.broadcast_to(flag, (FLAG, E)), extra])

    send = packed(total[half:], flag, extra)
    keep = total[:half]
    got = swap(send, 2)
    got_flag = got[half : half + 1]
    extra = extra + got[half + FLAG :]
    second = last(2)
    first_chip = jnp.where(second, got[:half], keep)
    chip_flag = jnp.where(second, got_flag, flag)
    late, late_flag = jnp.where(second, keep, got[:half]), jnp.where(second, flag, got_flag)
    total = late + (1.0 - late_flag) * first_chip
    flag = jnp.maximum(flag, got_flag)

    before, before_flag = jnp.zeros_like(total), jnp.zeros_like(flag)
    distance = 4
    while distance < count:
        got = swap(packed(total, flag, extra), distance)
        got_total, got_flag = got[:half], got[half : half + 1]
        extra = extra + got[half + FLAG :]
        second = last(distance)
        before = jnp.where(second, before + (1.0 - before_flag) * got_total, before)
        before_flag = jnp.where(second, jnp.maximum(before_flag, got_flag), before_flag)
        total = jnp.where(
            second, total + (1.0 - flag) * got_total, got_total + (1.0 - got_flag) * total
        )
        flag = jnp.maximum(flag, got_flag)
        distance *= 2

    after = first_chip + (1.0 - chip_flag) * before
    second = last(2)
    mine, theirs = jnp.where(second, after, before), jnp.where(second, before, after)
    before = jnp.concatenate([mine, swap(theirs, 2)])
    after = first_core + (1.0 - core_flag) * before
    second = last(1)
    mine, theirs = jnp.where(second, after, before), jnp.where(second, before, after)
    return mine, swap(theirs, 1), extra


def shards(queries, key_vectors, value_vectors, out_grad, norm_gain, doc_bounds):
    tokens, width = queries.shape
    block_count = doc_bounds.shape[1]
    pairs = width // PAIR
    rows = pairs * E
    sizes = dict(block_count=block_count, pairs=pairs)
    columns = pl.BlockSpec((tokens, PAIR), lambda j, *_: (0, j))
    whole = lambda count: pl.BlockSpec((count, E), lambda j, *_: (0, 0))
    params = pltpu.CompilerParams(
        dimension_semantics=("arbitrary",), vmem_limit_bytes=48 * 1024 * 1024
    )

    def call(kernel, in_specs, out_specs, out_shape, scratch):
        return pl.pallas_call(
            functools.partial(kernel, **sizes),
            grid_spec=pltpu.PrefetchScalarGridSpec(
                num_scalar_prefetch=1,
                grid=(pairs,),
                in_specs=in_specs,
                out_specs=out_specs,
                scratch_shapes=scratch,
            ),
            out_shape=out_shape,
            compiler_params=params,
        )

    keep, send = call(
        state_kernel,
        [columns, columns],
        [whole(rows), whole(rows + FLAG)],
        [jax.ShapeDtypeStruct((rows, E), F32), jax.ShapeDtypeStruct((rows + FLAG, E), F32)],
        [pltpu.VMEM((tokens, E), BF16)],
    )(doc_bounds, key_vectors, value_vectors)
    kept, got, _ = scan(keep, send, False)
    extra = rows + FLAG + 2 * pairs
    query_grad, key_part, value_part, keep, send = call(
        main_kernel,
        [columns] * 4 + [pl.BlockSpec((1, PAIR), lambda j, *_: (0, j))] + [whole(rows)] * 2,
        [columns] * 3 + [whole(rows), whole(extra)],
        [
            jax.ShapeDtypeStruct((tokens, width), BF16),
            jax.ShapeDtypeStruct((tokens, width), F32),
            jax.ShapeDtypeStruct((tokens, width), F32),
            jax.ShapeDtypeStruct((rows, E), F32),
            jax.ShapeDtypeStruct((extra, E), F32),
        ],
        [pltpu.VMEM((tokens, tokens), BF16), pltpu.VMEM((tokens, E), BF16)],
    )(doc_bounds, queries, key_vectors, value_vectors, out_grad, norm_gain.reshape(1, width), kept, got)
    kept, got, gain = scan(keep, send, True)
    key_grad, value_grad = call(
        final_kernel,
        [columns] * 4 + [whole(rows)] * 2,
        [columns] * 2,
        [jax.ShapeDtypeStruct((tokens, width), BF16)] * 2,
        [pltpu.VMEM((tokens, E), BF16)],
    )(doc_bounds, key_vectors, value_vectors, key_part, value_part, kept, got)
    gain_grad = gain.reshape(width) / math.sqrt(tokens * lax.axis_size("ctx"))
    return query_grad, key_grad, value_grad, gain_grad


def solution(mesh):
    tokens = P(("parts", "ctx"), None)
    return jax.shard_map(
        shards,
        mesh=mesh,
        in_specs=(tokens, tokens, tokens, tokens, P(), P(None, ("parts", "ctx"))),
        out_specs=(tokens, tokens, tokens, P("parts")),
        check_vma=False,
    )
```

time: 335 us -> 132 us (0.39)
  the two profiles are of different devices: /device:TPU:16 before, /device:TPU:1 now
where the time goes in v1:
time: 132 us; the launch traced here: 130 us
  waiting for transfers between devices  67.6 us (51%)
  Pallas kernels  27.3 us (21%)
  starting transfers between devices  16.1 us (12%)
  other arithmetic  14.6 us (11%)
  local copies, waits for them, and re-layouts  3.94 us (3%)
    ppermute x12, waiting for transfers between devices, swap(): return lax.ppermute(block, 'ctx', [(i, i ^ distance) for i in range(count)])  67.6 us
    pallas_call x1, Pallas kernels, shards(): call(main_kernel, [columns] * 4 + [pl.BlockSpec((1, PAIR), lambda j, *_:...  17.3 us
    ppermute x12, starting transfers between devices, swap(): return lax.ppermute(block, 'ctx', [(i, i ^ distance) for i in range(count)])  16.1 us
    pallas_call x1, Pallas kernels, shards(): call(final_kernel, [columns] * 4 + [whole(rows)] * 2, [columns] * 2, [jax...  7.09 us
    unnamed x28, local copies, waits for them, and re-layouts  3.89 us
    pallas_call x1, Pallas kernels, shards(): call(state_kernel, [columns, columns], [whole(rows), whole(rows + FLAG)],...  2.89 us
  transfers between devices with their start and end apart: 12, of which 12 were waited for; matrix products, arithmetic and copies ran while one was open for 1% of the time, Pallas kernels for 0%

profile of v1, /device:TPU:1, one launch (start us, length us, event | category | flops | bytes accessed | tf_op | source)
XLA Modules:
  0.0 130.4 jit_solution(12945171304312763425)
XLA Ops:
  0.6 1.2 copy-done
  1.9 1.2 copy-done.2
  3.8 2.9 %shard_map.93 = (f32[1024,128]{1,0:T(8,128)S(1)}, f32[1032,128]{1,0:T(8,128)S(1)}) custom-call(s32[2,2]{1,0:T(2,128)S(1)} %copy-done.6, bf16[256,2048]{1,0:T(8,128)(2,1)S(1)} %copy-done, bf16[256,2048]{1,0:T(8,128)(2,1)S(1)} %copy-done.2), custom_call_target="tpu_custom_call" | custom-call | tf_op jit(solution)/shard_map/pallas_call | solution.py:237
  6.8 1.9 %collective-permute-done = f32[1032,128]{1,0:T(8,128)S(1)} collective-permute-done((f32[1032,128]{1,0:T(8,128)S(1)}, f32[1032,128]{1,0:T(8,128)S(1)}, u32[]{:S(2)}, u32[]{:S(2)}) %collective-permute-start) | collective-permute-done | bytes 528416 | tf_op jit(solution)/shard_map/ppermute | solution.py:149
  8.8 2.4 %collective-permute-start.1 = (f32[520,128]{1,0:T(8,128)S(1)}, f32[520,128]{1,0:T(8,128)S(1)}, u32[]{:S(2)}, u32[]{:S(2)}) collective-permute-start(f32[520,128]{1,0:T(8,128)S(1)} %pad_maximum_fusion.5), channel_id=1, source_target_pairs={{0,2},{1,3},{2,0},{3,1},{4,6},{5,7},{6,4},{7,5},{8,10},{9,11},{10,... | collective-permute-start | bytes 798728 | tf_op jit(solution)/shard_map/ppermute | solution.py:149
  11.2 6.5 %collective-permute-done.1 = f32[520,128]{1,0:T(8,128)S(1)} collective-permute-done((f32[520,128]{1,0:T(8,128)S(1)}, f32[520,128]{1,0:T(8,128)S(1)}, u32[]{:S(2)}, u32[]{:S(2)}) %collective-permute-start.1) | collective-permute-done | bytes 266272 | tf_op jit(solution)/shard_map/ppermute | solution.py:149
  17.8 1.3 collective-permute-start.2
  19.1 5.8 %collective-permute-done.2 = f32[520,128]{1,0:T(8,128)S(1)} collective-permute-done((f32[520,128]{1,0:T(8,128)S(1)}, f32[520,128]{1,0:T(8,128)S(1)}, u32[]{:S(2)}, u32[]{:S(2)}) %collective-permute-start.2) | collective-permute-done | bytes 266272 | tf_op jit(solution)/shard_map/ppermute | solution.py:149
  25.0 1.9 %collective-permute-start.3 = (f32[520,128]{1,0:T(8,128)S(1)}, f32[520,128]{1,0:T(8,128)S(1)}, u32[]{:S(2)}, u32[]{:S(2)}) collective-permute-start(f32[520,128]{1,0:T(8,128)S(1)} %pad_maximum_fusion.7), channel_id=1, source_target_pairs={{0,8},{1,9},{2,10},{3,11},{4,12},{5,13},{6,14},{7,15},{8,0},{9,1},... | collective-permute-start | bytes 798728 | tf_op jit(solution)/shard_map/ppermute | solution.py:149
  26.9 12.4 %collective-permute-done.3 = f32[520,128]{1,0:T(8,128)S(1)} collective-permute-done((f32[520,128]{1,0:T(8,128)S(1)}, f32[520,128]{1,0:T(8,128)S(1)}, u32[]{:S(2)}, u32[]{:S(2)}) %collective-permute-start.3) | collective-permute-done | bytes 266272 | tf_op jit(solution)/shard_map/ppermute | solution.py:149
  40.1 1.3 fusion.7
  41.8 6.3 %collective-permute-done.4 = f32[512,128]{1,0:T(8,128)S(1)} collective-permute-done((f32[512,128]{1,0:T(8,128)S(1)}, f32[512,128]{1,0:T(8,128)S(1)}, u32[]{:S(2)}, u32[]{:S(2)}) %collective-permute-start.4) | collective-permute-done | bytes 262176 | tf_op jit(solution)/shard_map/ppermute | solution.py:149
  48.1 1.2 fusion.2
  49.2 2.1 %collective-permute-start.5 = (f32[1024,128]{1,0:T(8,128)S(1)}, f32[1024,128]{1,0:T(8,128)S(1)}, u32[]{:S(2)}, u32[]{:S(2)}) collective-permute-start(f32[1024,128]{1,0:T(8,128)S(1)} %get-tuple-element.24), channel_id=1, source_target_pairs={{0,1},{1,0},{2,3},{3,2},{4,5},{5,4},{6,7},{7,6},{8,9},{9,8},{10,11... | collective-permute-start | bytes 1572872 | tf_op jit(solution)/shard_map/ppermute | solution.py:149
  51.4 1.5 %collective-permute-done.5.got_ref = f32[1024,128]{1,0:T(8,128)S(1)} collective-permute-done((f32[1024,128]{1,0:T(8,128)S(1)}, f32[1024,128]{1,0:T(8,128)S(1)}, u32[]{:S(2)}, u32[]{:S(2)}) %collective-permute-start.5) | collective-permute-done | bytes 524320 | tf_op jit(solution)/shard_map/ppermute | solution.py:149
  52.9 17.3 %shard_map.94 = (bf16[256,2048]{1,0:T(8,128)(2,1)}, f32[256,2048]{1,0:T(8,128)}, f32[256,2048]{1,0:T(8,128)}, f32[1024,128]{1,0:T(8,128)S(1)}, f32[1048,128]{1,0:T(8,128)S(1)}) custom-call(s32[2,2]{1,0:T(2,128)S(1)} %copy-done.7, bf16[256,2048]{1,0:T(8,128)(2,1)S(1)} %copy-done.5, bf16[256,2048]{1,0:T(8,128)(2,1)S(1)} %copy-done.1, ...), custom_call_target="tpu_custom_call" | custom-call | tf_op jit(solution)/shard_map/pallas_call | solution.py:246
  70.6 1.7 %collective-permute-done.6 = f32[1048,128]{1,0:T(8,128)} collective-permute-done((f32[1048,128]{1,0:T(8,128)S(1)}, f32[1048,128]{1,0:T(8,128)}, u32[]{:S(2)}, u32[]{:S(2)}) %collective-permute-start.6) | collective-permute-done | bytes 536608 | tf_op jit(solution)/shard_map/ppermute | solution.py:149
  73.0 1.1 multiply_add_fusion.1
  74.1 0.7 slice_add_fusion.3
  75.3 7.5 %collective-permute-done.7 = f32[536,128]{1,0:T(8,128)} collective-permute-done((f32[536,128]{1,0:T(8,128)S(1)}, f32[536,128]{1,0:T(8,128)}, u32[]{:S(2)}, u32[]{:S(2)}) %collective-permute-start.7) | collective-permute-done | bytes 274464 | tf_op jit(solution)/shard_map/ppermute | solution.py:149
  84.2 1.1 multiply_add_fusion.5
  86.7 6.6 %collective-permute-done.8 = f32[536,128]{1,0:T(8,128)} collective-permute-done((f32[536,128]{1,0:T(8,128)}, f32[536,128]{1,0:T(8,128)}, u32[]{:S(2)}, u32[]{:S(2)}) %collective-permute-start.8) | collective-permute-done | bytes 274464 | tf_op jit(solution)/shard_map/ppermute | solution.py:149
  94.6 1.0 add_select_fusion.2
  95.7 2.6 %collective-permute-start.9 = (f32[536,128]{1,0:T(8,128)S(1)}, f32[536,128]{1,0:T(8,128)}, u32[]{:S(2)}, u32[]{:S(2)}) collective-permute-start(f32[536,128]{1,0:T(8,128)S(1)} %pad_maximum_fusion.4), channel_id=1, source_target_pairs={{0,8},{1,9},{2,10},{3,11},{4,12},{5,13},{6,14},{7,15},{8,0},{9,1},... | collective-permute-start | bytes 823304 | tf_op jit(solution)/shard_map/ppermute | solution.py:149
  98.3 12.1 %collective-permute-done.9 = f32[536,128]{1,0:T(8,128)} collective-permute-done((f32[536,128]{1,0:T(8,128)S(1)}, f32[536,128]{1,0:T(8,128)}, u32[]{:S(2)}, u32[]{:S(2)}) %collective-permute-start.9) | collective-permute-done | bytes 274464 | tf_op jit(solution)/shard_map/ppermute | solution.py:149
  110.4 1.3 %fusion.5 = (f32[512,128]{1,0:T(8,128)S(1)}, f32[512,128]{1,0:T(8,128)S(1)}) fusion(f32[128]{0:T(128)S(1)} %get-tuple-element.38, pred[]{:T(512)S(6)} %ne.88, f32[536,128]{1,0:T(8,128)} %collective-permute-done.9, f32[128]{0:T(128)S(1)} %get-tuple-element.41, f32[536,128]{1,0:T(8,128)} %collective-permute-done.8, pred[]{:T(512)S(6)} %ne.90, pred[]{:T(512)S(6)} %ne.89, ...), kind=kLoop, calls=%fused_computation.24 | loop fusion | flops 589824 | bytes 1573891 | tf_op jit(solution)/shard_map/jit(_where)/select_n | solution.py:203
  111.7 1.3 %collective-permute-start.10 = (f32[512,128]{1,0:T(8,128)S(1)}, f32[512,128]{1,0:T(8,128)S(1)}, u32[]{:S(2)}, u32[]{:S(2)}) collective-permute-start(f32[512,128]{1,0:T(8,128)S(1)} %get-tuple-element.27), channel_id=1, source_target_pairs={{0,2},{1,3},{2,0},{3,1},{4,6},{5,7},{6,4},{7,5},{8,10},{9,11},{10,... | collective-permute-start | bytes 786440 | tf_op jit(solution)/shard_map/ppermute | solution.py:149
  113.0 5.1 %collective-permute-done.10 = f32[512,128]{1,0:T(8,128)S(1)} collective-permute-done((f32[512,128]{1,0:T(8,128)S(1)}, f32[512,128]{1,0:T(8,128)S(1)}, u32[]{:S(2)}, u32[]{:S(2)}) %collective-permute-start.10) | collective-permute-done | bytes 262176 | tf_op jit(solution)/shard_map/ppermute | solution.py:149
  118.1 1.2 fusion
  119.3 2.4 %collective-permute-start.11 = (f32[1024,128]{1,0:T(8,128)S(1)}, f32[1024,128]{1,0:T(8,128)S(1)}, u32[]{:S(2)}, u32[]{:S(2)}) collective-permute-start(f32[1024,128]{1,0:T(8,128)S(1)} %get-tuple-element.22), channel_id=1, source_target_pairs={{0,1},{1,0},{2,3},{3,2},{4,5},{5,4},{6,7},{7,6},{8,9},{9,8},{10,11... | collective-permute-start | bytes 1572872 | tf_op jit(solution)/shard_map/ppermute | solution.py:149
  121.7 1.3 fusion.9
  123.3 7.1 %shard_map.95 = (bf16[256,2048]{1,0:T(8,128)(2,1)}, bf16[256,2048]{1,0:T(8,128)(2,1)}) custom-call(s32[2,2]{1,0:T(2,128)S(1)} %copy-done.7, bf16[256,2048]{1,0:T(8,128)(2,1)S(1)} %copy-done.1, bf16[256,2048]{1,0:T(8,128)(2,1)S(1)} %copy-done.3, f32[256,2048]{1,0:T(8,128)S(1)} %copy-done.4, f32[256,2048]{1,0:T(8,128)} %get-tuple-element.17.vp_ref, ...), custom_call_target="tpu_custom_call" | custom-call | tf_op jit(solution)/shard_map/pallas_call | solution.py:260
  (57 shorter events, 8.2 us)
Async XLA Ops:
  0.6 1.2 copy-start
  1.9 1.2 copy-start.2
  3.1 0.7 copy-start.6
  6.7 2.0 %collective-permute-start = (f32[1032,128]{1,0:T(8,128)S(1)}, f32[1032,128]{1,0:T(8,128)S(1)}, u32[]{:S(2)}, u32[]{:S(2)}) collective-permute-start(f32[1032,128]{1,0:T(8,128)S(1)} %get-tuple-element.13), channel_id=1, source_target_pairs={{0,1},{1,0},{2,3},{3,2},{4,5},{5,4},{6,7},{7,6},{8,9},{9,8},{10,11... | collective-permute-start | bytes 1585160 | tf_op jit(solution)/shard_map/ppermute | solution.py:149
  8.6 30.7 %copy-start.11 = (f32[1032,128]{1,0:T(8,128)}, f32[1032,128]{1,0:T(8,128)S(1)}, u32[]{:S(2)}) copy-start(f32[1032,128]{1,0:T(8,128)S(1)} %collective-permute-done) | copy-start | bytes 1585156
  8.8 8.9 %collective-permute-start.1 = (f32[520,128]{1,0:T(8,128)S(1)}, f32[520,128]{1,0:T(8,128)S(1)}, u32[]{:S(2)}, u32[]{:S(2)}) collective-permute-start(f32[520,128]{1,0:T(8,128)S(1)} %pad_maximum_fusion.5), channel_id=1, source_target_pairs={{0,2},{1,3},{2,0},{3,1},{4,6},{5,7},{6,4},{7,5},{8,10},{9,11},{10,... | collective-permute-start | bytes 798728 | tf_op jit(solution)/shard_map/ppermute | solution.py:149
  17.8 7.1 %collective-permute-start.2 = (f32[520,128]{1,0:T(8,128)S(1)}, f32[520,128]{1,0:T(8,128)S(1)}, u32[]{:S(2)}, u32[]{:S(2)}) collective-permute-start(f32[520,128]{1,0:T(8,128)S(1)} %pad_maximum_fusion.6), channel_id=1, source_target_pairs={{0,4},{1,5},{2,6},{3,7},{4,0},{5,1},{6,2},{7,3},{8,12},{9,13},{10,... | collective-permute-start | bytes 798728 | tf_op jit(solution)/shard_map/ppermute | solution.py:149
  24.9 14.5 %copy-start.12 = (f32[520,128]{1,0:T(8,128)}, f32[520,128]{1,0:T(8,128)S(1)}, u32[]{:S(2)}) copy-start(f32[520,128]{1,0:T(8,128)S(1)} %collective-permute-done.2) | copy-start | bytes 798724
  25.0 14.3 %collective-permute-start.3 = (f32[520,128]{1,0:T(8,128)S(1)}, f32[520,128]{1,0:T(8,128)S(1)}, u32[]{:S(2)}, u32[]{:S(2)}) collective-permute-start(f32[520,128]{1,0:T(8,128)S(1)} %pad_maximum_fusion.7), channel_id=1, source_target_pairs={{0,8},{1,9},{2,10},{3,11},{4,12},{5,13},{6,14},{7,15},{8,0},{9,1},... | collective-permute-start | bytes 798728 | tf_op jit(solution)/shard_map/ppermute | solution.py:149
  39.3 0.7 copy-start.13
  40.0 12.9 %copy-start.1 = (bf16[256,2048]{1,0:T(8,128)(2,1)S(1)}, bf16[256,2048]{1,0:T(8,128)(2,1)}, u32[]{:S(2)}) copy-start(bf16[256,2048]{1,0:T(8,128)(2,1)} %k_ref.5) | copy-start | bytes 3145732
  40.0 12.9 %copy-start.3 = (bf16[256,2048]{1,0:T(8,128)(2,1)S(1)}, bf16[256,2048]{1,0:T(8,128)(2,1)}, u32[]{:S(2)}) copy-start(bf16[256,2048]{1,0:T(8,128)(2,1)} %v_ref.5) | copy-start | bytes 3145732
  40.0 12.9 %copy-start.5 = (bf16[256,2048]{1,0:T(8,128)(2,1)S(1)}, bf16[256,2048]{1,0:T(8,128)(2,1)}, u32[]{:S(2)}) copy-start(bf16[256,2048]{1,0:T(8,128)(2,1)} %q_ref.1) | copy-start | bytes 3145732
  40.0 12.9 %copy-start.7 = (s32[2,2]{1,0:T(2,128)S(1)}, s32[2,2]{1,0:T(2,128)}, u32[]{:S(2)}) copy-start(s32[2,2]{1,0:T(2,128)} %bounds.5) | copy-start | bytes 52
  40.1 12.9 %copy-start.8 = (f32[2048]{0:T(1024)S(1)}, f32[2048]{0:T(1024)}, u32[]{:S(2)}) copy-start(f32[2048]{0:T(1024)} %param.10) | copy-start | bytes 24580
  41.3 6.7 %collective-permute-start.4 = (f32[512,128]{1,0:T(8,128)S(1)}, f32[512,128]{1,0:T(8,128)S(1)}, u32[]{:S(2)}, u32[]{:S(2)}) collective-permute-start(f32[512,128]{1,0:T(8,128)S(1)} %get-tuple-element.29), channel_id=1, source_target_pairs={{0,2},{1,3},{2,0},{3,1},{4,6},{5,7},{6,4},{7,5},{8,10},{9,11},{10,... | collective-permute-start | bytes 786440 | tf_op jit(solution)/shard_map/ppermute | solution.py:149
  49.2 3.7 %collective-permute-start.5 = (f32[1024,128]{1,0:T(8,128)S(1)}, f32[1024,128]{1,0:T(8,128)S(1)}, u32[]{:S(2)}, u32[]{:S(2)}) collective-permute-start(f32[1024,128]{1,0:T(8,128)S(1)} %get-tuple-element.24), channel_id=1, source_target_pairs={{0,1},{1,0},{2,3},{3,2},{4,5},{5,4},{6,7},{7,6},{8,9},{9,8},{10,11... | collective-permute-start | bytes 1572872 | tf_op jit(solution)/shard_map/ppermute | solution.py:149
  70.2 2.1 %collective-permute-start.6 = (f32[1048,128]{1,0:T(8,128)S(1)}, f32[1048,128]{1,0:T(8,128)}, u32[]{:S(2)}, u32[]{:S(2)}) collective-permute-start(f32[1048,128]{1,0:T(8,128)S(1)} %get-tuple-element.18), channel_id=1, source_target_pairs={{0,1},{1,0},{2,3},{3,2},{4,5},{5,4},{6,7},{7,6},{8,9},{9,8},{10,11... | collective-permute-start | bytes 1609736 | tf_op jit(solution)/shard_map/ppermute | solution.py:149
  74.1 0.8 copy-start.9
  74.9 35.5 %copy-start.10 = (f32[1024,128]{1,0:T(8,128)S(1)}, f32[1024,128]{1,0:T(8,128)}, u32[]{:S(2)}) copy-start(f32[1024,128]{1,0:T(8,128)} %copy-done.9) | copy-start | bytes 1572868
  74.9 8.0 %collective-permute-start.7 = (f32[536,128]{1,0:T(8,128)S(1)}, f32[536,128]{1,0:T(8,128)}, u32[]{:S(2)}, u32[]{:S(2)}) collective-permute-start(f32[536,128]{1,0:T(8,128)S(1)} %pad_maximum_fusion.2), channel_id=1, source_target_pairs={{0,2},{1,3},{2,0},{3,1},{4,6},{5,7},{6,4},{7,5},{8,10},{9,11},{10,... | collective-permute-start | bytes 823304 | tf_op jit(solution)/shard_map/ppermute | solution.py:149
  86.1 7.2 %collective-permute-start.8 = (f32[536,128]{1,0:T(8,128)}, f32[536,128]{1,0:T(8,128)}, u32[]{:S(2)}, u32[]{:S(2)}) collective-permute-start(f32[536,128]{1,0:T(8,128)} %pad_maximum_fusion.3), channel_id=1, source_target_pairs={{0,4},{1,5},{2,6},{3,7},{4,0},{5,1},{6,2},{7,3},{8,12},{9,13},{10,... | collective-permute-start | bytes 823304 | tf_op jit(solution)/shard_map/ppermute | solution.py:149
  95.7 14.7 %collective-permute-start.9 = (f32[536,128]{1,0:T(8,128)S(1)}, f32[536,128]{1,0:T(8,128)}, u32[]{:S(2)}, u32[]{:S(2)}) collective-permute-start(f32[536,128]{1,0:T(8,128)S(1)} %pad_maximum_fusion.4), channel_id=1, source_target_pairs={{0,8},{1,9},{2,10},{3,11},{4,12},{5,13},{6,14},{7,15},{8,0},{9,1},... | collective-permute-start | bytes 823304 | tf_op jit(solution)/shard_map/ppermute | solution.py:149
  110.4 12.9 %copy-start.4 = (f32[256,2048]{1,0:T(8,128)S(1)}, f32[256,2048]{1,0:T(8,128)}, u32[]{:S(2)}) copy-start(f32[256,2048]{1,0:T(8,128)} %get-tuple-element.16.kp_ref) | copy-start | bytes 6291460
  111.7 6.4 %collective-permute-start.10 = (f32[512,128]{1,0:T(8,128)S(1)}, f32[512,128]{1,0:T(8,128)S(1)}, u32[]{:S(2)}, u32[]{:S(2)}) collective-permute-start(f32[512,128]{1,0:T(8,128)S(1)} %get-tuple-element.27), channel_id=1, source_target_pairs={{0,2},{1,3},{2,0},{3,1},{4,6},{5,7},{6,4},{7,5},{8,10},{9,11},{10,... | collective-permute-start | bytes 786440 | tf_op jit(solution)/shard_map/ppermute | solution.py:149
  119.3 4.0 %collective-permute-start.11 = (f32[1024,128]{1,0:T(8,128)S(1)}, f32[1024,128]{1,0:T(8,128)S(1)}, u32[]{:S(2)}, u32[]{:S(2)}) collective-permute-start(f32[1024,128]{1,0:T(8,128)S(1)} %get-tuple-element.22), channel_id=1, source_target_pairs={{0,1},{1,0},{2,3},{3,2},{4,5},{5,4},{6,7},{7,6},{8,9},{9,8},{10,11... | collective-permute-start | bytes 1572872 | tf_op jit(solution)/shard_map/ppermute | solution.py:149

commit v2 on v1

v2 whole, which is shorter than its diff:
```python
import functools
import math

import jax
import jax.numpy as jnp
from jax import lax
from jax.experimental import pallas as pl
from jax.experimental.pallas import tpu as pltpu
from jax.sharding import PartitionSpec as P

E = 128
PAIR = 2 * E
FLAG = 8
EPS = 1e-06
VMEM_LIMIT = 8 * 1024 * 1024
F32 = jnp.float32
BF16 = jnp.bfloat16
VMEM = pl.BlockSpec(memory_space=pltpu.VMEM)
ANY = pl.BlockSpec(memory_space=pl.ANY)


def dot(a, b, a_dim, b_dim):
    return lax.dot_general(a, b, (((a_dim,), (b_dim,)), ((), ())), preferred_element_type=F32)


def head(h):
    return slice(h * E, (h + 1) * E)


def both(pair):
    return slice(pair * PAIR, (pair + 1) * PAIR)


def place(pair, pairs):
    y_bit = (lax.axis_index("ctx") // 2) % 2
    slot = ((pair % 2) ^ y_bit) * (pairs // 2) + pair // 2
    return pl.ds(pl.multiple_of(slot * E, E), E)


def put_states(states, pair, pairs, keep_ref, send_ref):
    where = place(pair, pairs)
    core = lax.axis_index("ctx") % 2
    keep_ref[where, :] = jnp.where(core == 0, states[0], states[1])
    send_ref[where, :] = jnp.where(core == 0, states[1], states[0])


def get_states(pair, pairs, kept_ref, got_ref):
    where = place(pair, pairs)
    core = lax.axis_index("ctx") % 2
    kept, got = kept_ref[where, :], got_ref[where, :]
    return (
        jnp.where(core == 0, kept, got).astype(BF16),
        jnp.where(core == 0, got, kept).astype(BF16),
    )


def fetch(group, sources, targets, sems):
    width = targets[0].shape[1]
    copies = []
    for pair in range(width // PAIR):
        copies.append([])
        for i, (source, target) in enumerate(zip(sources, targets)):
            copy = pltpu.make_async_copy(
                source.at[:, pl.ds(group * width + pair * PAIR, PAIR)],
                target.at[:, both(pair)],
                sems.at[pair, i],
            )
            copy.start()
            copies[-1].append(copy)
    return copies


def row_values(values, rows, dtype):
    position = lax.broadcasted_iota(jnp.int32, (rows, E), 0)
    result = jnp.full((rows, E), values[0])
    for block in range(1, len(values)):
        result = jnp.where(position >= block * (rows // len(values)), values[block], result)
    return result.astype(dtype)


def states_of(k_ref, v_ref, tail_ref, copies, keep_ref, send_ref):
    pairs = len(copies)
    tail = tail_ref[...]
    for pair in range(pairs):
        for copy in copies[pair]:
            copy.wait()
        states = [
            dot(k_ref[:, head(h)] * tail, v_ref[:, head(h)], 0, 0) for h in (2 * pair, 2 * pair + 1)
        ]
        put_states(states, pair, pairs, keep_ref, send_ref)


def first_state_kernel(
    bounds_hbm, k_hbm, v_hbm,
    keep_ref, send_ref, k_ref, v_ref, start_ref, end_ref, use_ref, tail_ref, flag_ref, bits_ref,
    bounds, sems, bounds_sem, *, group,
):
    bounds_copy = pltpu.make_async_copy(bounds_hbm, bounds, bounds_sem)
    bounds_copy.start()
    copies = fetch(group, (k_hbm, v_hbm), (k_ref, v_ref), sems)
    rows, width = k_ref.shape
    count = bounds.shape[1]
    block_len = rows // count
    me = lax.axis_index("ctx")
    first = me * count
    for bit in range(bits_ref.shape[0] // FLAG):
        value = jnp.full((FLAG, E), (me // 2**bit) % 2)
        bits_ref[bit * FLAG : (bit + 1) * FLAG, :] = value.astype(F32)
    bounds_copy.wait()
    opens = [bounds[0, b] for b in range(count)]
    closes = [bounds[1, b] for b in range(count)]
    flag = jnp.full((FLAG, E), (opens[-1] >= first).astype(F32))
    flag_ref[...] = flag
    send_ref[width // 2 :, :] = flag
    use_ref[...] = row_values([(x < first).astype(F32) for x in opens], rows, BF16)
    tail_ref[...] = row_values([(x >= first + count - 1).astype(F32) for x in closes], rows, BF16)
    start_ref[...] = row_values([(x - first) * block_len for x in opens], rows, jnp.int32)
    end_ref[...] = row_values([(x - first + 1) * block_len for x in closes], rows, jnp.int32)
    states_of(k_ref, v_ref, tail_ref, copies, keep_ref, send_ref)


def state_kernel(
    k_hbm, v_hbm, tail_ref, flag_ref, keep_ref, send_ref, k_ref, v_ref, sems, *, group
):
    copies = fetch(group, (k_hbm, v_hbm), (k_ref, v_ref), sems)
    send_ref[k_ref.shape[1] // 2 :, :] = flag_ref[...]
    states_of(k_ref, v_ref, tail_ref, copies, keep_ref, send_ref)


def sight(bound_ref, turned):
    rows = bound_ref.shape[0]
    row = lax.broadcasted_iota(jnp.int32, (rows, E), 0)
    parts = []
    for c in range(rows // E):
        column = lax.broadcasted_iota(jnp.int32, (rows, E), 1) + c * E
        if turned:
            seen = (column >= row) & (column < bound_ref[...])
        else:
            seen = (column <= row) & (column >= bound_ref[...])
        parts.append(jnp.where(seen, 1.0, 0.0).astype(BF16))
    return jnp.concatenate(parts, axis=1)


def local_kernel(
    q_hbm, g_hbm, gain_hbm, k_ref, v_ref, start_ref, _,
    out_ref, q_ref, g_ref, gain_ref, sems, gain_sem, *, group,
):
    width = k_ref.shape[1]
    copies = fetch(group, (q_hbm, g_hbm), (q_ref, g_ref), sems)
    gain_copy = pltpu.make_async_copy(
        gain_hbm.at[:, pl.ds(group * width, width)], gain_ref, gain_sem
    )
    gain_copy.start()
    mask = sight(start_ref, False)
    for pair in range(width // PAIR):
        copies[pair][0].wait()
        for h in (2 * pair, 2 * pair + 1):
            scores = dot(q_ref[:, head(h)], k_ref[:, head(h)], 1, 1).astype(BF16) * mask
            out_ref[:, head(h)] = dot(scores, v_ref[:, head(h)], 1, 0)
    for pair in range(width // PAIR):
        copies[pair][1].wait()
    gain_copy.wait()


def middle_kernel(
    q_ref, g_ref, gain_ref, local_ref, kept_ref, got_ref, use_ref, flag_ref,
    d_ref, keep_ref, send_ref,
):
    pairs = q_ref.shape[1] // PAIR
    use = use_ref[...]
    send_ref[pairs * E : pairs * E + FLAG, :] = flag_ref[...]
    for pair in range(pairs):
        states = []
        for h, carry in zip((2 * pair, 2 * pair + 1), get_states(pair, pairs, kept_ref, got_ref)):
            used = q_ref[:, head(h)] * use
            attended = local_ref[:, head(h)] + dot(used, carry, 1, 0)
            inverse = lax.rsqrt(jnp.mean(attended * attended, axis=1, keepdims=True) + EPS)
            normed = attended * inverse
            grad = g_ref[:, head(h)].astype(F32)
            gained = grad * normed
            row = pairs * E + FLAG + h
            send_ref[row : row + 1, :] = jnp.sum(gained, axis=0, keepdims=True)
            gain = gain_ref[:, head(h)]
            centre = jnp.mean(gained * gain, axis=1, keepdims=True)
            d_att = ((grad * gain - normed * centre) * inverse).astype(BF16)
            d_ref[:, head(h)] = d_att
            states.append(dot(used, d_att, 0, 0))
        put_states(states, pair, pairs, keep_ref, send_ref)


def spread_kernel(
    q_ref, k_ref, v_ref, d_ref, kept_ref, got_ref, use_ref, start_ref, end_ref, *rest, group
):
    qg_hbm, kp_ref, vp_ref, qg_ref, sems = rest[-5:]
    width = q_ref.shape[1]
    pairs = width // PAIR
    use = use_ref[...]
    mask = sight(start_ref, False)
    turned_mask = sight(end_ref, True)
    copies = []
    for pair in range(pairs):
        for h, carry in zip((2 * pair, 2 * pair + 1), get_states(pair, pairs, kept_ref, got_ref)):
            c = head(h)
            query, key, value, d_att = q_ref[:, c], k_ref[:, c], v_ref[:, c], d_ref[:, c]
            dscores = dot(d_att, value, 1, 1).astype(BF16) * mask
            from_carry = dot(d_att * use, carry, 1, 1)
            qg_ref[:, c] = (dot(dscores, key, 1, 0) + from_carry).astype(BF16)
            turned = dot(value, d_att, 1, 1).astype(BF16) * turned_mask
            kp_ref[:, c] = dot(turned, query, 1, 0)
            turned = dot(key, query, 1, 1).astype(BF16) * turned_mask
            vp_ref[:, c] = dot(turned, d_att, 1, 0)
        copy = pltpu.make_async_copy(
            qg_ref.at[:, both(pair)],
            qg_hbm.at[:, pl.ds(group * width + pair * PAIR, PAIR)],
            sems.at[pair],
        )
        copy.start()
        copies.append(copy)
    for copy in copies:
        copy.wait()


def final_kernel(k_ref, v_ref, kp_ref, vp_ref, kept_ref, got_ref, tail_ref, *rest, group):
    kg_hbm, vg_hbm, kg_ref, vg_ref, sems = rest[-5:]
    width = k_ref.shape[1]
    pairs = width // PAIR
    tail = tail_ref[...]
    copies = []
    for pair in range(pairs):
        for h, later in zip((2 * pair, 2 * pair + 1), get_states(pair, pairs, kept_ref, got_ref)):
            c = head(h)
            kg_ref[:, c] = (kp_ref[:, c] + dot(v_ref[:, c] * tail, later, 1, 1)).astype(BF16)
            vg_ref[:, c] = (vp_ref[:, c] + dot(k_ref[:, c] * tail, later, 1, 0)).astype(BF16)
        for i, (source, target) in enumerate(((kg_ref, kg_hbm), (vg_ref, vg_hbm))):
            copy = pltpu.make_async_copy(
                source.at[:, both(pair)],
                target.at[:, pl.ds(group * width + pair * PAIR, PAIR)],
                sems.at[pair, i],
            )
            copy.start()
            copies.append(copy)
    for copy in copies:
        copy.wait()


def swap(block, distance):
    count = lax.axis_size("ctx")
    return lax.ppermute(block, "ctx", [(i, i ^ distance) for i in range(count)])


def scan(keep, send, bits, backward):
    count = lax.axis_size("ctx")
    rows = keep.shape[0]
    half = rows // 2

    def last(distance):
        row = FLAG * (distance.bit_length() - 1)
        bit = bits[row : row + 1]
        return bit < 0.5 if backward else bit > 0.5

    def packed(block, flag, extra):
        return jnp.concatenate([block, jnp.broadcast_to(flag, (FLAG, E)), extra])

    got = yield send, 1
    flag, got_flag = send[rows : rows + 1], got[rows : rows + 1]
    extra = send[rows + FLAG :] + got[rows + FLAG :]
    second = last(1)
    first_core = jnp.where(second, got[:rows], keep)
    core_flag = jnp.where(second, got_flag, flag)
    late_flag = jnp.where(second, flag, got_flag)

    def both_cores(part):
        mine, other = keep[part], got[part]
        return jnp.where(second, mine, other) + (1.0 - late_flag) * jnp.where(second, other, mine)

    flag = jnp.maximum(flag, got_flag)

    block = packed(both_cores(slice(half, rows)), flag, extra)
    keep = both_cores(slice(0, half))
    got = yield block, 2
    got_flag = got[half : half + 1]
    extra = extra + got[half + FLAG :]
    second = last(2)
    first_chip = jnp.where(second, got[:half], keep)
    chip_flag = jnp.where(second, got_flag, flag)
    late, late_flag = jnp.where(second, keep, got[:half]), jnp.where(second, flag, got_flag)
    total = late + (1.0 - late_flag) * first_chip
    flag = jnp.maximum(flag, got_flag)

    before, before_flag = jnp.zeros_like(total), jnp.zeros_like(flag)
    distance = 4
    while distance < count:
        got = yield packed(total, flag, extra), distance
        got_total, got_flag = got[:half], got[half : half + 1]
        extra = extra + got[half + FLAG :]
        second = last(distance)
        before = jnp.where(second, before + (1.0 - before_flag) * got_total, before)
        before_flag = jnp.where(second, jnp.maximum(before_flag, got_flag), before_flag)
        total = jnp.where(
            second, total + (1.0 - flag) * got_total, got_total + (1.0 - got_flag) * total
        )
        flag = jnp.maximum(flag, got_flag)
        distance *= 2

    after = first_chip + (1.0 - chip_flag) * before
    second = last(2)
    mine, theirs = jnp.where(second, after, before), jnp.where(second, before, after)
    got = yield theirs, 2
    before = jnp.concatenate([mine, got])
    after = first_core + (1.0 - core_flag) * before
    second = last(1)
    mine, theirs = jnp.where(second, after, before), jnp.where(second, before, after)
    got = yield theirs, 1
    return mine, got, extra


def rounds(one, two, work):
    chains, waiting, results, pending = [one], {}, {}, ()
    number = 0
    while chains:
        if number == 1:
            chains.append(two)
        for chain in chains:
            if chain not in waiting:
                waiting[chain] = next(chain)
        blocks, _ = lax.optimization_barrier(([waiting[c][0] for c in chains], pending))
        pending = work[number](blocks[0]) if number in work else ()
        for chain, block in zip(list(chains), blocks):
            try:
                waiting[chain] = chain.send(swap(block, waiting[chain][1]))
            except StopIteration as end:
                results[chain] = end.value
                chains.remove(chain)
        number += 1
    return results[one], results[two]


def shards(queries, key_vectors, value_vectors, out_grad, norm_gain, doc_bounds):
    tokens, width = queries.shape
    groups = range(2)
    half = width // 2
    pairs = half // PAIR
    rows = pairs * E
    extra = rows + FLAG + 2 * pairs
    queries, key_vectors, value_vectors, out_grad, gains, doc_bounds = (
        pltpu.with_memory_space_constraint(x, pltpu.HBM)
        for x in (
            queries, key_vectors, value_vectors, out_grad, norm_gain.reshape(1, width), doc_bounds
        )
    )

    def shape(count, columns, dtype=F32):
        return jax.ShapeDtypeStruct((count, columns), dtype)

    def call(kernel, inputs, outputs, scratch=(), aliases={}, **sizes):
        return pl.pallas_call(
            functools.partial(kernel, **sizes),
            in_specs=inputs,
            out_specs=[spec for spec, _ in outputs],
            out_shape=[out for _, out in outputs],
            scratch_shapes=scratch,
            input_output_aliases=aliases,
            compiler_params=pltpu.CompilerParams(vmem_limit_bytes=VMEM_LIMIT),
        )

    def copies(*counts):
        return pltpu.SemaphoreType.DMA(counts)

    levels = lax.axis_size("ctx").bit_length() - 1
    narrow, single = (VMEM, shape(tokens, half, BF16)), (VMEM, shape(tokens, half))
    staging = pltpu.VMEM((tokens, half), BF16)
    states = [(VMEM, shape(rows, E)), (VMEM, shape(rows + FLAG, E))]
    local, carried, middle, spread = {}, {}, {}, {}
    *first, key, value, start, end, use, tail, flag, bits = call(
        first_state_kernel,
        [ANY] * 3,
        states + [narrow] * 2 + [(VMEM, shape(tokens, E, jnp.int32))] * 2
        + [(VMEM, shape(tokens, E, BF16))] * 2
        + [(VMEM, shape(FLAG, E)), (VMEM, shape(FLAG * levels, E))],
        [pltpu.SMEM(doc_bounds.shape, jnp.int32), copies(pairs, 2), copies()],
        group=0,
    )(doc_bounds, key_vectors, value_vectors)
    *second, other_key, other_value = call(
        state_kernel, [ANY] * 2 + [VMEM] * 2, states + [narrow] * 2, [copies(pairs, 2)], group=1
    )(key_vectors, value_vectors, tail, flag)
    keys, values = (key, other_key), (value, other_value)

    def local_of(g, token):
        local[g] = call(
            local_kernel,
            [ANY] * 3 + [VMEM] * 3 + [ANY],
            [single, narrow, narrow, (VMEM, shape(1, half))],
            [copies(pairs, 2), copies()],
            group=g,
        )(queries, out_grad, gains, keys[g], values[g], start, token)
        return local[g][0]

    def spread_of(g, token):
        done = spread[0][:1] if g else []
        spread[g] = call(
            spread_kernel,
            [VMEM] * 9 + [ANY] * (1 + len(done)),
            [(ANY, shape(tokens, width, BF16)), single, single],
            [staging, copies(pairs)],
            {10: 0} if done else {},
            group=g,
        )(
            local[g][1], keys[g], values[g], middle[g], *carried[g],
            use, start, end, token, *done,
        )
        return spread[g][1]

    def chain(g, state):
        *carried[g], _ = yield from scan(*state, bits, False)
        middle[g], *state = call(
            middle_kernel,
            [VMEM] * 8,
            [narrow, (VMEM, shape(rows, E)), (VMEM, shape(extra, E))],
        )(*local[g][1:], local[g][0], *carried[g], use, flag)
        return (yield from scan(*state, bits, True))

    count = levels + 2
    later = rounds(
        chain(0, first),
        chain(1, second),
        {
            1: functools.partial(local_of, 0),
            3: functools.partial(local_of, 1),
            count + 1: functools.partial(spread_of, 0),
            count + 3: functools.partial(spread_of, 1),
        },
    )
    grads = ()
    for g in groups:
        grads = call(
            final_kernel,
            [VMEM] * 7 + [ANY] * len(grads),
            [(ANY, shape(tokens, width, BF16))] * 2,
            [staging, staging, copies(pairs, 2)],
            {7: 0, 8: 1} if grads else {},
            group=g,
        )(keys[g], values[g], *spread[g][1:], *later[g][:2], tail, *grads)
    total = jnp.concatenate([later[g][2] for g in groups])
    gain_grad = total.reshape(width) / math.sqrt(tokens * lax.axis_size("ctx"))
    return spread[1][0], *grads, gain_grad


def solution(mesh):
    tokens = P(("parts", "ctx"), None)
    return jax.shard_map(
        shards,
        mesh=mesh,
        in_specs=(tokens, tokens, tokens, tokens, P(), P(None, ("parts", "ctx"))),
        out_specs=(tokens, tokens, tokens, P("parts")),
        check_vma=False,
    )
```

time: 132 us -> 83.2 us (0.63)
  waiting for transfers between devices: 67.6 us -> 16.4 us
  starting transfers between devices: 16.1 us -> 41.7 us
  other arithmetic: 14.6 us -> 1.69 us
  Pallas kernels: 27.3 us -> 21.3 us
  local copies, waits for them, and re-layouts: 3.94 us -> 0.03 us
    ppermute x12 -> x24, waiting for transfers between devices: 67.6 us -> 16.4 us  [swap(): return lax.ppermute(block, 'ctx', [(i, i ^ distance) for i in range(count)])]
    ppermute x12 -> x24, starting transfers between devices: 16.1 us -> 41.7 us  [swap(): return lax.ppermute(block, 'ctx', [(i, i ^ distance) for i in range(count)])]
    pallas_call x3 -> x10, Pallas kernels: 27.3 us -> 21.3 us  [the longest x2 6.32 us: spread_of(): call(spread_kernel, [VMEM] * 9 + [ANY] * (1 + len(done)), [(ANY, shape(to...]
    unnamed x28 -> x0, local copies, waits for them, and re-layouts: 3.89 us -> none
    select_n x2 -> x6, other arithmetic: 2.62 us -> 0.39 us  [scan(): jnp.where(second, after, before)]
    select_n x2, other arithmetic: 2.33 us -> 0.12 us  [scan(): jnp.where(second, before, after)]
    add x2 -> x6, other arithmetic: 1.4 us -> 0.02 us  [scan(): extra = extra + got[half + FLAG:]]
    mul x4, other arithmetic: 1.38 us -> 0.02 us  [the longest x2 0.01 us: scan(): before = jnp.where(second, before + (1.0 - before_flag) * got_total, before)]
  transfers between devices with their start and end apart: 12 -> 24, of which waited for: 12 -> 14; matrix products, arithmetic and copies ran while one was open for 1% -> 1% of each run, Pallas kernels for 0% -> 20%
where the time goes in v2:
time: 83.2 us; the launch traced here: 82.4 us
  starting transfers between devices  41.7 us (50%)
  Pallas kernels  21.3 us (26%)
  waiting for transfers between devices  16.4 us (20%)
  other arithmetic  1.69 us (2%)
  between operations  1.24 us (1%)
    ppermute x24, starting transfers between devices, swap(): return lax.ppermute(block, 'ctx', [(i, i ^ distance) for i in range(count)])  41.7 us
    ppermute x24, waiting for transfers between devices, swap(): return lax.ppermute(block, 'ctx', [(i, i ^ distance) for i in range(count)])  16.4 us
    pallas_call x2, Pallas kernels, spread_of(): call(spread_kernel, [VMEM] * 9 + [ANY] * (1 + len(done)), [(ANY, shape(to...  6.32 us
    pallas_call x2, Pallas kernels, local_of(): call(local_kernel, [ANY] * 3 + [VMEM] * 3 + [ANY], [single, narrow, narro...  5.49 us
    pallas_call x2, Pallas kernels, chain(): call(middle_kernel, [VMEM] * 8, [narrow, (VMEM, shape(rows, E)), (VMEM, s...  2.82 us
    pallas_call x2, Pallas kernels, shards(): call(final_kernel, [VMEM] * 7 + [ANY] * len(grads), [(ANY, shape(tokens,...  2.66 us
    pallas_call x1, Pallas kernels, shards(): call(first_state_kernel, [ANY] * 3, states + [narrow] * 2 + [(VMEM, shape...  2 us
    pallas_call x1, Pallas kernels, shards(): call(state_kernel, [ANY] * 2 + [VMEM] * 2, states + [narrow] * 2, [copies...  1.98 us
  transfers between devices with their start and end apart: 24, of which 14 were waited for; matrix products, arithmetic and copies ran while one was open for 1% of the time, Pallas kernels for 20%

profile of v2, /device:TPU:1, one launch (start us, length us, event | category | flops | bytes accessed | tf_op | source)
XLA Modules:
  0.0 82.4 jit_solution(5960892138466116018)
XLA Ops:
  0.6 2.0 %shard_map.93 = (f32[512,128]{1,0:T(8,128)S(1)}, f32[520,128]{1,0:T(8,128)S(1)}, bf16[256,1024]{1,0:T(8,128)(2,1)S(1)}, bf16[256,1024]{1,0:T(8,128)(2,1)S(1)}, s...) custom-call(s32[2,2]{1,0:T(2,128)} %bounds_hbm.1, ...), custom_call_target="tpu_custom_call" | custom-call | tf_op jit(solution)/shard_map/pallas_call | solution.py:374
  2.8 2.0 %shard_map.94 = (f32[512,128]{1,0:T(8,128)S(1)}, f32[520,128]{1,0:T(8,128)S(1)}, bf16[256,1024]{1,0:T(8,128)(2,1)S(1)}, bf16[256,1024]{1,0:T(8,128)(2,1)S(1)}) custom-call(bf16[256,2048]{1,0:T(8,128)(2,1)} %k_hbm.3, bf16[256,2048]{1,0:T(8,128)(2,1)} %v_hbm.3, bf16[256,128]{1,0:T(8,128)(2,1)S(1)} %get-tuple-element.64.tail_ref, ...), custom_call_target="tpu_custom_call" | custom-call | tf_op jit(solution)/shard_map/pallas_call | solution.py:383
  5.4 2.3 %collective-permute-start.1 = (f32[264,128]{1,0:T(8,128)S(1)}, f32[264,128]{1,0:T(8,128)S(1)}, u32[]{:S(2)}, u32[]{:S(2)}) collective-permute-start(f32[264,128]{1,0:T(8,128)S(1)} %pad_maximum_fusion.10._), channel_id=1, source_target_pairs={{0,2},{1,3},{2,0},{3,1},{4,6},{5,7},{6,4},{7,5},{8,10},{9,11},{10,... | collective-permute-start | bytes 405512 | tf_op jit(solution)/shard_map/ppermute | solution.py:248
  7.7 2.7 %shard_map.95 = (f32[256,1024]{1,0:T(8,128)S(1)}, bf16[256,1024]{1,0:T(8,128)(2,1)S(1)}, bf16[256,1024]{1,0:T(8,128)(2,1)S(1)}, f32[1,1024]{1,0:T(1,128)S(1)}) custom-call(bf16[256,2048]{1,0:T(8,128)(2,1)} %q_hbm.3, bf16[256,2048]{1,0:T(8,128)(2,1)} %g_hbm.3, f32[1,2048]{1,0:T(1,128)} %bitcast.95, bf16[256,1024]{1,0:T(8,128)(2,1)S(1)} %get-tuple-element.76.k_ref, ...), custom_call_target="tpu_custom_call" | custom-call | tf_op jit(solution)/shard_map/pallas_call | solution.py:389
  11.4 1.3 %collective-permute-start.3 = (f32[264,128]{1,0:T(8,128)S(1)}, f32[264,128]{1,0:T(8,128)S(1)}, u32[]{:S(2)}, u32[]{:S(2)}) collective-permute-start(f32[264,128]{1,0:T(8,128)S(1)} %pad_maximum_fusion.11), channel_id=1, source_target_pairs={{0,4},{1,5},{2,6},{3,7},{4,0},{5,1},{6,2},{7,3},{8,12},{9,13},{10,... | collective-permute-start | bytes 405512 | tf_op jit(solution)/shard_map/ppermute | solution.py:248
  12.7 1.2 %collective-permute-start.4 = (f32[264,128]{1,0:T(8,128)S(1)}, f32[264,128]{1,0:T(8,128)S(1)}, u32[]{:S(2)}, u32[]{:S(2)}) collective-permute-start(f32[264,128]{1,0:T(8,128)S(1)} %pad_maximum_fusion.12), channel_id=1, source_target_pairs={{0,2},{1,3},{2,0},{3,1},{4,6},{5,7},{6,4},{7,5},{8,10},{9,11},{10,... | collective-permute-start | bytes 405512 | tf_op jit(solution)/shard_map/ppermute | solution.py:248
  13.9 1.4 %collective-permute-done.3 = f32[264,128]{1,0:T(8,128)S(1)} collective-permute-done((f32[264,128]{1,0:T(8,128)S(1)}, f32[264,128]{1,0:T(8,128)S(1)}, u32[]{:S(2)}, u32[]{:S(2)}) %collective-permute-start.3) | collective-permute-done | bytes 135200 | tf_op jit(solution)/shard_map/ppermute | solution.py:248
  15.4 1.5 %collective-permute-done.4 = f32[264,128]{1,0:T(8,128)S(1)} collective-permute-done((f32[264,128]{1,0:T(8,128)S(1)}, f32[264,128]{1,0:T(8,128)S(1)}, u32[]{:S(2)}, u32[]{:S(2)}) %collective-permute-start.4) | collective-permute-done | bytes 135200 | tf_op jit(solution)/shard_map/ppermute | solution.py:248
  17.1 2.4 %collective-permute-start.6 = (f32[264,128]{1,0:T(8,128)S(1)}, f32[264,128]{1,0:T(8,128)S(1)}, u32[]{:S(2)}, u32[]{:S(2)}) collective-permute-start(f32[264,128]{1,0:T(8,128)S(1)} %pad_maximum_fusion.13._), channel_id=1, source_target_pairs={{0,8},{1,9},{2,10},{3,11},{4,12},{5,13},{6,14},{7,15},{8,0},{9,1},... | collective-permute-start | bytes 405512 | tf_op jit(solution)/shard_map/ppermute | solution.py:248
  19.4 2.7 %shard_map.96 = (f32[256,1024]{1,0:T(8,128)S(1)}, bf16[256,1024]{1,0:T(8,128)(2,1)S(1)}, bf16[256,1024]{1,0:T(8,128)(2,1)S(1)}, f32[1,1024]{1,0:T(1,128)S(1)}) custom-call(bf16[256,2048]{1,0:T(8,128)(2,1)} %q_hbm.3, bf16[256,2048]{1,0:T(8,128)(2,1)} %g_hbm.3, f32[1,2048]{1,0:T(1,128)} %bitcast.96, bf16[256,1024]{1,0:T(8,128)(2,1)S(1)} %get-tuple-element.66.k_ref, ...), custom_call_target="tpu_custom_call" | custom-call | tf_op jit(solution)/shard_map/pallas_call | solution.py:389
  22.6 1.2 %collective-permute-start.8 = (f32[256,128]{1,0:T(8,128)S(1)}, f32[256,128]{1,0:T(8,128)S(1)}, u32[]{:S(2)}, u32[]{:S(2)}) collective-permute-start(f32[256,128]{1,0:T(8,128)S(1)} %get-tuple-element.88), channel_id=1, source_target_pairs={{0,2},{1,3},{2,0},{3,1},{4,6},{5,7},{6,4},{7,5},{8,10},{9,11},{10,... | collective-permute-start | bytes 393224 | tf_op jit(solution)/shard_map/ppermute | solution.py:248
  23.8 2.7 %collective-permute-start.7 = (f32[264,128]{1,0:T(8,128)S(1)}, f32[264,128]{1,0:T(8,128)S(1)}, u32[]{:S(2)}, u32[]{:S(2)}) collective-permute-start(f32[264,128]{1,0:T(8,128)S(1)} %pad_maximum_fusion.15), channel_id=1, source_target_pairs={{0,8},{1,9},{2,10},{3,11},{4,12},{5,13},{6,14},{7,15},{8,0},{9,1},... | collective-permute-start | bytes 405512 | tf_op jit(solution)/shard_map/ppermute | solution.py:248
  26.6 2.3 %collective-permute-done.7 = f32[264,128]{1,0:T(8,128)S(1)} collective-permute-done((f32[264,128]{1,0:T(8,128)S(1)}, f32[264,128]{1,0:T(8,128)S(1)}, u32[]{:S(2)}, u32[]{:S(2)}) %collective-permute-start.7) | collective-permute-done | bytes 135200 | tf_op jit(solution)/shard_map/ppermute | solution.py:248
  28.9 2.6 %collective-permute-start.9 = (f32[256,128]{1,0:T(8,128)S(1)}, f32[256,128]{1,0:T(8,128)S(1)}, u32[]{:S(2)}, u32[]{:S(2)}) collective-permute-start(f32[256,128]{1,0:T(8,128)S(1)} %get-tuple-element.89), channel_id=1, source_target_pairs={{0,2},{1,3},{2,0},{3,1},{4,6},{5,7},{6,4},{7,5},{8,10},{9,11},{10,... | collective-permute-start | bytes 393224 | tf_op jit(solution)/shard_map/ppermute | solution.py:248
  31.5 3.2 %collective-permute-start.10 = (f32[512,128]{1,0:T(8,128)S(1)}, f32[512,128]{1,0:T(8,128)S(1)}, u32[]{:S(2)}, u32[]{:S(2)}) collective-permute-start(f32[512,128]{1,0:T(8,128)S(1)} %get-tuple-element.93), channel_id=1, source_target_pairs={{0,1},{1,0},{2,3},{3,2},{4,5},{5,4},{6,7},{7,6},{8,9},{9,8},{10,11... | collective-permute-start | bytes 786440 | tf_op jit(solution)/shard_map/ppermute | solution.py:248
  35.9 1.4 %shard_map.97 = (bf16[256,1024]{1,0:T(8,128)(2,1)S(1)}, f32[512,128]{1,0:T(8,128)S(1)}, f32[528,128]{1,0:T(8,128)S(1)}) custom-call(bf16[256,1024]{1,0:T(8,128)(2,1)S(1)} %get-tuple-element.90.q_ref, bf16[256,1024]{1,0:T(8,128)(2,1)S(1)} %get-tuple-element.91.g_ref, f32[1,1024]{1,0:T(1,128)S(1)} %get-tuple-element.92.gain_ref, ...), custom_call_target="tpu_custom_call" | custom-call | tf_op jit(solution)/shard_map/pallas_call | solution.py:415
  37.3 3.4 %collective-permute-start.12 = (f32[528,128]{1,0:T(8,128)S(1)}, f32[528,128]{1,0:T(8,128)S(1)}, u32[]{:S(2)}, u32[]{:S(2)}) collective-permute-start(f32[528,128]{1,0:T(8,128)S(1)} %get-tuple-element.100), channel_id=1, source_target_pairs={{0,1},{1,0},{2,3},{3,2},{4,5},{5,4},{6,7},{7,6},{8,9},{9,8},{10,11... | collective-permute-start | bytes 811016 | tf_op jit(solution)/shard_map/ppermute | solution.py:248
  40.9 1.5 %collective-permute-done.11.got_ref = f32[512,128]{1,0:T(8,128)S(1)} collective-permute-done((f32[512,128]{1,0:T(8,128)S(1)}, f32[512,128]{1,0:T(8,128)S(1)}, u32[]{:S(2)}, u32[]{:S(2)}) %collective-permute-start.11) | collective-permute-done | bytes 262176 | tf_op jit(solution)/shard_map/ppermute | solution.py:248
  42.3 1.4 %shard_map.98 = (bf16[256,1024]{1,0:T(8,128)(2,1)S(1)}, f32[512,128]{1,0:T(8,128)S(1)}, f32[528,128]{1,0:T(8,128)S(1)}) custom-call(bf16[256,1024]{1,0:T(8,128)(2,1)S(1)} %get-tuple-element.82.q_ref, bf16[256,1024]{1,0:T(8,128)(2,1)S(1)} %get-tuple-element.83.g_ref, f32[1,1024]{1,0:T(1,128)S(1)} %get-tuple-element.84.gain_ref, ...), custom_call_target="tpu_custom_call" | custom-call | tf_op jit(solution)/shard_map/pallas_call | solution.py:415
  44.8 3.1 %shard_map.99 = (bf16[256,2048]{1,0:T(8,128)(2,1)}, f32[256,1024]{1,0:T(8,128)S(1)}, f32[256,1024]{1,0:T(8,128)S(1)}) custom-call(bf16[256,1024]{1,0:T(8,128)(2,1)S(1)} %get-tuple-element.90.q_ref, bf16[256,1024]{1,0:T(8,128)(2,1)S(1)} %get-tuple-element.76.k_ref, bf16[256,1024]{1,0:T(8,128)(2,1)S(1)} %get-tuple-element.77.v_ref, ...), custom_call_target="tpu_custom_call" | custom-call | tf_op jit(solution)/shard_map/pallas_call | solution.py:400
  49.0 1.9 %collective-permute-start.15 = (f32[272,128]{1,0:T(8,128)S(1)}, f32[272,128]{1,0:T(8,128)S(1)}, u32[]{:S(2)}, u32[]{:S(2)}) collective-permute-start(f32[272,128]{1,0:T(8,128)S(1)} %pad_maximum_fusion.5), channel_id=1, source_target_pairs={{0,4},{1,5},{2,6},{3,7},{4,0},{5,1},{6,2},{7,3},{8,12},{9,13},{10,... | collective-permute-start | bytes 417800 | tf_op jit(solution)/shard_map/ppermute | solution.py:248
  51.2 2.5 %collective-permute-done.15 = f32[272,128]{1,0:T(8,128)S(1)} collective-permute-done((f32[272,128]{1,0:T(8,128)S(1)}, f32[272,128]{1,0:T(8,128)S(1)}, u32[]{:S(2)}, u32[]{:S(2)}) %collective-permute-start.15) | collective-permute-done | bytes 139296 | tf_op jit(solution)/shard_map/ppermute | solution.py:248
  53.6 1.4 %collective-permute-done.16 = f32[272,128]{1,0:T(8,128)S(1)} collective-permute-done((f32[272,128]{1,0:T(8,128)S(1)}, f32[272,128]{1,0:T(8,128)S(1)}, u32[]{:S(2)}, u32[]{:S(2)}) %collective-permute-start.16) | collective-permute-done | bytes 139296 | tf_op jit(solution)/shard_map/ppermute | solution.py:248
  55.3 2.6 %collective-permute-start.18 = (f32[272,128]{1,0:T(8,128)S(1)}, f32[272,128]{1,0:T(8,128)S(1)}, u32[]{:S(2)}, u32[]{:S(2)}) collective-permute-start(f32[272,128]{1,0:T(8,128)S(1)} %pad_maximum_fusion.7.rest_0_), channel_id=1, source_target_pairs={{0,8},{1,9},{2,10},{3,11},{4,12},{5,13},{6,14},{7,15},{8,0},{9,1},... | collective-permute-start | bytes 417800 | tf_op jit(solution)/shard_map/ppermute | solution.py:248
  57.9 3.3 %shard_map.100 = (bf16[256,2048]{1,0:T(8,128)(2,1)}, f32[256,1024]{1,0:T(8,128)S(1)}, f32[256,1024]{1,0:T(8,128)S(1)}) custom-call(bf16[256,1024]{1,0:T(8,128)(2,1)S(1)} %get-tuple-element.82.q_ref, bf16[256,1024]{1,0:T(8,128)(2,1)S(1)} %get-tuple-element.66.k_ref, bf16[256,1024]{1,0:T(8,128)(2,1)S(1)} %get-tuple-element.67.v_ref, ...), custom_call_target="tpu_custom_call", output_to_operand_aliasing={{0}: (10, {})} | custom-call | tf_op jit(solution)/shard_map/pallas_call | solution.py:400
  61.7 3.1 %collective-permute-start.19 = (f32[272,128]{1,0:T(8,128)S(1)}, f32[272,128]{1,0:T(8,128)S(1)}, u32[]{:S(2)}, u32[]{:S(2)}) collective-permute-start(f32[272,128]{1,0:T(8,128)S(1)} %pad_maximum_fusion.9), channel_id=1, source_target_pairs={{0,8},{1,9},{2,10},{3,11},{4,12},{5,13},{6,14},{7,15},{8,0},{9,1},... | collective-permute-start | bytes 417800 | tf_op jit(solution)/shard_map/ppermute | solution.py:248
  65.4 1.9 %collective-permute-done.19 = f32[272,128]{1,0:T(8,128)S(1)} collective-permute-done((f32[272,128]{1,0:T(8,128)S(1)}, f32[272,128]{1,0:T(8,128)S(1)}, u32[]{:S(2)}, u32[]{:S(2)}) %collective-permute-start.19) | collective-permute-done | bytes 139296 | tf_op jit(solution)/shard_map/ppermute | solution.py:248
  67.4 1.2 %collective-permute-start.21 = (f32[256,128]{1,0:T(8,128)S(1)}, f32[256,128]{1,0:T(8,128)S(1)}, u32[]{:S(2)}, u32[]{:S(2)}) collective-permute-start(f32[256,128]{1,0:T(8,128)S(1)} %get-tuple-element.117), channel_id=1, source_target_pairs={{0,2},{1,3},{2,0},{3,1},{4,6},{5,7},{6,4},{7,5},{8,10},{9,11},{10,... | collective-permute-start | bytes 393224 | tf_op jit(solution)/shard_map/ppermute | solution.py:248
  68.7 5.3 %collective-permute-start.23 = (f32[512,128]{1,0:T(8,128)S(1)}, f32[512,128]{1,0:T(8,128)S(1)}, u32[]{:S(2)}, u32[]{:S(2)}) collective-permute-start(f32[512,128]{1,0:T(8,128)S(1)} %get-tuple-element.119), channel_id=1, source_target_pairs={{0,1},{1,0},{2,3},{3,2},{4,5},{5,4},{6,7},{7,6},{8,9},{9,8},{10,11... | collective-permute-start | bytes 786440 | tf_op jit(solution)/shard_map/ppermute | solution.py:248
  74.0 4.9 %collective-permute-start.22 = (f32[512,128]{1,0:T(8,128)S(1)}, f32[512,128]{1,0:T(8,128)S(1)}, u32[]{:S(2)}, u32[]{:S(2)}) collective-permute-start(f32[512,128]{1,0:T(8,128)S(1)} %get-tuple-element.134), channel_id=1, source_target_pairs={{0,1},{1,0},{2,3},{3,2},{4,5},{5,4},{6,7},{7,6},{8,9},{9,8},{10,11... | collective-permute-start | bytes 786440 | tf_op jit(solution)/shard_map/ppermute | solution.py:248
  79.5 1.3 %shard_map.101 = (bf16[256,2048]{1,0:T(8,128)(2,1)}, bf16[256,2048]{1,0:T(8,128)(2,1)}) custom-call(bf16[256,1024]{1,0:T(8,128)(2,1)S(1)} %get-tuple-element.76.k_ref, bf16[256,1024]{1,0:T(8,128)(2,1)S(1)} %get-tuple-element.77.v_ref, f32[256,1024]{1,0:T(8,128)S(1)} %get-tuple-element.106.kp_ref, f32[256,1024]{1,0:T(8,128)S(1)} %get-tuple-element.118.vp_ref, ...), custom_call_target="tpu_custom_call" | custom-call | tf_op jit(solution)/shard_map/pallas_call | solution.py:435
  80.9 1.3 %shard_map.102 = (bf16[256,2048]{1,0:T(8,128)(2,1)}, bf16[256,2048]{1,0:T(8,128)(2,1)}) custom-call(bf16[256,1024]{1,0:T(8,128)(2,1)S(1)} %get-tuple-element.66.k_ref, bf16[256,1024]{1,0:T(8,128)(2,1)S(1)} %get-tuple-element.67.v_ref, f32[256,1024]{1,0:T(8,128)S(1)} %get-tuple-element.112.kp_ref, ...), custom_call_target="tpu_custom_call", output_to_operand_aliasing={{0}: (7, {}), {1}: (8, {})} | custom-call | tf_op jit(solution)/shard_map/pallas_call | solution.py:435
  (83 shorter events, 8.0 us)
Async XLA Ops:
  2.6 2.1 %collective-permute-start = (f32[520,128]{1,0:T(8,128)S(1)}, f32[520,128]{1,0:T(8,128)S(1)}, u32[]{:S(2)}, u32[]{:S(2)}) collective-permute-start(f32[520,128]{1,0:T(8,128)S(1)} %get-tuple-element.71), channel_id=1, source_target_pairs={{0,1},{1,0},{2,3},{3,2},{4,5},{5,4},{6,7},{7,6},{8,9},{9,8},{10,11... | collective-permute-start | bytes 798728 | tf_op jit(solution)/shard_map/ppermute | solution.py:248
  4.9 6.4 %collective-permute-start.2 = (f32[520,128]{1,0:T(8,128)S(1)}, f32[520,128]{1,0:T(8,128)S(1)}, u32[]{:S(2)}, u32[]{:S(2)}) collective-permute-start(f32[520,128]{1,0:T(8,128)S(1)} %get-tuple-element.75), channel_id=1, source_target_pairs={{0,1},{1,0},{2,3},{3,2},{4,5},{5,4},{6,7},{7,6},{8,9},{9,8},{10,11... | collective-permute-start | bytes 798728 | tf_op jit(solution)/shard_map/ppermute | solution.py:248
  5.4 5.9 %collective-permute-start.1 = (f32[264,128]{1,0:T(8,128)S(1)}, f32[264,128]{1,0:T(8,128)S(1)}, u32[]{:S(2)}, u32[]{:S(2)}) collective-permute-start(f32[264,128]{1,0:T(8,128)S(1)} %pad_maximum_fusion.10._), channel_id=1, source_target_pairs={{0,2},{1,3},{2,0},{3,1},{4,6},{5,7},{6,4},{7,5},{8,10},{9,11},{10,... | collective-permute-start | bytes 405512 | tf_op jit(solution)/shard_map/ppermute | solution.py:248
  11.4 3.9 %collective-permute-start.3 = (f32[264,128]{1,0:T(8,128)S(1)}, f32[264,128]{1,0:T(8,128)S(1)}, u32[]{:S(2)}, u32[]{:S(2)}) collective-permute-start(f32[264,128]{1,0:T(8,128)S(1)} %pad_maximum_fusion.11), channel_id=1, source_target_pairs={{0,4},{1,5},{2,6},{3,7},{4,0},{5,1},{6,2},{7,3},{8,12},{9,13},{10,... | collective-permute-start | bytes 405512 | tf_op jit(solution)/shard_map/ppermute | solution.py:248
  12.7 4.2 %collective-permute-start.4 = (f32[264,128]{1,0:T(8,128)S(1)}, f32[264,128]{1,0:T(8,128)S(1)}, u32[]{:S(2)}, u32[]{:S(2)}) collective-permute-start(f32[264,128]{1,0:T(8,128)S(1)} %pad_maximum_fusion.12), channel_id=1, source_target_pairs={{0,2},{1,3},{2,0},{3,1},{4,6},{5,7},{6,4},{7,5},{8,10},{9,11},{10,... | collective-permute-start | bytes 405512 | tf_op jit(solution)/shard_map/ppermute | solution.py:248
  17.0 5.4 %collective-permute-start.5 = (f32[264,128]{1,0:T(8,128)S(1)}, f32[264,128]{1,0:T(8,128)S(1)}, u32[]{:S(2)}, u32[]{:S(2)}) collective-permute-start(f32[264,128]{1,0:T(8,128)S(1)} %pad_maximum_fusion.14), channel_id=1, source_target_pairs={{0,4},{1,5},{2,6},{3,7},{4,0},{5,1},{6,2},{7,3},{8,12},{9,13},{10,... | collective-permute-start | bytes 405512 | tf_op jit(solution)/shard_map/ppermute | solution.py:248
  17.1 5.4 %collective-permute-start.6 = (f32[264,128]{1,0:T(8,128)S(1)}, f32[264,128]{1,0:T(8,128)S(1)}, u32[]{:S(2)}, u32[]{:S(2)}) collective-permute-start(f32[264,128]{1,0:T(8,128)S(1)} %pad_maximum_fusion.13._), channel_id=1, source_target_pairs={{0,8},{1,9},{2,10},{3,11},{4,12},{5,13},{6,14},{7,15},{8,0},{9,1},... | collective-permute-start | bytes 405512 | tf_op jit(solution)/shard_map/ppermute | solution.py:248
  22.6 3.9 %collective-permute-start.8 = (f32[256,128]{1,0:T(8,128)S(1)}, f32[256,128]{1,0:T(8,128)S(1)}, u32[]{:S(2)}, u32[]{:S(2)}) collective-permute-start(f32[256,128]{1,0:T(8,128)S(1)} %get-tuple-element.88), channel_id=1, source_target_pairs={{0,2},{1,3},{2,0},{3,1},{4,6},{5,7},{6,4},{7,5},{8,10},{9,11},{10,... | collective-permute-start | bytes 393224 | tf_op jit(solution)/shard_map/ppermute | solution.py:248
  23.8 5.1 %collective-permute-start.7 = (f32[264,128]{1,0:T(8,128)S(1)}, f32[264,128]{1,0:T(8,128)S(1)}, u32[]{:S(2)}, u32[]{:S(2)}) collective-permute-start(f32[264,128]{1,0:T(8,128)S(1)} %pad_maximum_fusion.15), channel_id=1, source_target_pairs={{0,8},{1,9},{2,10},{3,11},{4,12},{5,13},{6,14},{7,15},{8,0},{9,1},... | collective-permute-start | bytes 405512 | tf_op jit(solution)/shard_map/ppermute | solution.py:248
  28.9 5.8 %collective-permute-start.9 = (f32[256,128]{1,0:T(8,128)S(1)}, f32[256,128]{1,0:T(8,128)S(1)}, u32[]{:S(2)}, u32[]{:S(2)}) collective-permute-start(f32[256,128]{1,0:T(8,128)S(1)} %get-tuple-element.89), channel_id=1, source_target_pairs={{0,2},{1,3},{2,0},{3,1},{4,6},{5,7},{6,4},{7,5},{8,10},{9,11},{10,... | collective-permute-start | bytes 393224 | tf_op jit(solution)/shard_map/ppermute | solution.py:248
  31.5 4.4 %collective-permute-start.10 = (f32[512,128]{1,0:T(8,128)S(1)}, f32[512,128]{1,0:T(8,128)S(1)}, u32[]{:S(2)}, u32[]{:S(2)}) collective-permute-start(f32[512,128]{1,0:T(8,128)S(1)} %get-tuple-element.93), channel_id=1, source_target_pairs={{0,1},{1,0},{2,3},{3,2},{4,5},{5,4},{6,7},{7,6},{8,9},{9,8},{10,11... | collective-permute-start | bytes 786440 | tf_op jit(solution)/shard_map/ppermute | solution.py:248
  37.3 6.4 %collective-permute-start.12 = (f32[528,128]{1,0:T(8,128)S(1)}, f32[528,128]{1,0:T(8,128)S(1)}, u32[]{:S(2)}, u32[]{:S(2)}) collective-permute-start(f32[528,128]{1,0:T(8,128)S(1)} %get-tuple-element.100), channel_id=1, source_target_pairs={{0,1},{1,0},{2,3},{3,2},{4,5},{5,4},{6,7},{7,6},{8,9},{9,8},{10,11... | collective-permute-start | bytes 811016 | tf_op jit(solution)/shard_map/ppermute | solution.py:248
  40.8 1.5 %collective-permute-start.11 = (f32[512,128]{1,0:T(8,128)S(1)}, f32[512,128]{1,0:T(8,128)S(1)}, u32[]{:S(2)}, u32[]{:S(2)}) collective-permute-start(f32[512,128]{1,0:T(8,128)S(1)} %get-tuple-element.96), channel_id=1, source_target_pairs={{0,1},{1,0},{2,3},{3,2},{4,5},{5,4},{6,7},{7,6},{8,9},{9,8},{10,11... | collective-permute-start | bytes 786440 | tf_op jit(solution)/shard_map/ppermute | solution.py:248
  43.9 4.9 %collective-permute-start.13 = (f32[272,128]{1,0:T(8,128)S(1)}, f32[272,128]{1,0:T(8,128)S(1)}, u32[]{:S(2)}, u32[]{:S(2)}) collective-permute-start(f32[272,128]{1,0:T(8,128)S(1)} %pad_maximum_fusion.4.rest_0_), channel_id=1, source_target_pairs={{0,2},{1,3},{2,0},{3,1},{4,6},{5,7},{6,4},{7,5},{8,10},{9,11},{10,... | collective-permute-start | bytes 417800 | tf_op jit(solution)/shard_map/ppermute | solution.py:248
  44.1 4.7 %collective-permute-start.14 = (f32[528,128]{1,0:T(8,128)S(1)}, f32[528,128]{1,0:T(8,128)S(1)}, u32[]{:S(2)}, u32[]{:S(2)}) collective-permute-start(f32[528,128]{1,0:T(8,128)S(1)} %get-tuple-element.104), channel_id=1, source_target_pairs={{0,1},{1,0},{2,3},{3,2},{4,5},{5,4},{6,7},{7,6},{8,9},{9,8},{10,11... | collective-permute-start | bytes 811016 | tf_op jit(solution)/shard_map/ppermute | solution.py:248
  49.0 4.7 %collective-permute-start.15 = (f32[272,128]{1,0:T(8,128)S(1)}, f32[272,128]{1,0:T(8,128)S(1)}, u32[]{:S(2)}, u32[]{:S(2)}) collective-permute-start(f32[272,128]{1,0:T(8,128)S(1)} %pad_maximum_fusion.5), channel_id=1, source_target_pairs={{0,4},{1,5},{2,6},{3,7},{4,0},{5,1},{6,2},{7,3},{8,12},{9,13},{10,... | collective-permute-start | bytes 417800 | tf_op jit(solution)/shard_map/ppermute | solution.py:248
  50.8 4.2 %collective-permute-start.16 = (f32[272,128]{1,0:T(8,128)S(1)}, f32[272,128]{1,0:T(8,128)S(1)}, u32[]{:S(2)}, u32[]{:S(2)}) collective-permute-start(f32[272,128]{1,0:T(8,128)S(1)} %pad_maximum_fusion.6), channel_id=1, source_target_pairs={{0,2},{1,3},{2,0},{3,1},{4,6},{5,7},{6,4},{7,5},{8,10},{9,11},{10,... | collective-permute-start | bytes 417800 | tf_op jit(solution)/shard_map/ppermute | solution.py:248
  55.2 5.9 %collective-permute-start.17 = (f32[272,128]{1,0:T(8,128)S(1)}, f32[272,128]{1,0:T(8,128)S(1)}, u32[]{:S(2)}, u32[]{:S(2)}) collective-permute-start(f32[272,128]{1,0:T(8,128)S(1)} %pad_maximum_fusion.8), channel_id=1, source_target_pairs={{0,4},{1,5},{2,6},{3,7},{4,0},{5,1},{6,2},{7,3},{8,12},{9,13},{10,... | collective-permute-start | bytes 417800 | tf_op jit(solution)/shard_map/ppermute | solution.py:248
  55.3 6.1 %collective-permute-start.18 = (f32[272,128]{1,0:T(8,128)S(1)}, f32[272,128]{1,0:T(8,128)S(1)}, u32[]{:S(2)}, u32[]{:S(2)}) collective-permute-start(f32[272,128]{1,0:T(8,128)S(1)} %pad_maximum_fusion.7.rest_0_), channel_id=1, source_target_pairs={{0,8},{1,9},{2,10},{3,11},{4,12},{5,13},{6,14},{7,15},{8,0},{9,1},... | collective-permute-start | bytes 417800 | tf_op jit(solution)/shard_map/ppermute | solution.py:248
  61.5 3.9 %collective-permute-start.20 = (f32[256,128]{1,0:T(8,128)S(1)}, f32[256,128]{1,0:T(8,128)S(1)}, u32[]{:S(2)}, u32[]{:S(2)}) collective-permute-start(f32[256,128]{1,0:T(8,128)S(1)} %get-tuple-element.116), channel_id=1, source_target_pairs={{0,2},{1,3},{2,0},{3,1},{4,6},{5,7},{6,4},{7,5},{8,10},{9,11},{10,... | collective-permute-start | bytes 393224 | tf_op jit(solution)/shard_map/ppermute | solution.py:248
  61.7 5.7 %collective-permute-start.19 = (f32[272,128]{1,0:T(8,128)S(1)}, f32[272,128]{1,0:T(8,128)S(1)}, u32[]{:S(2)}, u32[]{:S(2)}) collective-permute-start(f32[272,128]{1,0:T(8,128)S(1)} %pad_maximum_fusion.9), channel_id=1, source_target_pairs={{0,8},{1,9},{2,10},{3,11},{4,12},{5,13},{6,14},{7,15},{8,0},{9,1},... | collective-permute-start | bytes 417800 | tf_op jit(solution)/shard_map/ppermute | solution.py:248
  67.4 6.5 %collective-permute-start.21 = (f32[256,128]{1,0:T(8,128)S(1)}, f32[256,128]{1,0:T(8,128)S(1)}, u32[]{:S(2)}, u32[]{:S(2)}) collective-permute-start(f32[256,128]{1,0:T(8,128)S(1)} %get-tuple-element.117), channel_id=1, source_target_pairs={{0,2},{1,3},{2,0},{3,1},{4,6},{5,7},{6,4},{7,5},{8,10},{9,11},{10,... | collective-permute-start | bytes 393224 | tf_op jit(solution)/shard_map/ppermute | solution.py:248
  68.7 10.9 %collective-permute-start.23 = (f32[512,128]{1,0:T(8,128)S(1)}, f32[512,128]{1,0:T(8,128)S(1)}, u32[]{:S(2)}, u32[]{:S(2)}) collective-permute-start(f32[512,128]{1,0:T(8,128)S(1)} %get-tuple-element.119), channel_id=1, source_target_pairs={{0,1},{1,0},{2,3},{3,2},{4,5},{5,4},{6,7},{7,6},{8,9},{9,8},{10,11... | collective-permute-start | bytes 786440 | tf_op jit(solution)/shard_map/ppermute | solution.py:248
  74.0 6.9 %collective-permute-start.22 = (f32[512,128]{1,0:T(8,128)S(1)}, f32[512,128]{1,0:T(8,128)S(1)}, u32[]{:S(2)}, u32[]{:S(2)}) collective-permute-start(f32[512,128]{1,0:T(8,128)S(1)} %get-tuple-element.134), channel_id=1, source_target_pairs={{0,1},{1,0},{2,3},{3,2},{4,5},{5,4},{6,7},{7,6},{8,9},{9,8},{10,11... | collective-permute-start | bytes 786440 | tf_op jit(solution)/shard_map/ppermute | solution.py:248

commit v3 on v2

--- a/solution.py
+++ b/solution.py
@@ -11,6 +11,7 @@
 E = 128
 PAIR = 2 * E
 FLAG = 8
+SQUARE = 4
 EPS = 1e-06
 VMEM_LIMIT = 8 * 1024 * 1024
 F32 = jnp.float32
@@ -32,8 +33,8 @@
 
 
 def place(pair, pairs):
-    y_bit = (lax.axis_index("ctx") // 2) % 2
-    slot = ((pair % 2) ^ y_bit) * (pairs // 2) + pair // 2
+    chip = (lax.axis_index("ctx") // 2) % SQUARE
+    slot = ((pair % SQUARE) ^ chip) * (pairs // SQUARE) + pair // SQUARE
     return pl.ds(pl.multiple_of(slot * E, E), E)
 
 
@@ -248,10 +249,26 @@
     return lax.ppermute(block, "ctx", [(i, i ^ distance) for i in range(count)])
 
 
+def combine(early, late):
+    return jnp.maximum(early[0], late[0]), late[1] + (1.0 - late[0]) * early[1]
+
+
+def crossed(bit, zero, one):
+    return jnp.where(bit, one, zero), jnp.where(bit, zero, one)
+
+
+def permuted(parts, low, high):
+    a, b = crossed(low, parts[0], parts[1])
+    c, d = crossed(low, parts[2], parts[3])
+    a, c = crossed(high, a, c)
+    b, d = crossed(high, b, d)
+    return [a, b, c, d]
+
+
 def scan(keep, send, bits, backward):
     count = lax.axis_size("ctx")
     rows = keep.shape[0]
-    half = rows // 2
+    part = rows // SQUARE
 
     def last(distance):
         row = FLAG * (distance.bit_length() - 1)
@@ -261,84 +278,67 @@
     def packed(block, flag, extra):
         return jnp.concatenate([block, jnp.broadcast_to(flag, (FLAG, E)), extra])
 
-    got = yield send, 1
-    flag, got_flag = send[rows : rows + 1], got[rows : rows + 1]
+    (got,) = yield [(send, 1)]
+    core_flag, late_flag = crossed(last(1), send[rows : rows + 1], got[rows : rows + 1])
     extra = send[rows + FLAG :] + got[rows + FLAG :]
-    second = last(1)
-    first_core = jnp.where(second, got[:rows], keep)
-    core_flag = jnp.where(second, got_flag, flag)
-    late_flag = jnp.where(second, flag, got_flag)
-
-    def both_cores(part):
-        mine, other = keep[part], got[part]
-        return jnp.where(second, mine, other) + (1.0 - late_flag) * jnp.where(second, other, mine)
-
-    flag = jnp.maximum(flag, got_flag)
-
-    block = packed(both_cores(slice(half, rows)), flag, extra)
-    keep = both_cores(slice(0, half))
-    got = yield block, 2
-    got_flag = got[half : half + 1]
-    extra = extra + got[half + FLAG :]
-    second = last(2)
-    first_chip = jnp.where(second, got[:half], keep)
-    chip_flag = jnp.where(second, got_flag, flag)
-    late, late_flag = jnp.where(second, keep, got[:half]), jnp.where(second, flag, got_flag)
-    total = late + (1.0 - late_flag) * first_chip
-    flag = jnp.maximum(flag, got_flag)
-
-    before, before_flag = jnp.zeros_like(total), jnp.zeros_like(flag)
-    distance = 4
+    first_core = jnp.where(last(1), got[:rows], keep)
+    flag = jnp.maximum(core_flag, late_flag)
+
+    def both_cores(number):
+        where = slice(number * part, (number + 1) * part)
+        early, late = crossed(last(1), keep[where], got[where])
+        return late + (1.0 - late_flag) * early
+
+    gots = yield [
+        (packed(both_cores(number), flag, extra), 2 * number) for number in range(1, SQUARE)
+    ]
+    extra = sum((got[part + FLAG :] for got in gots), extra)
+    flags = permuted([flag] + [got[part : part + 1] for got in gots], last(2), last(4))
+    sums = permuted([both_cores(0)] + [got[:part] for got in gots], last(2), last(4))
+    runs = [(flags[0], sums[0])]
+    for following in list(zip(flags, sums))[1:]:
+        runs.append(combine(runs[-1], following))
+    flag, total = runs.pop()
+
+    before = jnp.zeros_like(flag), jnp.zeros_like(total)
+    distance = 2 * SQUARE
     while distance < count:
-        got = yield packed(total, flag, extra), distance
-        got_total, got_flag = got[:half], got[half : half + 1]
-        extra = extra + got[half + FLAG :]
-        second = last(distance)
-        before = jnp.where(second, before + (1.0 - before_flag) * got_total, before)
-        before_flag = jnp.where(second, jnp.maximum(before_flag, got_flag), before_flag)
-        total = jnp.where(
-            second, total + (1.0 - flag) * got_total, got_total + (1.0 - got_flag) * total
-        )
-        flag = jnp.maximum(flag, got_flag)
+        (got,) = yield [(packed(total, flag, extra), distance)]
+        extra = extra + got[part + FLAG :]
+        got = got[part : part + 1], got[:part]
+        longer = combine(got, before)
+        before = [jnp.where(last(distance), new, old) for new, old in zip(longer, before)]
+        after, ahead = combine((flag, total), got), combine(got, (flag, total))
+        flag, total = (jnp.where(last(distance), b, a) for a, b in zip(after, ahead))
         distance *= 2
 
-    after = first_chip + (1.0 - chip_flag) * before
-    second = last(2)
-    mine, theirs = jnp.where(second, after, before), jnp.where(second, before, after)
-    got = yield theirs, 2
-    before = jnp.concatenate([mine, got])
+    results = [before[1]] + [combine(before, run)[1] for run in runs]
+    results = permuted(results, last(2), last(4))
+    gots = yield [(results[number], 2 * number) for number in range(1, SQUARE)]
+    before = jnp.concatenate([results[0], *gots])
     after = first_core + (1.0 - core_flag) * before
-    second = last(1)
-    mine, theirs = jnp.where(second, after, before), jnp.where(second, before, after)
-    got = yield theirs, 1
+    mine, theirs = crossed(last(1), before, after)
+    (got,) = yield [(theirs, 1)]
     return mine, got, extra
 
 
-def rounds(one, two, work):
-    chains, waiting, results, pending = [one], {}, {}, ()
-    number = 0
-    while chains:
-        if number == 1:
-            chains.append(two)
-        for chain in chains:
-            if chain not in waiting:
-                waiting[chain] = next(chain)
-        blocks, _ = lax.optimization_barrier(([waiting[c][0] for c in chains], pending))
-        pending = work[number](blocks[0]) if number in work else ()
-        for chain, block in zip(list(chains), blocks):
-            try:
-                waiting[chain] = chain.send(swap(block, waiting[chain][1]))
-            except StopIteration as end:
-                results[chain] = end.value
-                chains.remove(chain)
+def run(chain, work):
+    swaps = next(chain)
+    number, done = 0, ()
+    while True:
+        blocks, _ = lax.optimization_barrier(([block for block, _ in swaps], done))
+        done = work[number](blocks[0]) if number in work else ()
+        try:
+            swaps = chain.send([swap(b, distance) for b, (_, distance) in zip(blocks, swaps)])
+        except StopIteration as end:
+            return end.value
         number += 1
-    return results[one], results[two]
 
 
 def shards(queries, key_vectors, value_vectors, out_grad, norm_gain, doc_bounds):
     tokens, width = queries.shape
-    groups = range(2)
-    half = width // 2
+    groups = range(1)
+    half = width
     pairs = half // PAIR
     rows = pairs * E
     extra = rows + FLAG + 2 * pairs
@@ -380,10 +380,7 @@
         [pltpu.SMEM(doc_bounds.shape, jnp.int32), copies(pairs, 2), copies()],
         group=0,
     )(doc_bounds, key_vectors, value_vectors)
-    *second, other_key, other_value = call(
-        state_kernel, [ANY] * 2 + [VMEM] * 2, states + [narrow] * 2, [copies(pairs, 2)], group=1
-    )(key_vectors, value_vectors, tail, flag)
-    keys, values = (key, other_key), (value, other_value)
+    keys, values = (key,), (value,)
 
     def local_of(g, token):
         local[g] = call(
@@ -419,17 +416,18 @@
         )(*local[g][1:], local[g][0], *carried[g], use, flag)
         return (yield from scan(*state, bits, True))
 
-    count = levels + 2
-    later = rounds(
-        chain(0, first),
-        chain(1, second),
-        {
-            1: functools.partial(local_of, 0),
-            3: functools.partial(local_of, 1),
-            count + 1: functools.partial(spread_of, 0),
-            count + 3: functools.partial(spread_of, 1),
-        },
-    )
+    steps = levels + 1
+    longest = steps - 3
+    later = [
+        run(
+            chain(g, first),
+            {
+                longest: functools.partial(local_of, g),
+                steps + longest: functools.partial(spread_of, g),
+            },
+        )
+        for g in groups
+    ]
     grads = ()
     for g in groups:
         grads = call(
@@ -442,7 +440,7 @@
         )(keys[g], values[g], *spread[g][1:], *later[g][:2], tail, *grads)
     total = jnp.concatenate([later[g][2] for g in groups])
     gain_grad = total.reshape(width) / math.sqrt(tokens * lax.axis_size("ctx"))
-    return spread[1][0], *grads, gain_grad
+    return spread[0][0], *grads, gain_grad
 
 
 def solution(mesh):

time: 83.2 us -> 73.6 us (0.88)
  starting transfers between devices: 41.7 us -> 23.3 us
  waiting for transfers between devices: 16.4 us -> 29.8 us
  Pallas kernels: 21.3 us -> 17.6 us
    ppermute x24 -> x18, starting transfers between devices: 41.7 us -> 23.3 us  [swap(): return lax.ppermute(block, 'ctx', [(i, i ^ distance) for i in range(count)])]
    ppermute x24 -> x18, waiting for transfers between devices: 16.4 us -> 29.8 us  [swap(): return lax.ppermute(block, 'ctx', [(i, i ^ distance) for i in range(count)])]
    pallas_call x1 -> x0, Pallas kernels: 1.98 us -> none  [shards(): call(state_kernel, [ANY] * 2 + [VMEM] * 2, states + [narrow] * 2, [copies...]
    pallas_call x2 -> x1, Pallas kernels: 5.49 us -> 4.46 us  [local_of(): call(local_kernel, [ANY] * 3 + [VMEM] * 3 + [ANY], [single, narrow, narro...]
    pallas_call x1, Pallas kernels: 2 us -> 3.01 us  [shards(): call(first_state_kernel, [ANY] * 3, states + [narrow] * 2 + [(VMEM, shape...]
    pallas_call x2 -> x1, Pallas kernels: 6.32 us -> 5.49 us  [spread_of(): call(spread_kernel, [VMEM] * 9 + [ANY] * (1 + len(done)), [(ANY, shape(to...]
    pallas_call x2 -> x1, Pallas kernels: 2.66 us -> 1.92 us  [shards(): call(final_kernel, [VMEM] * 7 + [ANY] * len(grads), [(ANY, shape(tokens,...]
    pallas_call x2 -> x1, Pallas kernels: 2.82 us -> 2.74 us  [chain(): call(middle_kernel, [VMEM] * 8, [narrow, (VMEM, shape(rows, E)), (VMEM, s...]
  transfers between devices with their start and end apart: 24 -> 18, of which waited for: 14 -> 18; matrix products, arithmetic and copies ran while one was open for 1% -> 1% of each run, Pallas kernels for 20% -> 14%
where the time goes in v3:
time: 73.6 us; the launch traced here: 73.1 us
  waiting for transfers between devices  29.8 us (40%)
  starting transfers between devices  23.3 us (32%)
  Pallas kernels  17.6 us (24%)
  other arithmetic  1.55 us (2%)
  between operations  0.81 us (1%)
    ppermute x18, waiting for transfers between devices, swap(): return lax.ppermute(block, 'ctx', [(i, i ^ distance) for i in range(count)])  29.8 us
    ppermute x18, starting transfers between devices, swap(): return lax.ppermute(block, 'ctx', [(i, i ^ distance) for i in range(count)])  23.3 us
    pallas_call x1, Pallas kernels, spread_of(): call(spread_kernel, [VMEM] * 9 + [ANY] * (1 + len(done)), [(ANY, shape(to...  5.49 us
    pallas_call x1, Pallas kernels, local_of(): call(local_kernel, [ANY] * 3 + [VMEM] * 3 + [ANY], [single, narrow, narro...  4.46 us
    pallas_call x1, Pallas kernels, shards(): call(first_state_kernel, [ANY] * 3, states + [narrow] * 2 + [(VMEM, shape...  3.01 us
    pallas_call x1, Pallas kernels, chain(): call(middle_kernel, [VMEM] * 8, [narrow, (VMEM, shape(rows, E)), (VMEM, s...  2.74 us
    pallas_call x1, Pallas kernels, shards(): call(final_kernel, [VMEM] * 7 + [ANY] * len(grads), [(ANY, shape(tokens,...  1.92 us
  transfers between devices with their start and end apart: 18, of which 18 were waited for; matrix products, arithmetic and copies ran while one was open for 1% of the time, Pallas kernels for 14%

profile of v3, /device:TPU:1, one launch (start us, length us, event | category | flops | bytes accessed | tf_op | source)
XLA Modules:
  0.0 73.1 jit_solution(11304023403860362212)
XLA Ops:
  0.6 3.0 %shard_map.93 = (f32[1024,128]{1,0:T(8,128)S(1)}, f32[1032,128]{1,0:T(8,128)S(1)}, bf16[256,2048]{1,0:T(8,128)(2,1)S(1)}, bf16[256,2048]{1,0:T(8,128)(2,1)S(1)},...) custom-call(s32[2,2]{1,0:T(2,128)} %bounds_hbm.1, ...), custom_call_target="tpu_custom_call" | custom-call | tf_op jit(solution)/shard_map/pallas_call | solution.py:374
  3.8 1.8 %collective-permute-done = f32[1032,128]{1,0:T(8,128)S(1)} collective-permute-done((f32[1032,128]{1,0:T(8,128)S(1)}, f32[1032,128]{1,0:T(8,128)S(1)}, u32[]{:S(2)}, u32[]{:S(2)}) %collective-permute-start) | collective-permute-done | bytes 528416 | tf_op jit(solution)/shard_map/ppermute | solution.py:249
  5.8 2.4 %collective-permute-start.1 = (f32[264,128]{1,0:T(8,128)S(1)}, f32[264,128]{1,0:T(8,128)S(1)}, u32[]{:S(2)}, u32[]{:S(2)}) collective-permute-start(f32[264,128]{1,0:T(8,128)S(1)} %get-tuple-element.44), channel_id=1, source_target_pairs={{0,2},{1,3},{2,0},{3,1},{4,6},{5,7},{6,4},{7,5},{8,10},{9,11},{10,... | collective-permute-start | bytes 405512 | tf_op jit(solution)/shard_map/ppermute | solution.py:249
  8.2 1.3 %collective-permute-start.2 = (f32[264,128]{1,0:T(8,128)S(1)}, f32[264,128]{1,0:T(8,128)S(1)}, u32[]{:S(2)}, u32[]{:S(2)}) collective-permute-start(f32[264,128]{1,0:T(8,128)S(1)} %get-tuple-element.45), channel_id=1, source_target_pairs={{0,4},{1,5},{2,6},{3,7},{4,0},{5,1},{6,2},{7,3},{8,12},{9,13},{10,... | collective-permute-start | bytes 405512 | tf_op jit(solution)/shard_map/ppermute | solution.py:249
  9.5 2.4 %collective-permute-done.1 = f32[264,128]{1,0:T(8,128)S(1)} collective-permute-done((f32[264,128]{1,0:T(8,128)S(1)}, f32[264,128]{1,0:T(8,128)S(1)}, u32[]{:S(2)}, u32[]{:S(2)}) %collective-permute-start.1) | collective-permute-done | bytes 135200 | tf_op jit(solution)/shard_map/ppermute | solution.py:249
  11.9 0.8 %collective-permute-done.2 = f32[264,128]{1,0:T(8,128)S(1)} collective-permute-done((f32[264,128]{1,0:T(8,128)S(1)}, f32[264,128]{1,0:T(8,128)S(1)}, u32[]{:S(2)}, u32[]{:S(2)}) %collective-permute-start.2) | collective-permute-done | bytes 135200 | tf_op jit(solution)/shard_map/ppermute | solution.py:249
  12.7 2.9 %collective-permute-done.3 = f32[264,128]{1,0:T(8,128)S(1)} collective-permute-done((f32[264,128]{1,0:T(8,128)S(1)}, f32[264,128]{1,0:T(8,128)S(1)}, u32[]{:S(2)}, u32[]{:S(2)}) %collective-permute-start.3) | collective-permute-done | bytes 135200 | tf_op jit(solution)/shard_map/ppermute | solution.py:249
  15.7 2.7 %collective-permute-start.4 = (f32[264,128]{1,0:T(8,128)S(1)}, f32[264,128]{1,0:T(8,128)S(1)}, u32[]{:S(2)}, u32[]{:S(2)}) collective-permute-start(f32[264,128]{1,0:T(8,128)S(1)} %pad_maximum_fusion.12._), channel_id=1, source_target_pairs={{0,8},{1,9},{2,10},{3,11},{4,12},{5,13},{6,14},{7,15},{8,0},{9,1},... | collective-permute-start | bytes 405512 | tf_op jit(solution)/shard_map/ppermute | solution.py:249
  18.4 4.5 %shard_map.94 = (f32[256,2048]{1,0:T(8,128)S(1)}, bf16[256,2048]{1,0:T(8,128)(2,1)S(1)}, bf16[256,2048]{1,0:T(8,128)(2,1)S(1)}, f32[1,2048]{1,0:T(1,128)S(1)}) custom-call(bf16[256,2048]{1,0:T(8,128)(2,1)} %q_hbm.1, bf16[256,2048]{1,0:T(8,128)(2,1)} %g_hbm.1, f32[1,2048]{1,0:T(1,128)} %bitcast.57, bf16[256,2048]{1,0:T(8,128)(2,1)S(1)} %get-tuple-element.38.k_ref, ...), custom_call_target="tpu_custom_call" | custom-call | tf_op jit(solution)/shard_map/pallas_call | solution.py:386
  22.8 1.7 %collective-permute-done.4 = f32[264,128]{1,0:T(8,128)S(1)} collective-permute-done((f32[264,128]{1,0:T(8,128)S(1)}, f32[264,128]{1,0:T(8,128)S(1)}, u32[]{:S(2)}, u32[]{:S(2)}) %collective-permute-start.4) | collective-permute-done | bytes 135200 | tf_op jit(solution)/shard_map/ppermute | solution.py:249
  25.4 1.0 %collective-permute-start.6 = (f32[256,128]{1,0:T(8,128)S(1)}, f32[256,128]{1,0:T(8,128)S(1)}, u32[]{:S(2)}, u32[]{:S(2)}) collective-permute-start(f32[256,128]{1,0:T(8,128)S(1)} %get-tuple-element.52), channel_id=1, source_target_pairs={{0,4},{1,5},{2,6},{3,7},{4,0},{5,1},{6,2},{7,3},{8,12},{9,13},{10,... | collective-permute-start | bytes 393224 | tf_op jit(solution)/shard_map/ppermute | solution.py:249
  26.4 1.0 %collective-permute-start.7 = (f32[256,128]{1,0:T(8,128)S(1)}, f32[256,128]{1,0:T(8,128)S(1)}, u32[]{:S(2)}, u32[]{:S(2)}) collective-permute-start(f32[256,128]{1,0:T(8,128)S(1)} %get-tuple-element.53), channel_id=1, source_target_pairs={{0,6},{1,7},{2,4},{3,5},{4,2},{5,3},{6,0},{7,1},{8,14},{9,15},{10,... | collective-permute-start | bytes 393224 | tf_op jit(solution)/shard_map/ppermute | solution.py:249
  27.3 1.2 %collective-permute-done.5 = f32[256,128]{1,0:T(8,128)S(1)} collective-permute-done((f32[256,128]{1,0:T(8,128)S(1)}, f32[256,128]{1,0:T(8,128)S(1)}, u32[]{:S(2)}, u32[]{:S(2)}) %collective-permute-start.5) | collective-permute-done | bytes 131104 | tf_op jit(solution)/shard_map/ppermute | solution.py:249
  28.5 1.0 %collective-permute-done.6 = f32[256,128]{1,0:T(8,128)S(1)} collective-permute-done((f32[256,128]{1,0:T(8,128)S(1)}, f32[256,128]{1,0:T(8,128)S(1)}, u32[]{:S(2)}, u32[]{:S(2)}) %collective-permute-start.6) | collective-permute-done | bytes 131104 | tf_op jit(solution)/shard_map/ppermute | solution.py:249
  29.5 2.3 %collective-permute-done.7 = f32[256,128]{1,0:T(8,128)S(1)} collective-permute-done((f32[256,128]{1,0:T(8,128)S(1)}, f32[256,128]{1,0:T(8,128)S(1)}, u32[]{:S(2)}, u32[]{:S(2)}) %collective-permute-start.7) | collective-permute-done | bytes 131104 | tf_op jit(solution)/shard_map/ppermute | solution.py:249
  31.9 2.9 %collective-permute-start.8 = (f32[1024,128]{1,0:T(8,128)S(1)}, f32[1024,128]{1,0:T(8,128)S(1)}, u32[]{:S(2)}, u32[]{:S(2)}) collective-permute-start(f32[1024,128]{1,0:T(8,128)S(1)} %get-tuple-element.106), channel_id=1, source_target_pairs={{0,1},{1,0},{2,3},{3,2},{4,5},{5,4},{6,7},{7,6},{8,9},{9,8},{10,11... | collective-permute-start | bytes 1572872 | tf_op jit(solution)/shard_map/ppermute | solution.py:249
  34.8 1.5 %collective-permute-done.8.got_ref = f32[1024,128]{1,0:T(8,128)S(1)} collective-permute-done((f32[1024,128]{1,0:T(8,128)S(1)}, f32[1024,128]{1,0:T(8,128)S(1)}, u32[]{:S(2)}, u32[]{:S(2)}) %collective-permute-start.8) | collective-permute-done | bytes 524320 | tf_op jit(solution)/shard_map/ppermute | solution.py:249
  36.3 2.7 %shard_map.95 = (bf16[256,2048]{1,0:T(8,128)(2,1)S(1)}, f32[1024,128]{1,0:T(8,128)S(1)}, f32[1048,128]{1,0:T(8,128)S(1)}) custom-call(bf16[256,2048]{1,0:T(8,128)(2,1)S(1)} %get-tuple-element.47.q_ref, bf16[256,2048]{1,0:T(8,128)(2,1)S(1)} %get-tuple-element.48.g_ref, f32[1,2048]{1,0:T(1,128)S(1)} %get-tuple-element.49.gain_ref, ...), custom_call_target="tpu_custom_call" | custom-call | tf_op jit(solution)/shard_map/pallas_call | solution.py:412
  39.5 1.6 %collective-permute-done.9 = f32[1048,128]{1,0:T(8,128)S(1)} collective-permute-done((f32[1048,128]{1,0:T(8,128)S(1)}, f32[1048,128]{1,0:T(8,128)S(1)}, u32[]{:S(2)}, u32[]{:S(2)}) %collective-permute-start.9) | collective-permute-done | bytes 536608 | tf_op jit(solution)/shard_map/ppermute | solution.py:249
  42.0 0.9 %collective-permute-start.11 = (f32[280,128]{1,0:T(8,128)S(1)}, f32[280,128]{1,0:T(8,128)S(1)}, u32[]{:S(2)}, u32[]{:S(2)}) collective-permute-start(f32[280,128]{1,0:T(8,128)S(1)} %get-tuple-element.61), channel_id=1, source_target_pairs={{0,4},{1,5},{2,6},{3,7},{4,0},{5,1},{6,2},{7,3},{8,12},{9,13},{10,... | collective-permute-start | bytes 430088 | tf_op jit(solution)/shard_map/ppermute | solution.py:249
  42.9 1.0 %collective-permute-start.12 = (f32[280,128]{1,0:T(8,128)S(1)}, f32[280,128]{1,0:T(8,128)S(1)}, u32[]{:S(2)}, u32[]{:S(2)}) collective-permute-start(f32[280,128]{1,0:T(8,128)S(1)} %get-tuple-element.62), channel_id=1, source_target_pairs={{0,6},{1,7},{2,4},{3,5},{4,2},{5,3},{6,0},{7,1},{8,14},{9,15},{10,... | collective-permute-start | bytes 430088 | tf_op jit(solution)/shard_map/ppermute | solution.py:249
  43.9 2.3 %collective-permute-done.10 = f32[280,128]{1,0:T(8,128)S(1)} collective-permute-done((f32[280,128]{1,0:T(8,128)S(1)}, f32[280,128]{1,0:T(8,128)S(1)}, u32[]{:S(2)}, u32[]{:S(2)}) %collective-permute-start.10) | collective-permute-done | bytes 143392 | tf_op jit(solution)/shard_map/ppermute | solution.py:249
  46.7 3.5 %collective-permute-done.12 = f32[280,128]{1,0:T(8,128)S(1)} collective-permute-done((f32[280,128]{1,0:T(8,128)S(1)}, f32[280,128]{1,0:T(8,128)S(1)}, u32[]{:S(2)}, u32[]{:S(2)}) %collective-permute-start.12) | collective-permute-done | bytes 143392 | tf_op jit(solution)/shard_map/ppermute | solution.py:249
  50.3 2.6 %collective-permute-start.13 = (f32[280,128]{1,0:T(8,128)S(1)}, f32[280,128]{1,0:T(8,128)S(1)}, u32[]{:S(2)}, u32[]{:S(2)}) collective-permute-start(f32[280,128]{1,0:T(8,128)S(1)} %pad_maximum_fusion.11.rest_0_), channel_id=1, source_target_pairs={{0,8},{1,9},{2,10},{3,11},{4,12},{5,13},{6,14},{7,15},{8,0},{9,1},... | collective-permute-start | bytes 430088 | tf_op jit(solution)/shard_map/ppermute | solution.py:249
  52.9 5.5 %shard_map.96 = (bf16[256,2048]{1,0:T(8,128)(2,1)}, f32[256,2048]{1,0:T(8,128)S(1)}, f32[256,2048]{1,0:T(8,128)S(1)}) custom-call(bf16[256,2048]{1,0:T(8,128)(2,1)S(1)} %get-tuple-element.47.q_ref, bf16[256,2048]{1,0:T(8,128)(2,1)S(1)} %get-tuple-element.38.k_ref, bf16[256,2048]{1,0:T(8,128)(2,1)S(1)} %get-tuple-element.39.v_ref, ...), custom_call_target="tpu_custom_call" | custom-call | tf_op jit(solution)/shard_map/pallas_call | solution.py:397
  60.1 1.2 %collective-permute-start.15 = (f32[256,128]{1,0:T(8,128)S(1)}, f32[256,128]{1,0:T(8,128)S(1)}, u32[]{:S(2)}, u32[]{:S(2)}) collective-permute-start(f32[256,128]{1,0:T(8,128)S(1)} %get-tuple-element.67), channel_id=1, source_target_pairs={{0,4},{1,5},{2,6},{3,7},{4,0},{5,1},{6,2},{7,3},{8,12},{9,13},{10,... | collective-permute-start | bytes 393224 | tf_op jit(solution)/shard_map/ppermute | solution.py:249
  62.1 1.2 %collective-permute-done.14 = f32[256,128]{1,0:T(8,128)S(1)} collective-permute-done((f32[256,128]{1,0:T(8,128)S(1)}, f32[256,128]{1,0:T(8,128)S(1)}, u32[]{:S(2)}, u32[]{:S(2)}) %collective-permute-start.14) | collective-permute-done | bytes 131104 | tf_op jit(solution)/shard_map/ppermute | solution.py:249
  63.3 0.9 %collective-permute-done.15 = f32[256,128]{1,0:T(8,128)S(1)} collective-permute-done((f32[256,128]{1,0:T(8,128)S(1)}, f32[256,128]{1,0:T(8,128)S(1)}, u32[]{:S(2)}, u32[]{:S(2)}) %collective-permute-start.15) | collective-permute-done | bytes 131104 | tf_op jit(solution)/shard_map/ppermute | solution.py:249
  64.2 2.6 %collective-permute-done.16 = f32[256,128]{1,0:T(8,128)S(1)} collective-permute-done((f32[256,128]{1,0:T(8,128)S(1)}, f32[256,128]{1,0:T(8,128)S(1)}, u32[]{:S(2)}, u32[]{:S(2)}) %collective-permute-start.16) | collective-permute-done | bytes 131104 | tf_op jit(solution)/shard_map/ppermute | solution.py:249
  66.9 2.8 %collective-permute-start.17 = (f32[1024,128]{1,0:T(8,128)S(1)}, f32[1024,128]{1,0:T(8,128)S(1)}, u32[]{:S(2)}, u32[]{:S(2)}) collective-permute-start(f32[1024,128]{1,0:T(8,128)S(1)} %get-tuple-element.104), channel_id=1, source_target_pairs={{0,1},{1,0},{2,3},{3,2},{4,5},{5,4},{6,7},{7,6},{8,9},{9,8},{10,11... | collective-permute-start | bytes 1572872 | tf_op jit(solution)/shard_map/ppermute | solution.py:249
  70.3 0.9 %collective-permute-done.17.got_ref = f32[1024,128]{1,0:T(8,128)S(1)} collective-permute-done((f32[1024,128]{1,0:T(8,128)S(1)}, f32[1024,128]{1,0:T(8,128)S(1)}, u32[]{:S(2)}, u32[]{:S(2)}) %collective-permute-start.17) | collective-permute-done | bytes 524320 | tf_op jit(solution)/shard_map/ppermute | solution.py:249
  71.2 1.9 %shard_map.97 = (bf16[256,2048]{1,0:T(8,128)(2,1)}, bf16[256,2048]{1,0:T(8,128)(2,1)}) custom-call(bf16[256,2048]{1,0:T(8,128)(2,1)S(1)} %get-tuple-element.38.k_ref, bf16[256,2048]{1,0:T(8,128)(2,1)S(1)} %get-tuple-element.39.v_ref, f32[256,2048]{1,0:T(8,128)S(1)} %get-tuple-element.64.kp_ref, f32[256,2048]{1,0:T(8,128)S(1)} %get-tuple-element.65.vp_ref, ...), custom_call_target="tpu_custom_call" | custom-call | tf_op jit(solution)/shard_map/pallas_call | solution.py:433
  (39 shorter events, 6.4 us)
Async XLA Ops:
  3.7 2.0 %collective-permute-start = (f32[1032,128]{1,0:T(8,128)S(1)}, f32[1032,128]{1,0:T(8,128)S(1)}, u32[]{:S(2)}, u32[]{:S(2)}) collective-permute-start(f32[1032,128]{1,0:T(8,128)S(1)} %get-tuple-element.43), channel_id=1, source_target_pairs={{0,1},{1,0},{2,3},{3,2},{4,5},{5,4},{6,7},{7,6},{8,9},{9,8},{10,11... | collective-permute-start | bytes 1585160 | tf_op jit(solution)/shard_map/ppermute | solution.py:249
  5.8 6.1 %collective-permute-start.1 = (f32[264,128]{1,0:T(8,128)S(1)}, f32[264,128]{1,0:T(8,128)S(1)}, u32[]{:S(2)}, u32[]{:S(2)}) collective-permute-start(f32[264,128]{1,0:T(8,128)S(1)} %get-tuple-element.44), channel_id=1, source_target_pairs={{0,2},{1,3},{2,0},{3,1},{4,6},{5,7},{6,4},{7,5},{8,10},{9,11},{10,... | collective-permute-start | bytes 405512 | tf_op jit(solution)/shard_map/ppermute | solution.py:249
  8.2 4.5 %collective-permute-start.2 = (f32[264,128]{1,0:T(8,128)S(1)}, f32[264,128]{1,0:T(8,128)S(1)}, u32[]{:S(2)}, u32[]{:S(2)}) collective-permute-start(f32[264,128]{1,0:T(8,128)S(1)} %get-tuple-element.45), channel_id=1, source_target_pairs={{0,4},{1,5},{2,6},{3,7},{4,0},{5,1},{6,2},{7,3},{8,12},{9,13},{10,... | collective-permute-start | bytes 405512 | tf_op jit(solution)/shard_map/ppermute | solution.py:249
  9.5 6.0 %collective-permute-start.3 = (f32[264,128]{1,0:T(8,128)S(1)}, f32[264,128]{1,0:T(8,128)S(1)}, u32[]{:S(2)}, u32[]{:S(2)}) collective-permute-start(f32[264,128]{1,0:T(8,128)S(1)} %get-tuple-element.46), channel_id=1, source_target_pairs={{0,6},{1,7},{2,4},{3,5},{4,2},{5,3},{6,0},{7,1},{8,14},{9,15},{10,... | collective-permute-start | bytes 405512 | tf_op jit(solution)/shard_map/ppermute | solution.py:249
  15.7 8.8 %collective-permute-start.4 = (f32[264,128]{1,0:T(8,128)S(1)}, f32[264,128]{1,0:T(8,128)S(1)}, u32[]{:S(2)}, u32[]{:S(2)}) collective-permute-start(f32[264,128]{1,0:T(8,128)S(1)} %pad_maximum_fusion.12._), channel_id=1, source_target_pairs={{0,8},{1,9},{2,10},{3,11},{4,12},{5,13},{6,14},{7,15},{8,0},{9,1},... | collective-permute-start | bytes 405512 | tf_op jit(solution)/shard_map/ppermute | solution.py:249
  24.6 3.9 %collective-permute-start.5 = (f32[256,128]{1,0:T(8,128)S(1)}, f32[256,128]{1,0:T(8,128)S(1)}, u32[]{:S(2)}, u32[]{:S(2)}) collective-permute-start(f32[256,128]{1,0:T(8,128)S(1)} %get-tuple-element.51), channel_id=1, source_target_pairs={{0,2},{1,3},{2,0},{3,1},{4,6},{5,7},{6,4},{7,5},{8,10},{9,11},{10,... | collective-permute-start | bytes 393224 | tf_op jit(solution)/shard_map/ppermute | solution.py:249
  25.4 4.1 %collective-permute-start.6 = (f32[256,128]{1,0:T(8,128)S(1)}, f32[256,128]{1,0:T(8,128)S(1)}, u32[]{:S(2)}, u32[]{:S(2)}) collective-permute-start(f32[256,128]{1,0:T(8,128)S(1)} %get-tuple-element.52), channel_id=1, source_target_pairs={{0,4},{1,5},{2,6},{3,7},{4,0},{5,1},{6,2},{7,3},{8,12},{9,13},{10,... | collective-permute-start | bytes 393224 | tf_op jit(solution)/shard_map/ppermute | solution.py:249
  26.4 5.4 %collective-permute-start.7 = (f32[256,128]{1,0:T(8,128)S(1)}, f32[256,128]{1,0:T(8,128)S(1)}, u32[]{:S(2)}, u32[]{:S(2)}) collective-permute-start(f32[256,128]{1,0:T(8,128)S(1)} %get-tuple-element.53), channel_id=1, source_target_pairs={{0,6},{1,7},{2,4},{3,5},{4,2},{5,3},{6,0},{7,1},{8,14},{9,15},{10,... | collective-permute-start | bytes 393224 | tf_op jit(solution)/shard_map/ppermute | solution.py:249
  31.9 4.4 %collective-permute-start.8 = (f32[1024,128]{1,0:T(8,128)S(1)}, f32[1024,128]{1,0:T(8,128)S(1)}, u32[]{:S(2)}, u32[]{:S(2)}) collective-permute-start(f32[1024,128]{1,0:T(8,128)S(1)} %get-tuple-element.106), channel_id=1, source_target_pairs={{0,1},{1,0},{2,3},{3,2},{4,5},{5,4},{6,7},{7,6},{8,9},{9,8},{10,11... | collective-permute-start | bytes 1572872 | tf_op jit(solution)/shard_map/ppermute | solution.py:249
  39.1 2.0 %collective-permute-start.9 = (f32[1048,128]{1,0:T(8,128)S(1)}, f32[1048,128]{1,0:T(8,128)S(1)}, u32[]{:S(2)}, u32[]{:S(2)}) collective-permute-start(f32[1048,128]{1,0:T(8,128)S(1)} %get-tuple-element.59), channel_id=1, source_target_pairs={{0,1},{1,0},{2,3},{3,2},{4,5},{5,4},{6,7},{7,6},{8,9},{9,8},{10,11... | collective-permute-start | bytes 1609736 | tf_op jit(solution)/shard_map/ppermute | solution.py:249
  41.2 5.0 %collective-permute-start.10 = (f32[280,128]{1,0:T(8,128)S(1)}, f32[280,128]{1,0:T(8,128)S(1)}, u32[]{:S(2)}, u32[]{:S(2)}) collective-permute-start(f32[280,128]{1,0:T(8,128)S(1)} %get-tuple-element.60), channel_id=1, source_target_pairs={{0,2},{1,3},{2,0},{3,1},{4,6},{5,7},{6,4},{7,5},{8,10},{9,11},{10,... | collective-permute-start | bytes 430088 | tf_op jit(solution)/shard_map/ppermute | solution.py:249
  42.0 4.7 %collective-permute-start.11 = (f32[280,128]{1,0:T(8,128)S(1)}, f32[280,128]{1,0:T(8,128)S(1)}, u32[]{:S(2)}, u32[]{:S(2)}) collective-permute-start(f32[280,128]{1,0:T(8,128)S(1)} %get-tuple-element.61), channel_id=1, source_target_pairs={{0,4},{1,5},{2,6},{3,7},{4,0},{5,1},{6,2},{7,3},{8,12},{9,13},{10,... | collective-permute-start | bytes 430088 | tf_op jit(solution)/shard_map/ppermute | solution.py:249
  42.9 7.2 %collective-permute-start.12 = (f32[280,128]{1,0:T(8,128)S(1)}, f32[280,128]{1,0:T(8,128)S(1)}, u32[]{:S(2)}, u32[]{:S(2)}) collective-permute-start(f32[280,128]{1,0:T(8,128)S(1)} %get-tuple-element.62), channel_id=1, source_target_pairs={{0,6},{1,7},{2,4},{3,5},{4,2},{5,3},{6,0},{7,1},{8,14},{9,15},{10,... | collective-permute-start | bytes 430088 | tf_op jit(solution)/shard_map/ppermute | solution.py:249
  50.3 8.9 %collective-permute-start.13 = (f32[280,128]{1,0:T(8,128)S(1)}, f32[280,128]{1,0:T(8,128)S(1)}, u32[]{:S(2)}, u32[]{:S(2)}) collective-permute-start(f32[280,128]{1,0:T(8,128)S(1)} %pad_maximum_fusion.11.rest_0_), channel_id=1, source_target_pairs={{0,8},{1,9},{2,10},{3,11},{4,12},{5,13},{6,14},{7,15},{8,0},{9,1},... | collective-permute-start | bytes 430088 | tf_op jit(solution)/shard_map/ppermute | solution.py:249
  59.4 3.9 %collective-permute-start.14 = (f32[256,128]{1,0:T(8,128)S(1)}, f32[256,128]{1,0:T(8,128)S(1)}, u32[]{:S(2)}, u32[]{:S(2)}) collective-permute-start(f32[256,128]{1,0:T(8,128)S(1)} %get-tuple-element.66), channel_id=1, source_target_pairs={{0,2},{1,3},{2,0},{3,1},{4,6},{5,7},{6,4},{7,5},{8,10},{9,11},{10,... | collective-permute-start | bytes 393224 | tf_op jit(solution)/shard_map/ppermute | solution.py:249
  60.1 4.1 %collective-permute-start.15 = (f32[256,128]{1,0:T(8,128)S(1)}, f32[256,128]{1,0:T(8,128)S(1)}, u32[]{:S(2)}, u32[]{:S(2)}) collective-permute-start(f32[256,128]{1,0:T(8,128)S(1)} %get-tuple-element.67), channel_id=1, source_target_pairs={{0,4},{1,5},{2,6},{3,7},{4,0},{5,1},{6,2},{7,3},{8,12},{9,13},{10,... | collective-permute-start | bytes 393224 | tf_op jit(solution)/shard_map/ppermute | solution.py:249
  61.3 5.5 %collective-permute-start.16 = (f32[256,128]{1,0:T(8,128)S(1)}, f32[256,128]{1,0:T(8,128)S(1)}, u32[]{:S(2)}, u32[]{:S(2)}) collective-permute-start(f32[256,128]{1,0:T(8,128)S(1)} %get-tuple-element.68), channel_id=1, source_target_pairs={{0,6},{1,7},{2,4},{3,5},{4,2},{5,3},{6,0},{7,1},{8,14},{9,15},{10,... | collective-permute-start | bytes 393224 | tf_op jit(solution)/shard_map/ppermute | solution.py:249
  66.9 4.3 %collective-permute-start.17 = (f32[1024,128]{1,0:T(8,128)S(1)}, f32[1024,128]{1,0:T(8,128)S(1)}, u32[]{:S(2)}, u32[]{:S(2)}) collective-permute-start(f32[1024,128]{1,0:T(8,128)S(1)} %get-tuple-element.104), channel_id=1, source_target_pairs={{0,1},{1,0},{2,3},{3,2},{4,5},{5,4},{6,7},{7,6},{8,9},{9,8},{10,11... | collective-permute-start | bytes 1572872 | tf_op jit(solution)/shard_map/ppermute | solution.py:249

commit v4 on v3

v4 whole, which is shorter than its diff:
```python
import functools
import math

import jax
import jax.numpy as jnp
from jax import lax
from jax.experimental import pallas as pl
from jax.experimental.pallas import tpu as pltpu
from jax.sharding import PartitionSpec as P

E = 128
PAIR = 2 * E
FLAG = 8
SQUARE = 4
TOGETHER = 4
EPS = 1e-06
VMEM_LIMIT = 8 * 1024 * 1024
F32 = jnp.float32
BF16 = jnp.bfloat16
VMEM = pl.BlockSpec(memory_space=pltpu.VMEM)
ANY = pl.BlockSpec(memory_space=pl.ANY)


def dot(a, b, a_dim, b_dim):
    return lax.dot_general(a, b, (((a_dim,), (b_dim,)), ((), ())), preferred_element_type=F32)


def head(h):
    return slice(h * E, (h + 1) * E)


def place(pair, pairs):
    chip = (lax.axis_index("ctx") // 2) % SQUARE
    slot = ((pair % SQUARE) ^ chip) * (pairs // SQUARE) + pair // SQUARE
    return pl.ds(pl.multiple_of(slot * E, E), E)


def owner_column(pair, other):
    core = lax.axis_index("ctx") % 2
    return pl.ds(pl.multiple_of((2 * pair + (core + other) % 2) * E, E), E)


def fetch(other, sources, targets, sems):
    copies = []
    for pair in range(targets[0].shape[1] // E):
        copies.append([])
        for i, (source, target) in enumerate(zip(sources, targets)):
            copy = pltpu.make_async_copy(
                source.at[:, owner_column(pair, other)], target.at[:, head(pair)], sems.at[pair, i]
            )
            copy.start()
            copies[-1].append(copy)
    return copies


def put(source, target, pair, other, sem):
    copy = pltpu.make_async_copy(
        source.at[:, head(pair)], target.at[:, owner_column(pair, other)], sem
    )
    copy.start()
    return copy


def row_values(values, rows, dtype):
    position = lax.broadcasted_iota(jnp.int32, (rows, E), 0)
    result = jnp.full((rows, E), values[0])
    for block in range(1, len(values)):
        result = jnp.where(position >= block * (rows // len(values)), values[block], result)
    return result.astype(dtype)


def states_of(k_ref, v_ref, tail_ref, copies, out_ref):
    pairs = len(copies)
    for begin in range(0, pairs, TOGETHER):
        together = range(begin, min(begin + TOGETHER, pairs))
        for pair in together:
            for copy in copies[pair]:
                copy.wait()
        for pair in together:
            state = dot(k_ref[:, head(pair)] * tail_ref[...], v_ref[:, head(pair)], 0, 0)
            out_ref[place(pair, pairs), :] = state


def send_state_kernel(
    bounds_hbm, k_hbm, v_hbm,
    send_ref, k_ref, v_ref, start_ref, end_ref, use_ref, tail_ref, flag_ref, bits_ref,
    bounds, sems, bounds_sem,
):
    bounds_copy = pltpu.make_async_copy(bounds_hbm, bounds, bounds_sem)
    bounds_copy.start()
    copies = fetch(1, (k_hbm, v_hbm), (k_ref, v_ref), sems)
    rows, width = k_ref.shape
    count = bounds.shape[1]
    block_len = rows // count
    me = lax.axis_index("ctx")
    first = me * count
    for bit in range(bits_ref.shape[0] // FLAG):
        value = jnp.full((FLAG, E), (me // 2**bit) % 2)
        bits_ref[bit * FLAG : (bit + 1) * FLAG, :] = value.astype(F32)
    bounds_copy.wait()
    opens = [bounds[0, b] for b in range(count)]
    closes = [bounds[1, b] for b in range(count)]
    flag = jnp.full((FLAG, E), (opens[-1] >= first).astype(F32))
    flag_ref[...] = flag
    send_ref[width:, :] = flag
    use_ref[...] = row_values([(x < first).astype(F32) for x in opens], rows, BF16)
    tail_ref[...] = row_values([(x >= first + count - 1).astype(F32) for x in closes], rows, BF16)
    start_ref[...] = row_values([(x - first) * block_len for x in opens], rows, jnp.int32)
    end_ref[...] = row_values([(x - first + 1) * block_len for x in closes], rows, jnp.int32)
    states_of(k_ref, v_ref, tail_ref, copies, send_ref)


def keep_state_kernel(k_hbm, v_hbm, tail_ref, keep_ref, k_ref, v_ref, sems):
    copies = fetch(0, (k_hbm, v_hbm), (k_ref, v_ref), sems)
    states_of(k_ref, v_ref, tail_ref, copies, keep_ref)


def sight(bound_ref, turned):
    rows = bound_ref.shape[0]
    row = lax.broadcasted_iota(jnp.int32, (rows, E), 0)
    parts = []
    for c in range(rows // E):
        column = lax.broadcasted_iota(jnp.int32, (rows, E), 1) + c * E
        if turned:
            seen = (column >= row) & (column < bound_ref[...])
        else:
            seen = (column <= row) & (column >= bound_ref[...])
        parts.append(jnp.where(seen, 1.0, 0.0).astype(BF16))
    return jnp.concatenate(parts, axis=1)


def local_kernel(
    q_hbm, g_hbm, gain_hbm, k_ref, v_ref, start_ref, _,
    out_ref, q_ref, g_ref, gain_ref, q_sems, g_sems, gain_sem, *, other,
):
    copies = fetch(other, [q_hbm], [q_ref], q_sems)
    grad_copies = fetch(other, [g_hbm], [g_ref], g_sems)
    gain_copy = pltpu.make_async_copy(gain_hbm, gain_ref, gain_sem)
    gain_copy.start()
    mask = sight(start_ref, False)
    pairs = len(copies)
    for begin in range(0, pairs, TOGETHER):
        together = range(begin, min(begin + TOGETHER, pairs))
        for pair in together:
            copies[pair][0].wait()
        for pair in together:
            c = head(pair)
            scores = dot(q_ref[:, c], k_ref[:, c], 1, 1).astype(BF16) * mask
            out_ref[:, c] = dot(scores, v_ref[:, c], 1, 0)
    for (copy,) in grad_copies:
        copy.wait()
    gain_copy.wait()


def middle_kernel(q_ref, g_ref, gain_ref, local_ref, carry_ref, use_ref, *rest, other):
    if other:
        flag_ref, sums_ref, d_ref, state_ref = rest
    else:
        d_ref, state_ref, sums_ref = rest
    pairs = q_ref.shape[1] // E
    use = use_ref[...]
    core = lax.axis_index("ctx") % 2
    for pair in range(pairs):
        c = head(pair)
        used = q_ref[:, c] * use
        carry = carry_ref[place(pair, pairs), :].astype(BF16)
        attended = local_ref[:, c] + dot(used, carry, 1, 0)
        inverse = lax.rsqrt(jnp.mean(attended * attended, axis=1, keepdims=True) + EPS)
        normed = attended * inverse
        grad = g_ref[:, c].astype(F32)
        gained = grad * normed
        gain = gain_ref[:, owner_column(pair, other)]
        centre = jnp.mean(gained * gain, axis=1, keepdims=True)
        d_att = ((grad * gain - normed * centre) * inverse).astype(BF16)
        d_ref[:, c] = d_att
        state_ref[place(pair, pairs), :] = dot(used, d_att, 0, 0)
        total = jnp.sum(gained, axis=0, keepdims=True)
        if other:
            both = jnp.concatenate(
                crossed(core == 0, total, sums_ref[pair : pair + 1, :])
            )
            begin = pairs * E + FLAG + 2 * pair
            state_ref[begin : begin + 2, :] = both
        else:
            sums_ref[pair : pair + 1, :] = total
    if other:
        state_ref[pairs * E : pairs * E + FLAG, :] = flag_ref[...]


def spread_kernel(
    q_ref, k_ref, v_ref, d_ref, carry_ref, use_ref, start_ref, end_ref, *rest, other
):
    qg_hbm, kp_ref, vp_ref, qg_ref, sems = rest[-5:]
    pairs = q_ref.shape[1] // E
    use = use_ref[...]
    mask = sight(start_ref, False)
    turned_mask = sight(end_ref, True)
    copies = []
    for pair in range(pairs):
        c = head(pair)
        carry = carry_ref[place(pair, pairs), :].astype(BF16)
        query, key, value, d_att = q_ref[:, c], k_ref[:, c], v_ref[:, c], d_ref[:, c]
        dscores = dot(d_att, value, 1, 1).astype(BF16) * mask
        from_carry = dot(d_att * use, carry, 1, 1)
        qg_ref[:, c] = (dot(dscores, key, 1, 0) + from_carry).astype(BF16)
        turned = dot(value, d_att, 1, 1).astype(BF16) * turned_mask
        kp_ref[:, c] = dot(turned, query, 1, 0)
        turned = dot(key, query, 1, 1).astype(BF16) * turned_mask
        vp_ref[:, c] = dot(turned, d_att, 1, 0)
        copies.append(put(qg_ref, qg_hbm, pair, other, sems.at[pair]))
    for copy in copies:
        copy.wait()


def final_kernel(k_ref, v_ref, kp_ref, vp_ref, later_ref, tail_ref, *rest, other):
    kg_hbm, vg_hbm, kg_ref, vg_ref, sems = rest[-5:]
    pairs = k_ref.shape[1] // E
    tail = tail_ref[...]
    copies = []
    for pair in range(pairs):
        c = head(pair)
        later = later_ref[place(pair, pairs), :].astype(BF16)
        kg_ref[:, c] = (kp_ref[:, c] + dot(v_ref[:, c] * tail, later, 1, 1)).astype(BF16)
        vg_ref[:, c] = (vp_ref[:, c] + dot(k_ref[:, c] * tail, later, 1, 0)).astype(BF16)
        copies.append(put(kg_ref, kg_hbm, pair, other, sems.at[pair, 0]))
        copies.append(put(vg_ref, vg_hbm, pair, other, sems.at[pair, 1]))
    for copy in copies:
        copy.wait()


def swap(block, distance):
    count = lax.axis_size("ctx")
    return lax.ppermute(block, "ctx", [(i, i ^ distance) for i in range(count)])


def combine(early, late):
    return jnp.maximum(early[0], late[0]), late[1] + (1.0 - late[0]) * early[1]


def crossed(bit, zero, one):
    return jnp.where(bit, one, zero), jnp.where(bit, zero, one)


def permuted(parts, low, high):
    a, b = crossed(low, parts[0], parts[1])
    c, d = crossed(low, parts[2], parts[3])
    a, c = crossed(high, a, c)
    b, d = crossed(high, b, d)
    return [a, b, c, d]


def scan(keep, send, bits, backward, early):
    count = lax.axis_size("ctx")
    rows = keep.shape[0]
    part = rows // SQUARE

    def last(distance):
        row = FLAG * (distance.bit_length() - 1)
        bit = bits[row : row + 1]
        return bit < 0.5 if backward else bit > 0.5

    def packed(block, flag, extra):
        return jnp.concatenate([block, jnp.broadcast_to(flag, (FLAG, E)), extra])

    (got,) = yield [(send, 1)]
    core_flag, late_flag = crossed(last(1), send[rows : rows + 1], got[rows : rows + 1])
    extra = send[rows + FLAG :] + got[rows + FLAG :]
    first_core = jnp.where(last(1), got[:rows], keep)
    flag = jnp.maximum(core_flag, late_flag)

    def both_cores(number):
        where = slice(number * part, (number + 1) * part)
        early, late = crossed(last(1), keep[where], got[where])
        return late + (1.0 - late_flag) * early

    gots = yield [
        (packed(both_cores(number), flag, extra), 2 * number) for number in range(1, SQUARE)
    ]
    extra = sum((got[part + FLAG :] for got in gots), extra)
    flags = permuted([flag] + [got[part : part + 1] for got in gots], last(2), last(4))
    sums = permuted([both_cores(0)] + [got[:part] for got in gots], last(2), last(4))
    runs = [(flags[0], sums[0])]
    for following in list(zip(flags, sums))[1:]:
        runs.append(combine(runs[-1], following))
    flag, total = runs.pop()

    before = jnp.zeros_like(flag), jnp.zeros_like(total)
    distance = 2 * SQUARE
    while distance < count:
        (got,) = yield [(packed(total, flag, extra), distance)]
        extra = extra + got[part + FLAG :]
        got = got[part : part + 1], got[:part]
        longer = combine(got, before)
        before = [jnp.where(last(distance), new, old) for new, old in zip(longer, before)]
        after, ahead = combine((flag, total), got), combine(got, (flag, total))
        flag, total = (jnp.where(last(distance), b, a) for a, b in zip(after, ahead))
        distance *= 2

    results = [before[1]] + [combine(before, run)[1] for run in runs]
    results = permuted(results, last(2), last(4))
    gots = yield [(results[number], 2 * number) for number in range(1, SQUARE)]
    before = jnp.concatenate([results[0], *gots])
    after = first_core + (1.0 - core_flag) * before
    mine, theirs = crossed(last(1), before, after)
    early(mine)
    (got,) = yield [(theirs, 1)]
    return got, extra


def run(chain, work):
    swaps = next(chain)
    number, done = 0, ()
    while True:
        blocks, _ = lax.optimization_barrier(([block for block, _ in swaps], done))
        done = work[number](blocks[-1]) if number in work else ()
        try:
            swaps = chain.send([swap(b, distance) for b, (_, distance) in zip(blocks, swaps)])
        except StopIteration as end:
            return end.value
        number += 1


def shards(queries, key_vectors, value_vectors, out_grad, norm_gain, doc_bounds):
    tokens, width = queries.shape
    half = width // 2
    pairs = half // E
    rows = pairs * E
    levels = lax.axis_size("ctx").bit_length() - 1
    queries, key_vectors, value_vectors, out_grad, gains, doc_bounds = (
        pltpu.with_memory_space_constraint(x, pltpu.HBM)
        for x in (
            queries, key_vectors, value_vectors, out_grad, norm_gain.reshape(1, width), doc_bounds
        )
    )

    def held(count, columns, dtype=F32, spec=VMEM):
        return spec, jax.ShapeDtypeStruct((count, columns), dtype)

    def call(kernel, inputs, outputs, scratch=(), aliases={}, **sizes):
        return pl.pallas_call(
            functools.partial(kernel, **sizes),
            in_specs=inputs,
            out_specs=[spec for spec, _ in outputs],
            out_shape=[out for _, out in outputs],
            scratch_shapes=scratch,
            input_output_aliases=aliases,
            compiler_params=pltpu.CompilerParams(vmem_limit_bytes=VMEM_LIMIT),
        )

    def copies(*counts):
        return pltpu.SemaphoreType.DMA(counts)

    narrow, single = held(tokens, half, BF16), held(tokens, half)
    grad = held(tokens, width, BF16, ANY)
    row = held(tokens, E, BF16)
    staging = pltpu.VMEM((tokens, half), BF16)
    keys, values, local, carried, middle, spread = {}, {}, {}, {}, {}, {}
    send, keys[1], values[1], start, end, use, tail, flag, bits = call(
        send_state_kernel,
        [ANY] * 3,
        [held(rows + FLAG, E), narrow, narrow, held(tokens, E, jnp.int32),
         held(tokens, E, jnp.int32), row, row, held(FLAG, E), held(FLAG * levels, E)],
        [pltpu.SMEM(doc_bounds.shape, jnp.int32), copies(pairs, 2), copies()],
    )(doc_bounds, key_vectors, value_vectors)
    keep, keys[0], values[0] = call(
        keep_state_kernel,
        [ANY, ANY, VMEM],
        [held(rows, E), narrow, narrow],
        [copies(pairs, 2)],
    )(key_vectors, value_vectors, tail)

    def local_of(other, token):
        local[other] = call(
            local_kernel,
            [ANY] * 3 + [VMEM] * 3 + [ANY],
            [single, narrow, narrow, held(1, width)],
            [copies(pairs, 1), copies(pairs, 1), copies()],
            other=other,
        )(queries, out_grad, gains, keys[other], values[other], start, token)
        return local[other][0]

    def middle_of(other, carry):
        carried[other] = carry
        state = held(rows + FLAG + 2 * pairs, E) if other else held(rows, E)
        middle[other] = call(
            middle_kernel,
            [VMEM] * (8 if other else 6),
            [narrow, state] if other else [narrow, state, held(pairs, E)],
            other=other,
        )(
            *local[other][1:], local[other][0], carry, use,
            *([flag, middle[0][2]] if other else []),
        )

    def spread_of(other, token):
        done = spread[0][:1] if other else []
        spread[other] = call(
            spread_kernel,
            [VMEM] * 8 + [ANY] * (1 + len(done)),
            [grad, single, single],
            [staging, copies(pairs)],
            {9: 0} if done else {},
            other=other,
        )(
            local[other][1], keys[other], values[other], middle[other][0], carried[other],
            use, start, end, token, *done,
        )
        return spread[other][1]

    grads = []

    def final_of(other, later):
        grads[:] = call(
            final_kernel,
            [VMEM] * 6 + [ANY] * len(grads),
            [grad, grad],
            [staging, staging, copies(pairs, 2)],
            {6: 0, 7: 1} if grads else {},
            other=other,
        )(keys[other], values[other], *spread[other][1:], later, tail, *grads)

    def chain():
        got, _ = yield from scan(keep, send, bits, False, functools.partial(middle_of, 0))
        middle_of(1, got)
        states = middle[0][1], middle[1][1]
        got, total = yield from scan(*states, bits, True, functools.partial(final_of, 0))
        final_of(1, got)
        return total

    steps = levels + 1
    work = {}
    for begin, part in ((0, local_of), (steps, spread_of)):
        work[begin + 1] = functools.partial(part, 0)
        work[begin + steps - 3] = functools.partial(part, 1)
    total = run(chain(), work)
    gain_grad = total.reshape(width) / math.sqrt(tokens * lax.axis_size("ctx"))
    return spread[1][0], *grads, gain_grad


def solution(mesh):
    tokens = P(("parts", "ctx"), None)
    return jax.shard_map(
        shards,
        mesh=mesh,
        in_specs=(tokens, tokens, tokens, tokens, P(), P(None, ("parts", "ctx"))),
        out_specs=(tokens, tokens, tokens, P("parts")),
        check_vma=False,
    )
```

time: 73.6 us -> 71.9 us (0.977)
  waiting for transfers between devices: 29.8 us -> 25.8 us
  Pallas kernels: 17.6 us -> 20.1 us
    ppermute x18, waiting for transfers between devices: 29.8 us -> 25.8 us  [swap(): return lax.ppermute(block, 'ctx', [(i, i ^ distance) for i in range(count)])]
    pallas_call x4 -> x8, Pallas kernels: 13.2 us -> 15.2 us  [the longest x2 6.16 us: spread_of(): call(spread_kernel, [VMEM] * 8 + [ANY] * (1 + len(done)), [grad, single,...]
    pallas_call x1 -> x2, Pallas kernels: 4.46 us -> 4.87 us  [local_of(): call(local_kernel, [ANY] * 3 + [VMEM] * 3 + [ANY], [single, narrow, narro...]
  transfers between devices with their start and end apart: 18 -> 18, of which waited for: 18 -> 14; matrix products, arithmetic and copies ran while one was open for 1% -> 1% of each run, Pallas kernels for 14% -> 22%
where the time goes in v4:
time: 71.9 us; the launch traced here: 71.5 us
  waiting for transfers between devices  25.8 us (36%)
  starting transfers between devices  23.2 us (32%)
  Pallas kernels  20.1 us (28%)
  other arithmetic  1.59 us (2%)
  between operations  0.87 us (1%)
    ppermute x18, waiting for transfers between devices, swap(): return lax.ppermute(block, 'ctx', [(i, i ^ distance) for i in range(count)])  25.8 us
    ppermute x18, starting transfers between devices, swap(): return lax.ppermute(block, 'ctx', [(i, i ^ distance) for i in range(count)])  23.2 us
    pallas_call x2, Pallas kernels, spread_of(): call(spread_kernel, [VMEM] * 8 + [ANY] * (1 + len(done)), [grad, single,...  6.16 us
    pallas_call x2, Pallas kernels, local_of(): call(local_kernel, [ANY] * 3 + [VMEM] * 3 + [ANY], [single, narrow, narro...  4.87 us
    pallas_call x2, Pallas kernels, middle_of(): call(middle_kernel, [VMEM] * (8 if other else 6), [narrow, state] if othe...  2.78 us
    pallas_call x2, Pallas kernels, final_of(): call(final_kernel, [VMEM] * 6 + [ANY] * len(grads), [grad, grad], [stagin...  2.67 us
    pallas_call x1, Pallas kernels, shards(): call(send_state_kernel, [ANY] * 3, [held(rows + FLAG, E), narrow, narrow,...  1.82 us
    pallas_call x1, Pallas kernels, shards(): call(keep_state_kernel, [ANY, ANY, VMEM], [held(rows, E), narrow, narrow]...  1.78 us
  transfers between devices with their start and end apart: 18, of which 14 were waited for; matrix products, arithmetic and copies ran while one was open for 1% of the time, Pallas kernels for 22%

profile of v4, /device:TPU:1, one launch (start us, length us, event | category | flops | bytes accessed | tf_op | source)
XLA Modules:
  0.0 71.5 jit_solution(4163992879277904544)
XLA Ops:
  0.6 1.8 %shard_map.93 = (f32[1032,128]{1,0:T(8,128)S(1)}, bf16[256,1024]{1,0:T(8,128)(2,1)S(1)}, bf16[256,1024]{1,0:T(8,128)(2,1)S(1)}, s32[256,128]{1,0:T(8,128)S(1)}, ...) custom-call(s32[2,2]{1,0:T(2,128)} %bounds_hbm.1, ...), custom_call_target="tpu_custom_call" | custom-call | tf_op jit(solution)/shard_map/pallas_call | solution.py:358
  2.6 1.8 %shard_map.94 = (f32[1024,128]{1,0:T(8,128)S(1)}, bf16[256,1024]{1,0:T(8,128)(2,1)S(1)}, bf16[256,1024]{1,0:T(8,128)(2,1)S(1)}) custom-call(bf16[256,2048]{1,0:T(8,128)(2,1)} %k_hbm.3, bf16[256,2048]{1,0:T(8,128)(2,1)} %v_hbm.3, bf16[256,128]{1,0:T(8,128)(2,1)S(1)} %get-tuple-element.57.tail_ref), custom_call_target="tpu_custom_call" | custom-call | tf_op jit(solution)/shard_map/pallas_call | solution.py:365
  4.6 2.7 %collective-permute-start.1 = (f32[264,128]{1,0:T(8,128)S(1)}, f32[264,128]{1,0:T(8,128)S(1)}, u32[]{:S(2)}, u32[]{:S(2)}) collective-permute-start(f32[264,128]{1,0:T(8,128)S(1)} %get-tuple-element.60), channel_id=1, source_target_pairs={{0,2},{1,3},{2,0},{3,1},{4,6},{5,7},{6,4},{7,5},{8,10},{9,11},{10,... | collective-permute-start | bytes 405512 | tf_op jit(solution)/shard_map/ppermute | solution.py:233
  7.3 1.3 %collective-permute-start.2 = (f32[264,128]{1,0:T(8,128)S(1)}, f32[264,128]{1,0:T(8,128)S(1)}, u32[]{:S(2)}, u32[]{:S(2)}) collective-permute-start(f32[264,128]{1,0:T(8,128)S(1)} %get-tuple-element.61), channel_id=1, source_target_pairs={{0,4},{1,5},{2,6},{3,7},{4,0},{5,1},{6,2},{7,3},{8,12},{9,13},{10,... | collective-permute-start | bytes 405512 | tf_op jit(solution)/shard_map/ppermute | solution.py:233
  8.6 2.4 %shard_map.95 = (f32[256,1024]{1,0:T(8,128)S(1)}, bf16[256,1024]{1,0:T(8,128)(2,1)S(1)}, bf16[256,1024]{1,0:T(8,128)(2,1)S(1)}, f32[1,2048]{1,0:T(1,128)S(1)}) custom-call(bf16[256,2048]{1,0:T(8,128)(2,1)} %q_hbm.3, bf16[256,2048]{1,0:T(8,128)(2,1)} %g_hbm.3, f32[1,2048]{1,0:T(1,128)} %bitcast.57, bf16[256,1024]{1,0:T(8,128)(2,1)S(1)} %get-tuple-element.63.k_ref, ...), custom_call_target="tpu_custom_call" | custom-call | tf_op jit(solution)/shard_map/pallas_call | solution.py:373
  12.1 2.8 %collective-permute-done.3 = f32[264,128]{1,0:T(8,128)S(1)} collective-permute-done((f32[264,128]{1,0:T(8,128)S(1)}, f32[264,128]{1,0:T(8,128)S(1)}, u32[]{:S(2)}, u32[]{:S(2)}) %collective-permute-start.3) | collective-permute-done | bytes 135200 | tf_op jit(solution)/shard_map/ppermute | solution.py:233
  15.1 2.6 %collective-permute-start.4 = (f32[264,128]{1,0:T(8,128)S(1)}, f32[264,128]{1,0:T(8,128)S(1)}, u32[]{:S(2)}, u32[]{:S(2)}) collective-permute-start(f32[264,128]{1,0:T(8,128)S(1)} %pad_maximum_fusion.12._), channel_id=1, source_target_pairs={{0,8},{1,9},{2,10},{3,11},{4,12},{5,13},{6,14},{7,15},{8,0},{9,1},... | collective-permute-start | bytes 405512 | tf_op jit(solution)/shard_map/ppermute | solution.py:233
  17.7 2.4 %shard_map.96 = (f32[256,1024]{1,0:T(8,128)S(1)}, bf16[256,1024]{1,0:T(8,128)(2,1)S(1)}, bf16[256,1024]{1,0:T(8,128)(2,1)S(1)}, f32[1,2048]{1,0:T(1,128)S(1)}) custom-call(bf16[256,2048]{1,0:T(8,128)(2,1)} %q_hbm.3, bf16[256,2048]{1,0:T(8,128)(2,1)} %g_hbm.3, f32[1,2048]{1,0:T(1,128)} %bitcast.58, bf16[256,1024]{1,0:T(8,128)(2,1)S(1)} %get-tuple-element.53.k_ref, ...), custom_call_target="tpu_custom_call" | custom-call | tf_op jit(solution)/shard_map/pallas_call | solution.py:373
  20.1 3.6 %collective-permute-done.4 = f32[264,128]{1,0:T(8,128)S(1)} collective-permute-done((f32[264,128]{1,0:T(8,128)S(1)}, f32[264,128]{1,0:T(8,128)S(1)}, u32[]{:S(2)}, u32[]{:S(2)}) %collective-permute-start.4) | collective-permute-done | bytes 135200 | tf_op jit(solution)/shard_map/ppermute | solution.py:233
  23.9 1.0 %collective-permute-start.5 = (f32[256,128]{1,0:T(8,128)S(1)}, f32[256,128]{1,0:T(8,128)S(1)}, u32[]{:S(2)}, u32[]{:S(2)}) collective-permute-start(f32[256,128]{1,0:T(8,128)S(1)} %get-tuple-element.71), channel_id=1, source_target_pairs={{0,2},{1,3},{2,0},{3,1},{4,6},{5,7},{6,4},{7,5},{8,10},{9,11},{10,... | collective-permute-start | bytes 393224 | tf_op jit(solution)/shard_map/ppermute | solution.py:233
  24.9 1.4 %collective-permute-start.6 = (f32[256,128]{1,0:T(8,128)S(1)}, f32[256,128]{1,0:T(8,128)S(1)}, u32[]{:S(2)}, u32[]{:S(2)}) collective-permute-start(f32[256,128]{1,0:T(8,128)S(1)} %get-tuple-element.72), channel_id=1, source_target_pairs={{0,4},{1,5},{2,6},{3,7},{4,0},{5,1},{6,2},{7,3},{8,12},{9,13},{10,... | collective-permute-start | bytes 393224 | tf_op jit(solution)/shard_map/ppermute | solution.py:233
  26.6 1.2 %collective-permute-done.5 = f32[256,128]{1,0:T(8,128)S(1)} collective-permute-done((f32[256,128]{1,0:T(8,128)S(1)}, f32[256,128]{1,0:T(8,128)S(1)}, u32[]{:S(2)}, u32[]{:S(2)}) %collective-permute-start.5) | collective-permute-done | bytes 131104 | tf_op jit(solution)/shard_map/ppermute | solution.py:233
  27.8 1.2 %collective-permute-done.6 = f32[256,128]{1,0:T(8,128)S(1)} collective-permute-done((f32[256,128]{1,0:T(8,128)S(1)}, f32[256,128]{1,0:T(8,128)S(1)}, u32[]{:S(2)}, u32[]{:S(2)}) %collective-permute-start.6) | collective-permute-done | bytes 131104 | tf_op jit(solution)/shard_map/ppermute | solution.py:233
  29.0 3.3 %collective-permute-done.7 = f32[256,128]{1,0:T(8,128)S(1)} collective-permute-done((f32[256,128]{1,0:T(8,128)S(1)}, f32[256,128]{1,0:T(8,128)S(1)}, u32[]{:S(2)}, u32[]{:S(2)}) %collective-permute-start.7) | collective-permute-done | bytes 131104 | tf_op jit(solution)/shard_map/ppermute | solution.py:233
  32.4 2.3 %collective-permute-start.8 = (f32[1024,128]{1,0:T(8,128)S(1)}, f32[1024,128]{1,0:T(8,128)S(1)}, u32[]{:S(2)}, u32[]{:S(2)}) collective-permute-start(f32[1024,128]{1,0:T(8,128)S(1)} %get-tuple-element.137), channel_id=1, source_target_pairs={{0,1},{1,0},{2,3},{3,2},{4,5},{5,4},{6,7},{7,6},{8,9},{9,8},{10,11... | collective-permute-start | bytes 1572872 | tf_op jit(solution)/shard_map/ppermute | solution.py:233
  34.7 1.4 %shard_map.97 = (bf16[256,1024]{1,0:T(8,128)(2,1)S(1)}, f32[1024,128]{1,0:T(8,128)S(1)}, f32[8,128]{1,0:T(8,128)S(1)}) custom-call(bf16[256,1024]{1,0:T(8,128)(2,1)S(1)} %get-tuple-element.76.q_ref, bf16[256,1024]{1,0:T(8,128)(2,1)S(1)} %get-tuple-element.77.g_ref, f32[1,2048]{1,0:T(1,128)S(1)} %get-tuple-element.78.gain_ref, ...), custom_call_target="tpu_custom_call" | custom-call | tf_op jit(solution)/shard_map/pallas_call | solution.py:385
  36.2 1.4 %shard_map.98 = (bf16[256,1024]{1,0:T(8,128)(2,1)S(1)}, f32[1048,128]{1,0:T(8,128)S(1)}) custom-call(bf16[256,1024]{1,0:T(8,128)(2,1)S(1)} %get-tuple-element.67.q_ref, bf16[256,1024]{1,0:T(8,128)(2,1)S(1)} %get-tuple-element.68.g_ref, f32[1,2048]{1,0:T(1,128)S(1)} %get-tuple-element.69.gain_ref, f32[256,1024]{1,0:T(8,128)S(1)} %get-tuple-element.70.local_ref, ...), custom_call_target="tpu_custom_call" | custom-call | tf_op jit(solution)/shard_map/pallas_call | solution.py:385
  38.0 1.6 %collective-permute-done.9 = f32[1048,128]{1,0:T(8,128)S(1)} collective-permute-done((f32[1048,128]{1,0:T(8,128)S(1)}, f32[1048,128]{1,0:T(8,128)S(1)}, u32[]{:S(2)}, u32[]{:S(2)}) %collective-permute-start.9) | collective-permute-done | bytes 536608 | tf_op jit(solution)/shard_map/ppermute | solution.py:233
  40.1 1.3 %collective-permute-start.11 = (f32[280,128]{1,0:T(8,128)S(1)}, f32[280,128]{1,0:T(8,128)S(1)}, u32[]{:S(2)}, u32[]{:S(2)}) collective-permute-start(f32[280,128]{1,0:T(8,128)S(1)} %get-tuple-element.85), channel_id=1, source_target_pairs={{0,4},{1,5},{2,6},{3,7},{4,0},{5,1},{6,2},{7,3},{8,12},{9,13},{10,... | collective-permute-start | bytes 430088 | tf_op jit(solution)/shard_map/ppermute | solution.py:233
  41.5 1.0 %collective-permute-start.12 = (f32[280,128]{1,0:T(8,128)S(1)}, f32[280,128]{1,0:T(8,128)S(1)}, u32[]{:S(2)}, u32[]{:S(2)}) collective-permute-start(f32[280,128]{1,0:T(8,128)S(1)} %get-tuple-element.86.rest_0_), channel_id=1, source_target_pairs={{0,6},{1,7},{2,4},{3,5},{4,2},{5,3},{6,0},{7,1},{8,14},{9,15},{10,... | collective-permute-start | bytes 430088 | tf_op jit(solution)/shard_map/ppermute | solution.py:233
  42.4 3.1 %shard_map.99 = (bf16[256,2048]{1,0:T(8,128)(2,1)}, f32[256,1024]{1,0:T(8,128)S(1)}, f32[256,1024]{1,0:T(8,128)S(1)}) custom-call(bf16[256,1024]{1,0:T(8,128)(2,1)S(1)} %get-tuple-element.76.q_ref, bf16[256,1024]{1,0:T(8,128)(2,1)S(1)} %get-tuple-element.63.k_ref, bf16[256,1024]{1,0:T(8,128)(2,1)S(1)} %get-tuple-element.64.v_ref, ...), custom_call_target="tpu_custom_call" | custom-call | tf_op jit(solution)/shard_map/pallas_call | solution.py:397
  45.5 3.2 %collective-permute-done.12 = f32[280,128]{1,0:T(8,128)S(1)} collective-permute-done((f32[280,128]{1,0:T(8,128)S(1)}, f32[280,128]{1,0:T(8,128)S(1)}, u32[]{:S(2)}, u32[]{:S(2)}) %collective-permute-start.12) | collective-permute-done | bytes 143392 | tf_op jit(solution)/shard_map/ppermute | solution.py:233
  48.9 2.6 %collective-permute-start.13 = (f32[280,128]{1,0:T(8,128)S(1)}, f32[280,128]{1,0:T(8,128)S(1)}, u32[]{:S(2)}, u32[]{:S(2)}) collective-permute-start(f32[280,128]{1,0:T(8,128)S(1)} %pad_maximum_fusion.11.rest_0_), channel_id=1, source_target_pairs={{0,8},{1,9},{2,10},{3,11},{4,12},{5,13},{6,14},{7,15},{8,0},{9,1},... | collective-permute-start | bytes 430088 | tf_op jit(solution)/shard_map/ppermute | solution.py:233
  51.5 3.1 %shard_map.100 = (bf16[256,2048]{1,0:T(8,128)(2,1)}, f32[256,1024]{1,0:T(8,128)S(1)}, f32[256,1024]{1,0:T(8,128)S(1)}) custom-call(bf16[256,1024]{1,0:T(8,128)(2,1)S(1)} %get-tuple-element.67.q_ref, bf16[256,1024]{1,0:T(8,128)(2,1)S(1)} %get-tuple-element.53.k_ref, bf16[256,1024]{1,0:T(8,128)(2,1)S(1)} %get-tuple-element.54.v_ref, ...), custom_call_target="tpu_custom_call", output_to_operand_aliasing={{0}: (9, {})} | custom-call | tf_op jit(solution)/shard_map/pallas_call | solution.py:397
  54.6 3.3 %collective-permute-done.13 = f32[280,128]{1,0:T(8,128)S(1)} collective-permute-done((f32[280,128]{1,0:T(8,128)S(1)}, f32[280,128]{1,0:T(8,128)S(1)}, u32[]{:S(2)}, u32[]{:S(2)}) %collective-permute-start.13) | collective-permute-done | bytes 143392 | tf_op jit(solution)/shard_map/ppermute | solution.py:233
  58.5 1.3 %collective-permute-start.15 = (f32[256,128]{1,0:T(8,128)S(1)}, f32[256,128]{1,0:T(8,128)S(1)}, u32[]{:S(2)}, u32[]{:S(2)}) collective-permute-start(f32[256,128]{1,0:T(8,128)S(1)} %get-tuple-element.95), channel_id=1, source_target_pairs={{0,4},{1,5},{2,6},{3,7},{4,0},{5,1},{6,2},{7,3},{8,12},{9,13},{10,... | collective-permute-start | bytes 393224 | tf_op jit(solution)/shard_map/ppermute | solution.py:233
  59.8 1.0 %collective-permute-start.16 = (f32[256,128]{1,0:T(8,128)S(1)}, f32[256,128]{1,0:T(8,128)S(1)}, u32[]{:S(2)}, u32[]{:S(2)}) collective-permute-start(f32[256,128]{1,0:T(8,128)S(1)} %get-tuple-element.96), channel_id=1, source_target_pairs={{0,6},{1,7},{2,4},{3,5},{4,2},{5,3},{6,0},{7,1},{8,14},{9,15},{10,... | collective-permute-start | bytes 393224 | tf_op jit(solution)/shard_map/ppermute | solution.py:233
  60.8 1.2 %collective-permute-done.14 = f32[256,128]{1,0:T(8,128)S(1)} collective-permute-done((f32[256,128]{1,0:T(8,128)S(1)}, f32[256,128]{1,0:T(8,128)S(1)}, u32[]{:S(2)}, u32[]{:S(2)}) %collective-permute-start.14) | collective-permute-done | bytes 131104 | tf_op jit(solution)/shard_map/ppermute | solution.py:233
  62.3 2.9 %collective-permute-done.16 = f32[256,128]{1,0:T(8,128)S(1)} collective-permute-done((f32[256,128]{1,0:T(8,128)S(1)}, f32[256,128]{1,0:T(8,128)S(1)}, u32[]{:S(2)}, u32[]{:S(2)}) %collective-permute-start.16) | collective-permute-done | bytes 131104 | tf_op jit(solution)/shard_map/ppermute | solution.py:233
  65.3 2.9 %collective-permute-start.17 = (f32[1024,128]{1,0:T(8,128)S(1)}, f32[1024,128]{1,0:T(8,128)S(1)}, u32[]{:S(2)}, u32[]{:S(2)}) collective-permute-start(f32[1024,128]{1,0:T(8,128)S(1)} %get-tuple-element.135), channel_id=1, source_target_pairs={{0,1},{1,0},{2,3},{3,2},{4,5},{5,4},{6,7},{7,6},{8,9},{9,8},{10,11... | collective-permute-start | bytes 1572872 | tf_op jit(solution)/shard_map/ppermute | solution.py:233
  68.8 1.3 %shard_map.101 = (bf16[256,2048]{1,0:T(8,128)(2,1)}, bf16[256,2048]{1,0:T(8,128)(2,1)}) custom-call(bf16[256,1024]{1,0:T(8,128)(2,1)S(1)} %get-tuple-element.63.k_ref, bf16[256,1024]{1,0:T(8,128)(2,1)S(1)} %get-tuple-element.64.v_ref, f32[256,1024]{1,0:T(8,128)S(1)} %get-tuple-element.88.kp_ref, f32[256,1024]{1,0:T(8,128)S(1)} %get-tuple-element.97.vp_ref, ...), custom_call_target="tpu_custom_call" | custom-call | tf_op jit(solution)/shard_map/pallas_call | solution.py:413
  70.2 1.3 %shard_map.102 = (bf16[256,2048]{1,0:T(8,128)(2,1)}, bf16[256,2048]{1,0:T(8,128)(2,1)}) custom-call(bf16[256,1024]{1,0:T(8,128)(2,1)S(1)} %get-tuple-element.53.k_ref, bf16[256,1024]{1,0:T(8,128)(2,1)S(1)} %get-tuple-element.54.v_ref, f32[256,1024]{1,0:T(8,128)S(1)} %get-tuple-element.92.kp_ref, ...), custom_call_target="tpu_custom_call", output_to_operand_aliasing={{0}: (6, {}), {1}: (7, {})} | custom-call | tf_op jit(solution)/shard_map/pallas_call | solution.py:413
  (44 shorter events, 5.0 us)
Async XLA Ops:
  2.5 2.0 %collective-permute-start = (f32[1032,128]{1,0:T(8,128)S(1)}, f32[1032,128]{1,0:T(8,128)S(1)}, u32[]{:S(2)}, u32[]{:S(2)}) collective-permute-start(f32[1032,128]{1,0:T(8,128)S(1)} %get-tuple-element.59), channel_id=1, source_target_pairs={{0,1},{1,0},{2,3},{3,2},{4,5},{5,4},{6,7},{7,6},{8,9},{9,8},{10,11... | collective-permute-start | bytes 1585160 | tf_op jit(solution)/shard_map/ppermute | solution.py:233
  4.6 6.6 %collective-permute-start.1 = (f32[264,128]{1,0:T(8,128)S(1)}, f32[264,128]{1,0:T(8,128)S(1)}, u32[]{:S(2)}, u32[]{:S(2)}) collective-permute-start(f32[264,128]{1,0:T(8,128)S(1)} %get-tuple-element.60), channel_id=1, source_target_pairs={{0,2},{1,3},{2,0},{3,1},{4,6},{5,7},{6,4},{7,5},{8,10},{9,11},{10,... | collective-permute-start | bytes 405512 | tf_op jit(solution)/shard_map/ppermute | solution.py:233
  7.3 4.8 %collective-permute-start.2 = (f32[264,128]{1,0:T(8,128)S(1)}, f32[264,128]{1,0:T(8,128)S(1)}, u32[]{:S(2)}, u32[]{:S(2)}) collective-permute-start(f32[264,128]{1,0:T(8,128)S(1)} %get-tuple-element.61), channel_id=1, source_target_pairs={{0,4},{1,5},{2,6},{3,7},{4,0},{5,1},{6,2},{7,3},{8,12},{9,13},{10,... | collective-permute-start | bytes 405512 | tf_op jit(solution)/shard_map/ppermute | solution.py:233
  8.6 6.3 %collective-permute-start.3 = (f32[264,128]{1,0:T(8,128)S(1)}, f32[264,128]{1,0:T(8,128)S(1)}, u32[]{:S(2)}, u32[]{:S(2)}) collective-permute-start(f32[264,128]{1,0:T(8,128)S(1)} %get-tuple-element.62._), channel_id=1, source_target_pairs={{0,6},{1,7},{2,4},{3,5},{4,2},{5,3},{6,0},{7,1},{8,14},{9,15},{10,... | collective-permute-start | bytes 405512 | tf_op jit(solution)/shard_map/ppermute | solution.py:233
  15.1 8.6 %collective-permute-start.4 = (f32[264,128]{1,0:T(8,128)S(1)}, f32[264,128]{1,0:T(8,128)S(1)}, u32[]{:S(2)}, u32[]{:S(2)}) collective-permute-start(f32[264,128]{1,0:T(8,128)S(1)} %pad_maximum_fusion.12._), channel_id=1, source_target_pairs={{0,8},{1,9},{2,10},{3,11},{4,12},{5,13},{6,14},{7,15},{8,0},{9,1},... | collective-permute-start | bytes 405512 | tf_op jit(solution)/shard_map/ppermute | solution.py:233
  23.9 3.9 %collective-permute-start.5 = (f32[256,128]{1,0:T(8,128)S(1)}, f32[256,128]{1,0:T(8,128)S(1)}, u32[]{:S(2)}, u32[]{:S(2)}) collective-permute-start(f32[256,128]{1,0:T(8,128)S(1)} %get-tuple-element.71), channel_id=1, source_target_pairs={{0,2},{1,3},{2,0},{3,1},{4,6},{5,7},{6,4},{7,5},{8,10},{9,11},{10,... | collective-permute-start | bytes 393224 | tf_op jit(solution)/shard_map/ppermute | solution.py:233
  24.9 4.1 %collective-permute-start.6 = (f32[256,128]{1,0:T(8,128)S(1)}, f32[256,128]{1,0:T(8,128)S(1)}, u32[]{:S(2)}, u32[]{:S(2)}) collective-permute-start(f32[256,128]{1,0:T(8,128)S(1)} %get-tuple-element.72), channel_id=1, source_target_pairs={{0,4},{1,5},{2,6},{3,7},{4,0},{5,1},{6,2},{7,3},{8,12},{9,13},{10,... | collective-permute-start | bytes 393224 | tf_op jit(solution)/shard_map/ppermute | solution.py:233
  26.2 6.0 %collective-permute-start.7 = (f32[256,128]{1,0:T(8,128)S(1)}, f32[256,128]{1,0:T(8,128)S(1)}, u32[]{:S(2)}, u32[]{:S(2)}) collective-permute-start(f32[256,128]{1,0:T(8,128)S(1)} %get-tuple-element.73), channel_id=1, source_target_pairs={{0,6},{1,7},{2,4},{3,5},{4,2},{5,3},{6,0},{7,1},{8,14},{9,15},{10,... | collective-permute-start | bytes 393224 | tf_op jit(solution)/shard_map/ppermute | solution.py:233
  32.4 3.8 %collective-permute-start.8 = (f32[1024,128]{1,0:T(8,128)S(1)}, f32[1024,128]{1,0:T(8,128)S(1)}, u32[]{:S(2)}, u32[]{:S(2)}) collective-permute-start(f32[1024,128]{1,0:T(8,128)S(1)} %get-tuple-element.137), channel_id=1, source_target_pairs={{0,1},{1,0},{2,3},{3,2},{4,5},{5,4},{6,7},{7,6},{8,9},{9,8},{10,11... | collective-permute-start | bytes 1572872 | tf_op jit(solution)/shard_map/ppermute | solution.py:233
  37.6 2.0 %collective-permute-start.9 = (f32[1048,128]{1,0:T(8,128)S(1)}, f32[1048,128]{1,0:T(8,128)S(1)}, u32[]{:S(2)}, u32[]{:S(2)}) collective-permute-start(f32[1048,128]{1,0:T(8,128)S(1)} %get-tuple-element.83), channel_id=1, source_target_pairs={{0,1},{1,0},{2,3},{3,2},{4,5},{5,4},{6,7},{7,6},{8,9},{9,8},{10,11... | collective-permute-start | bytes 1609736 | tf_op jit(solution)/shard_map/ppermute | solution.py:233
  39.7 5.8 %collective-permute-start.10 = (f32[280,128]{1,0:T(8,128)S(1)}, f32[280,128]{1,0:T(8,128)S(1)}, u32[]{:S(2)}, u32[]{:S(2)}) collective-permute-start(f32[280,128]{1,0:T(8,128)S(1)} %get-tuple-element.84), channel_id=1, source_target_pairs={{0,2},{1,3},{2,0},{3,1},{4,6},{5,7},{6,4},{7,5},{8,10},{9,11},{10,... | collective-permute-start | bytes 430088 | tf_op jit(solution)/shard_map/ppermute | solution.py:233
  40.1 5.4 %collective-permute-start.11 = (f32[280,128]{1,0:T(8,128)S(1)}, f32[280,128]{1,0:T(8,128)S(1)}, u32[]{:S(2)}, u32[]{:S(2)}) collective-permute-start(f32[280,128]{1,0:T(8,128)S(1)} %get-tuple-element.85), channel_id=1, source_target_pairs={{0,4},{1,5},{2,6},{3,7},{4,0},{5,1},{6,2},{7,3},{8,12},{9,13},{10,... | collective-permute-start | bytes 430088 | tf_op jit(solution)/shard_map/ppermute | solution.py:233
  41.5 7.2 %collective-permute-start.12 = (f32[280,128]{1,0:T(8,128)S(1)}, f32[280,128]{1,0:T(8,128)S(1)}, u32[]{:S(2)}, u32[]{:S(2)}) collective-permute-start(f32[280,128]{1,0:T(8,128)S(1)} %get-tuple-element.86.rest_0_), channel_id=1, source_target_pairs={{0,6},{1,7},{2,4},{3,5},{4,2},{5,3},{6,0},{7,1},{8,14},{9,15},{10,... | collective-permute-start | bytes 430088 | tf_op jit(solution)/shard_map/ppermute | solution.py:233
  48.9 9.1 %collective-permute-start.13 = (f32[280,128]{1,0:T(8,128)S(1)}, f32[280,128]{1,0:T(8,128)S(1)}, u32[]{:S(2)}, u32[]{:S(2)}) collective-permute-start(f32[280,128]{1,0:T(8,128)S(1)} %pad_maximum_fusion.11.rest_0_), channel_id=1, source_target_pairs={{0,8},{1,9},{2,10},{3,11},{4,12},{5,13},{6,14},{7,15},{8,0},{9,1},... | collective-permute-start | bytes 430088 | tf_op jit(solution)/shard_map/ppermute | solution.py:233
  58.1 3.9 %collective-permute-start.14 = (f32[256,128]{1,0:T(8,128)S(1)}, f32[256,128]{1,0:T(8,128)S(1)}, u32[]{:S(2)}, u32[]{:S(2)}) collective-permute-start(f32[256,128]{1,0:T(8,128)S(1)} %get-tuple-element.94), channel_id=1, source_target_pairs={{0,2},{1,3},{2,0},{3,1},{4,6},{5,7},{6,4},{7,5},{8,10},{9,11},{10,... | collective-permute-start | bytes 393224 | tf_op jit(solution)/shard_map/ppermute | solution.py:233
  58.5 3.8 %collective-permute-start.15 = (f32[256,128]{1,0:T(8,128)S(1)}, f32[256,128]{1,0:T(8,128)S(1)}, u32[]{:S(2)}, u32[]{:S(2)}) collective-permute-start(f32[256,128]{1,0:T(8,128)S(1)} %get-tuple-element.95), channel_id=1, source_target_pairs={{0,4},{1,5},{2,6},{3,7},{4,0},{5,1},{6,2},{7,3},{8,12},{9,13},{10,... | collective-permute-start | bytes 393224 | tf_op jit(solution)/shard_map/ppermute | solution.py:233
  59.8 5.4 %collective-permute-start.16 = (f32[256,128]{1,0:T(8,128)S(1)}, f32[256,128]{1,0:T(8,128)S(1)}, u32[]{:S(2)}, u32[]{:S(2)}) collective-permute-start(f32[256,128]{1,0:T(8,128)S(1)} %get-tuple-element.96), channel_id=1, source_target_pairs={{0,6},{1,7},{2,4},{3,5},{4,2},{5,3},{6,0},{7,1},{8,14},{9,15},{10,... | collective-permute-start | bytes 393224 | tf_op jit(solution)/shard_map/ppermute | solution.py:233
  65.3 4.9 %collective-permute-start.17 = (f32[1024,128]{1,0:T(8,128)S(1)}, f32[1024,128]{1,0:T(8,128)S(1)}, u32[]{:S(2)}, u32[]{:S(2)}) collective-permute-start(f32[1024,128]{1,0:T(8,128)S(1)} %get-tuple-element.135), channel_id=1, source_target_pairs={{0,1},{1,0},{2,3},{3,2},{4,5},{5,4},{6,7},{7,6},{8,9},{9,8},{10,11... | collective-permute-start | bytes 1572872 | tf_op jit(solution)/shard_map/ppermute | solution.py:233

commit v5 on v4

--- a/solution.py
+++ b/solution.py
@@ -12,7 +12,7 @@
 PAIR = 2 * E
 FLAG = 8
 SQUARE = 4
-TOGETHER = 4
+TOGETHER = 8
 EPS = 1e-06
 VMEM_LIMIT = 8 * 1024 * 1024
 F32 = jnp.float32
@@ -165,13 +165,13 @@
         used = q_ref[:, c] * use
         carry = carry_ref[place(pair, pairs), :].astype(BF16)
         attended = local_ref[:, c] + dot(used, carry, 1, 0)
-        inverse = lax.rsqrt(jnp.mean(attended * attended, axis=1, keepdims=True) + EPS)
-        normed = attended * inverse
         grad = g_ref[:, c].astype(F32)
-        gained = grad * normed
-        gain = gain_ref[:, owner_column(pair, other)]
-        centre = jnp.mean(gained * gain, axis=1, keepdims=True)
-        d_att = ((grad * gain - normed * centre) * inverse).astype(BF16)
+        d_norm = grad * gain_ref[:, owner_column(pair, other)]
+        square = jnp.mean(attended * attended, axis=1, keepdims=True)
+        centre = jnp.mean(d_norm * attended, axis=1, keepdims=True)
+        inverse = lax.rsqrt(square + EPS)
+        gained = grad * (attended * inverse)
+        d_att = ((d_norm - attended * (centre * inverse * inverse)) * inverse).astype(BF16)
         d_ref[:, c] = d_att
         state_ref[place(pair, pairs), :] = dot(used, d_att, 0, 0)
         total = jnp.sum(gained, axis=0, keepdims=True)

time: 71.9 us -> 71.7 us (level)
  transfers between devices with their start and end apart: 18 -> 18, of which waited for: 14 -> 15; matrix products, arithmetic and copies ran while one was open for 1% -> 1% of each run, Pallas kernels for 22% -> 21%
where the time goes in v5:
time: 71.7 us; the launch traced here: 71.3 us
  waiting for transfers between devices  26.1 us (36%)
  starting transfers between devices  23.2 us (32%)
  Pallas kernels  19.5 us (27%)
  other arithmetic  1.59 us (2%)
  between operations  0.87 us (1%)
    ppermute x18, waiting for transfers between devices, swap(): return lax.ppermute(block, 'ctx', [(i, i ^ distance) for i in range(count)])  26.1 us
    ppermute x18, starting transfers between devices, swap(): return lax.ppermute(block, 'ctx', [(i, i ^ distance) for i in range(count)])  23.2 us
    pallas_call x2, Pallas kernels, spread_of(): call(spread_kernel, [VMEM] * 8 + [ANY] * (1 + len(done)), [grad, single,...  6.16 us
    pallas_call x2, Pallas kernels, local_of(): call(local_kernel, [ANY] * 3 + [VMEM] * 3 + [ANY], [single, narrow, narro...  4.71 us
    pallas_call x2, Pallas kernels, final_of(): call(final_kernel, [VMEM] * 6 + [ANY] * len(grads), [grad, grad], [stagin...  2.67 us
    pallas_call x2, Pallas kernels, middle_of(): call(middle_kernel, [VMEM] * (8 if other else 6), [narrow, state] if othe...  2.42 us
    pallas_call x1, Pallas kernels, shards(): call(send_state_kernel, [ANY] * 3, [held(rows + FLAG, E), narrow, narrow,...  1.79 us
    pallas_call x1, Pallas kernels, shards(): call(keep_state_kernel, [ANY, ANY, VMEM], [held(rows, E), narrow, narrow]...  1.75 us
  transfers between devices with their start and end apart: 18, of which 15 were waited for; matrix products, arithmetic and copies ran while one was open for 1% of the time, Pallas kernels for 21%

profile of v5, /device:TPU:1, one launch (start us, length us, event | category | flops | bytes accessed | tf_op | source)
XLA Modules:
  0.0 71.3 jit_solution(12284582196354989651)
XLA Ops:
  0.6 1.8 %shard_map.93 = (f32[1032,128]{1,0:T(8,128)S(1)}, bf16[256,1024]{1,0:T(8,128)(2,1)S(1)}, bf16[256,1024]{1,0:T(8,128)(2,1)S(1)}, s32[256,128]{1,0:T(8,128)S(1)}, ...) custom-call(s32[2,2]{1,0:T(2,128)} %bounds_hbm.1, ...), custom_call_target="tpu_custom_call" | custom-call | tf_op jit(solution)/shard_map/pallas_call | solution.py:358
  2.6 1.8 %shard_map.94 = (f32[1024,128]{1,0:T(8,128)S(1)}, bf16[256,1024]{1,0:T(8,128)(2,1)S(1)}, bf16[256,1024]{1,0:T(8,128)(2,1)S(1)}) custom-call(bf16[256,2048]{1,0:T(8,128)(2,1)} %k_hbm.3, bf16[256,2048]{1,0:T(8,128)(2,1)} %v_hbm.3, bf16[256,128]{1,0:T(8,128)(2,1)S(1)} %get-tuple-element.57.tail_ref), custom_call_target="tpu_custom_call" | custom-call | tf_op jit(solution)/shard_map/pallas_call | solution.py:365
  4.5 2.7 %collective-permute-start.1 = (f32[264,128]{1,0:T(8,128)S(1)}, f32[264,128]{1,0:T(8,128)S(1)}, u32[]{:S(2)}, u32[]{:S(2)}) collective-permute-start(f32[264,128]{1,0:T(8,128)S(1)} %get-tuple-element.60), channel_id=1, source_target_pairs={{0,2},{1,3},{2,0},{3,1},{4,6},{5,7},{6,4},{7,5},{8,10},{9,11},{10,... | collective-permute-start | bytes 405512 | tf_op jit(solution)/shard_map/ppermute | solution.py:233
  7.3 1.3 %collective-permute-start.2 = (f32[264,128]{1,0:T(8,128)S(1)}, f32[264,128]{1,0:T(8,128)S(1)}, u32[]{:S(2)}, u32[]{:S(2)}) collective-permute-start(f32[264,128]{1,0:T(8,128)S(1)} %get-tuple-element.61), channel_id=1, source_target_pairs={{0,4},{1,5},{2,6},{3,7},{4,0},{5,1},{6,2},{7,3},{8,12},{9,13},{10,... | collective-permute-start | bytes 405512 | tf_op jit(solution)/shard_map/ppermute | solution.py:233
  8.6 2.4 %shard_map.95 = (f32[256,1024]{1,0:T(8,128)S(1)}, bf16[256,1024]{1,0:T(8,128)(2,1)S(1)}, bf16[256,1024]{1,0:T(8,128)(2,1)S(1)}, f32[1,2048]{1,0:T(1,128)S(1)}) custom-call(bf16[256,2048]{1,0:T(8,128)(2,1)} %q_hbm.3, bf16[256,2048]{1,0:T(8,128)(2,1)} %g_hbm.3, f32[1,2048]{1,0:T(1,128)} %bitcast.57, bf16[256,1024]{1,0:T(8,128)(2,1)S(1)} %get-tuple-element.63.k_ref, ...), custom_call_target="tpu_custom_call" | custom-call | tf_op jit(solution)/shard_map/pallas_call | solution.py:373
  11.1 1.0 %collective-permute-done.2 = f32[264,128]{1,0:T(8,128)S(1)} collective-permute-done((f32[264,128]{1,0:T(8,128)S(1)}, f32[264,128]{1,0:T(8,128)S(1)}, u32[]{:S(2)}, u32[]{:S(2)}) %collective-permute-start.2) | collective-permute-done | bytes 135200 | tf_op jit(solution)/shard_map/ppermute | solution.py:233
  12.1 2.8 %collective-permute-done.3 = f32[264,128]{1,0:T(8,128)S(1)} collective-permute-done((f32[264,128]{1,0:T(8,128)S(1)}, f32[264,128]{1,0:T(8,128)S(1)}, u32[]{:S(2)}, u32[]{:S(2)}) %collective-permute-start.3) | collective-permute-done | bytes 135200 | tf_op jit(solution)/shard_map/ppermute | solution.py:233
  15.0 2.6 %collective-permute-start.4 = (f32[264,128]{1,0:T(8,128)S(1)}, f32[264,128]{1,0:T(8,128)S(1)}, u32[]{:S(2)}, u32[]{:S(2)}) collective-permute-start(f32[264,128]{1,0:T(8,128)S(1)} %pad_maximum_fusion.12._), channel_id=1, source_target_pairs={{0,8},{1,9},{2,10},{3,11},{4,12},{5,13},{6,14},{7,15},{8,0},{9,1},... | collective-permute-start | bytes 405512 | tf_op jit(solution)/shard_map/ppermute | solution.py:233
  17.7 2.4 %shard_map.96 = (f32[256,1024]{1,0:T(8,128)S(1)}, bf16[256,1024]{1,0:T(8,128)(2,1)S(1)}, bf16[256,1024]{1,0:T(8,128)(2,1)S(1)}, f32[1,2048]{1,0:T(1,128)S(1)}) custom-call(bf16[256,2048]{1,0:T(8,128)(2,1)} %q_hbm.3, bf16[256,2048]{1,0:T(8,128)(2,1)} %g_hbm.3, f32[1,2048]{1,0:T(1,128)} %bitcast.58, bf16[256,1024]{1,0:T(8,128)(2,1)S(1)} %get-tuple-element.53.k_ref, ...), custom_call_target="tpu_custom_call" | custom-call | tf_op jit(solution)/shard_map/pallas_call | solution.py:373
  20.0 3.7 %collective-permute-done.4 = f32[264,128]{1,0:T(8,128)S(1)} collective-permute-done((f32[264,128]{1,0:T(8,128)S(1)}, f32[264,128]{1,0:T(8,128)S(1)}, u32[]{:S(2)}, u32[]{:S(2)}) %collective-permute-start.4) | collective-permute-done | bytes 135200 | tf_op jit(solution)/shard_map/ppermute | solution.py:233
  23.8 1.0 %collective-permute-start.5 = (f32[256,128]{1,0:T(8,128)S(1)}, f32[256,128]{1,0:T(8,128)S(1)}, u32[]{:S(2)}, u32[]{:S(2)}) collective-permute-start(f32[256,128]{1,0:T(8,128)S(1)} %get-tuple-element.71), channel_id=1, source_target_pairs={{0,2},{1,3},{2,0},{3,1},{4,6},{5,7},{6,4},{7,5},{8,10},{9,11},{10,... | collective-permute-start | bytes 393224 | tf_op jit(solution)/shard_map/ppermute | solution.py:233
  24.8 1.4 %collective-permute-start.6 = (f32[256,128]{1,0:T(8,128)S(1)}, f32[256,128]{1,0:T(8,128)S(1)}, u32[]{:S(2)}, u32[]{:S(2)}) collective-permute-start(f32[256,128]{1,0:T(8,128)S(1)} %get-tuple-element.72), channel_id=1, source_target_pairs={{0,4},{1,5},{2,6},{3,7},{4,0},{5,1},{6,2},{7,3},{8,12},{9,13},{10,... | collective-permute-start | bytes 393224 | tf_op jit(solution)/shard_map/ppermute | solution.py:233
  26.6 1.2 %collective-permute-done.5 = f32[256,128]{1,0:T(8,128)S(1)} collective-permute-done((f32[256,128]{1,0:T(8,128)S(1)}, f32[256,128]{1,0:T(8,128)S(1)}, u32[]{:S(2)}, u32[]{:S(2)}) %collective-permute-start.5) | collective-permute-done | bytes 131104 | tf_op jit(solution)/shard_map/ppermute | solution.py:233
  27.7 1.2 %collective-permute-done.6 = f32[256,128]{1,0:T(8,128)S(1)} collective-permute-done((f32[256,128]{1,0:T(8,128)S(1)}, f32[256,128]{1,0:T(8,128)S(1)}, u32[]{:S(2)}, u32[]{:S(2)}) %collective-permute-start.6) | collective-permute-done | bytes 131104 | tf_op jit(solution)/shard_map/ppermute | solution.py:233
  28.9 3.2 %collective-permute-done.7 = f32[256,128]{1,0:T(8,128)S(1)} collective-permute-done((f32[256,128]{1,0:T(8,128)S(1)}, f32[256,128]{1,0:T(8,128)S(1)}, u32[]{:S(2)}, u32[]{:S(2)}) %collective-permute-start.7) | collective-permute-done | bytes 131104 | tf_op jit(solution)/shard_map/ppermute | solution.py:233
  32.3 2.3 %collective-permute-start.8 = (f32[1024,128]{1,0:T(8,128)S(1)}, f32[1024,128]{1,0:T(8,128)S(1)}, u32[]{:S(2)}, u32[]{:S(2)}) collective-permute-start(f32[1024,128]{1,0:T(8,128)S(1)} %get-tuple-element.137), channel_id=1, source_target_pairs={{0,1},{1,0},{2,3},{3,2},{4,5},{5,4},{6,7},{7,6},{8,9},{9,8},{10,11... | collective-permute-start | bytes 1572872 | tf_op jit(solution)/shard_map/ppermute | solution.py:233
  34.6 1.2 %shard_map.97 = (bf16[256,1024]{1,0:T(8,128)(2,1)S(1)}, f32[1024,128]{1,0:T(8,128)S(1)}, f32[8,128]{1,0:T(8,128)S(1)}) custom-call(bf16[256,1024]{1,0:T(8,128)(2,1)S(1)} %get-tuple-element.76.q_ref, bf16[256,1024]{1,0:T(8,128)(2,1)S(1)} %get-tuple-element.77.g_ref, f32[1,2048]{1,0:T(1,128)S(1)} %get-tuple-element.78.gain_ref, ...), custom_call_target="tpu_custom_call" | custom-call | tf_op jit(solution)/shard_map/pallas_call | solution.py:385
  36.1 1.2 %shard_map.98 = (bf16[256,1024]{1,0:T(8,128)(2,1)S(1)}, f32[1048,128]{1,0:T(8,128)S(1)}) custom-call(bf16[256,1024]{1,0:T(8,128)(2,1)S(1)} %get-tuple-element.67.q_ref, bf16[256,1024]{1,0:T(8,128)(2,1)S(1)} %get-tuple-element.68.g_ref, f32[1,2048]{1,0:T(1,128)S(1)} %get-tuple-element.69.gain_ref, f32[256,1024]{1,0:T(8,128)S(1)} %get-tuple-element.70.local_ref, ...), custom_call_target="tpu_custom_call" | custom-call | tf_op jit(solution)/shard_map/pallas_call | solution.py:385
  37.8 1.6 %collective-permute-done.9 = f32[1048,128]{1,0:T(8,128)S(1)} collective-permute-done((f32[1048,128]{1,0:T(8,128)S(1)}, f32[1048,128]{1,0:T(8,128)S(1)}, u32[]{:S(2)}, u32[]{:S(2)}) %collective-permute-start.9) | collective-permute-done | bytes 536608 | tf_op jit(solution)/shard_map/ppermute | solution.py:233
  39.9 1.3 %collective-permute-start.11 = (f32[280,128]{1,0:T(8,128)S(1)}, f32[280,128]{1,0:T(8,128)S(1)}, u32[]{:S(2)}, u32[]{:S(2)}) collective-permute-start(f32[280,128]{1,0:T(8,128)S(1)} %get-tuple-element.85), channel_id=1, source_target_pairs={{0,4},{1,5},{2,6},{3,7},{4,0},{5,1},{6,2},{7,3},{8,12},{9,13},{10,... | collective-permute-start | bytes 430088 | tf_op jit(solution)/shard_map/ppermute | solution.py:233
  42.2 3.1 %shard_map.99 = (bf16[256,2048]{1,0:T(8,128)(2,1)}, f32[256,1024]{1,0:T(8,128)S(1)}, f32[256,1024]{1,0:T(8,128)S(1)}) custom-call(bf16[256,1024]{1,0:T(8,128)(2,1)S(1)} %get-tuple-element.76.q_ref, bf16[256,1024]{1,0:T(8,128)(2,1)S(1)} %get-tuple-element.63.k_ref, bf16[256,1024]{1,0:T(8,128)(2,1)S(1)} %get-tuple-element.64.v_ref, ...), custom_call_target="tpu_custom_call" | custom-call | tf_op jit(solution)/shard_map/pallas_call | solution.py:397
  45.3 3.2 %collective-permute-done.12 = f32[280,128]{1,0:T(8,128)S(1)} collective-permute-done((f32[280,128]{1,0:T(8,128)S(1)}, f32[280,128]{1,0:T(8,128)S(1)}, u32[]{:S(2)}, u32[]{:S(2)}) %collective-permute-start.12) | collective-permute-done | bytes 143392 | tf_op jit(solution)/shard_map/ppermute | solution.py:233
  48.6 2.6 %collective-permute-start.13 = (f32[280,128]{1,0:T(8,128)S(1)}, f32[280,128]{1,0:T(8,128)S(1)}, u32[]{:S(2)}, u32[]{:S(2)}) collective-permute-start(f32[280,128]{1,0:T(8,128)S(1)} %pad_maximum_fusion.11.rest_0_), channel_id=1, source_target_pairs={{0,8},{1,9},{2,10},{3,11},{4,12},{5,13},{6,14},{7,15},{8,0},{9,1},... | collective-permute-start | bytes 430088 | tf_op jit(solution)/shard_map/ppermute | solution.py:233
  51.3 3.1 %shard_map.100 = (bf16[256,2048]{1,0:T(8,128)(2,1)}, f32[256,1024]{1,0:T(8,128)S(1)}, f32[256,1024]{1,0:T(8,128)S(1)}) custom-call(bf16[256,1024]{1,0:T(8,128)(2,1)S(1)} %get-tuple-element.67.q_ref, bf16[256,1024]{1,0:T(8,128)(2,1)S(1)} %get-tuple-element.53.k_ref, bf16[256,1024]{1,0:T(8,128)(2,1)S(1)} %get-tuple-element.54.v_ref, ...), custom_call_target="tpu_custom_call", output_to_operand_aliasing={{0}: (9, {})} | custom-call | tf_op jit(solution)/shard_map/pallas_call | solution.py:397
  54.4 3.3 %collective-permute-done.13 = f32[280,128]{1,0:T(8,128)S(1)} collective-permute-done((f32[280,128]{1,0:T(8,128)S(1)}, f32[280,128]{1,0:T(8,128)S(1)}, u32[]{:S(2)}, u32[]{:S(2)}) %collective-permute-start.13) | collective-permute-done | bytes 143392 | tf_op jit(solution)/shard_map/ppermute | solution.py:233
  58.3 1.3 %collective-permute-start.15 = (f32[256,128]{1,0:T(8,128)S(1)}, f32[256,128]{1,0:T(8,128)S(1)}, u32[]{:S(2)}, u32[]{:S(2)}) collective-permute-start(f32[256,128]{1,0:T(8,128)S(1)} %get-tuple-element.95), channel_id=1, source_target_pairs={{0,4},{1,5},{2,6},{3,7},{4,0},{5,1},{6,2},{7,3},{8,12},{9,13},{10,... | collective-permute-start | bytes 393224 | tf_op jit(solution)/shard_map/ppermute | solution.py:233
  59.5 1.0 %collective-permute-start.16 = (f32[256,128]{1,0:T(8,128)S(1)}, f32[256,128]{1,0:T(8,128)S(1)}, u32[]{:S(2)}, u32[]{:S(2)}) collective-permute-start(f32[256,128]{1,0:T(8,128)S(1)} %get-tuple-element.96), channel_id=1, source_target_pairs={{0,6},{1,7},{2,4},{3,5},{4,2},{5,3},{6,0},{7,1},{8,14},{9,15},{10,... | collective-permute-start | bytes 393224 | tf_op jit(solution)/shard_map/ppermute | solution.py:233
  60.6 1.2 %collective-permute-done.14 = f32[256,128]{1,0:T(8,128)S(1)} collective-permute-done((f32[256,128]{1,0:T(8,128)S(1)}, f32[256,128]{1,0:T(8,128)S(1)}, u32[]{:S(2)}, u32[]{:S(2)}) %collective-permute-start.14) | collective-permute-done | bytes 131104 | tf_op jit(solution)/shard_map/ppermute | solution.py:233
  62.1 2.9 %collective-permute-done.16 = f32[256,128]{1,0:T(8,128)S(1)} collective-permute-done((f32[256,128]{1,0:T(8,128)S(1)}, f32[256,128]{1,0:T(8,128)S(1)}, u32[]{:S(2)}, u32[]{:S(2)}) %collective-permute-start.16) | collective-permute-done | bytes 131104 | tf_op jit(solution)/shard_map/ppermute | solution.py:233
  65.1 2.9 %collective-permute-start.17 = (f32[1024,128]{1,0:T(8,128)S(1)}, f32[1024,128]{1,0:T(8,128)S(1)}, u32[]{:S(2)}, u32[]{:S(2)}) collective-permute-start(f32[1024,128]{1,0:T(8,128)S(1)} %get-tuple-element.135), channel_id=1, source_target_pairs={{0,1},{1,0},{2,3},{3,2},{4,5},{5,4},{6,7},{7,6},{8,9},{9,8},{10,11... | collective-permute-start | bytes 1572872 | tf_op jit(solution)/shard_map/ppermute | solution.py:233
  68.6 1.3 %shard_map.101 = (bf16[256,2048]{1,0:T(8,128)(2,1)}, bf16[256,2048]{1,0:T(8,128)(2,1)}) custom-call(bf16[256,1024]{1,0:T(8,128)(2,1)S(1)} %get-tuple-element.63.k_ref, bf16[256,1024]{1,0:T(8,128)(2,1)S(1)} %get-tuple-element.64.v_ref, f32[256,1024]{1,0:T(8,128)S(1)} %get-tuple-element.88.kp_ref, f32[256,1024]{1,0:T(8,128)S(1)} %get-tuple-element.97.vp_ref, ...), custom_call_target="tpu_custom_call" | custom-call | tf_op jit(solution)/shard_map/pallas_call | solution.py:413
  69.9 1.3 %shard_map.102 = (bf16[256,2048]{1,0:T(8,128)(2,1)}, bf16[256,2048]{1,0:T(8,128)(2,1)}) custom-call(bf16[256,1024]{1,0:T(8,128)(2,1)S(1)} %get-tuple-element.53.k_ref, bf16[256,1024]{1,0:T(8,128)(2,1)S(1)} %get-tuple-element.54.v_ref, f32[256,1024]{1,0:T(8,128)S(1)} %get-tuple-element.92.kp_ref, ...), custom_call_target="tpu_custom_call", output_to_operand_aliasing={{0}: (6, {}), {1}: (7, {})} | custom-call | tf_op jit(solution)/shard_map/pallas_call | solution.py:413
  (44 shorter events, 5.3 us)
Async XLA Ops:
  2.4 2.0 %collective-permute-start = (f32[1032,128]{1,0:T(8,128)S(1)}, f32[1032,128]{1,0:T(8,128)S(1)}, u32[]{:S(2)}, u32[]{:S(2)}) collective-permute-start(f32[1032,128]{1,0:T(8,128)S(1)} %get-tuple-element.59), channel_id=1, source_target_pairs={{0,1},{1,0},{2,3},{3,2},{4,5},{5,4},{6,7},{7,6},{8,9},{9,8},{10,11... | collective-permute-start | bytes 1585160 | tf_op jit(solution)/shard_map/ppermute | solution.py:233
  4.5 6.5 %collective-permute-start.1 = (f32[264,128]{1,0:T(8,128)S(1)}, f32[264,128]{1,0:T(8,128)S(1)}, u32[]{:S(2)}, u32[]{:S(2)}) collective-permute-start(f32[264,128]{1,0:T(8,128)S(1)} %get-tuple-element.60), channel_id=1, source_target_pairs={{0,2},{1,3},{2,0},{3,1},{4,6},{5,7},{6,4},{7,5},{8,10},{9,11},{10,... | collective-permute-start | bytes 405512 | tf_op jit(solution)/shard_map/ppermute | solution.py:233
  7.3 4.8 %collective-permute-start.2 = (f32[264,128]{1,0:T(8,128)S(1)}, f32[264,128]{1,0:T(8,128)S(1)}, u32[]{:S(2)}, u32[]{:S(2)}) collective-permute-start(f32[264,128]{1,0:T(8,128)S(1)} %get-tuple-element.61), channel_id=1, source_target_pairs={{0,4},{1,5},{2,6},{3,7},{4,0},{5,1},{6,2},{7,3},{8,12},{9,13},{10,... | collective-permute-start | bytes 405512 | tf_op jit(solution)/shard_map/ppermute | solution.py:233
  8.6 6.3 %collective-permute-start.3 = (f32[264,128]{1,0:T(8,128)S(1)}, f32[264,128]{1,0:T(8,128)S(1)}, u32[]{:S(2)}, u32[]{:S(2)}) collective-permute-start(f32[264,128]{1,0:T(8,128)S(1)} %get-tuple-element.62._), channel_id=1, source_target_pairs={{0,6},{1,7},{2,4},{3,5},{4,2},{5,3},{6,0},{7,1},{8,14},{9,15},{10,... | collective-permute-start | bytes 405512 | tf_op jit(solution)/shard_map/ppermute | solution.py:233
  15.0 8.7 %collective-permute-start.4 = (f32[264,128]{1,0:T(8,128)S(1)}, f32[264,128]{1,0:T(8,128)S(1)}, u32[]{:S(2)}, u32[]{:S(2)}) collective-permute-start(f32[264,128]{1,0:T(8,128)S(1)} %pad_maximum_fusion.12._), channel_id=1, source_target_pairs={{0,8},{1,9},{2,10},{3,11},{4,12},{5,13},{6,14},{7,15},{8,0},{9,1},... | collective-permute-start | bytes 405512 | tf_op jit(solution)/shard_map/ppermute | solution.py:233
  23.8 3.9 %collective-permute-start.5 = (f32[256,128]{1,0:T(8,128)S(1)}, f32[256,128]{1,0:T(8,128)S(1)}, u32[]{:S(2)}, u32[]{:S(2)}) collective-permute-start(f32[256,128]{1,0:T(8,128)S(1)} %get-tuple-element.71), channel_id=1, source_target_pairs={{0,2},{1,3},{2,0},{3,1},{4,6},{5,7},{6,4},{7,5},{8,10},{9,11},{10,... | collective-permute-start | bytes 393224 | tf_op jit(solution)/shard_map/ppermute | solution.py:233
  24.8 4.1 %collective-permute-start.6 = (f32[256,128]{1,0:T(8,128)S(1)}, f32[256,128]{1,0:T(8,128)S(1)}, u32[]{:S(2)}, u32[]{:S(2)}) collective-permute-start(f32[256,128]{1,0:T(8,128)S(1)} %get-tuple-element.72), channel_id=1, source_target_pairs={{0,4},{1,5},{2,6},{3,7},{4,0},{5,1},{6,2},{7,3},{8,12},{9,13},{10,... | collective-permute-start | bytes 393224 | tf_op jit(solution)/shard_map/ppermute | solution.py:233
  26.2 6.0 %collective-permute-start.7 = (f32[256,128]{1,0:T(8,128)S(1)}, f32[256,128]{1,0:T(8,128)S(1)}, u32[]{:S(2)}, u32[]{:S(2)}) collective-permute-start(f32[256,128]{1,0:T(8,128)S(1)} %get-tuple-element.73), channel_id=1, source_target_pairs={{0,6},{1,7},{2,4},{3,5},{4,2},{5,3},{6,0},{7,1},{8,14},{9,15},{10,... | collective-permute-start | bytes 393224 | tf_op jit(solution)/shard_map/ppermute | solution.py:233
  32.3 3.8 %collective-permute-start.8 = (f32[1024,128]{1,0:T(8,128)S(1)}, f32[1024,128]{1,0:T(8,128)S(1)}, u32[]{:S(2)}, u32[]{:S(2)}) collective-permute-start(f32[1024,128]{1,0:T(8,128)S(1)} %get-tuple-element.137), channel_id=1, source_target_pairs={{0,1},{1,0},{2,3},{3,2},{4,5},{5,4},{6,7},{7,6},{8,9},{9,8},{10,11... | collective-permute-start | bytes 1572872 | tf_op jit(solution)/shard_map/ppermute | solution.py:233
  37.4 2.0 %collective-permute-start.9 = (f32[1048,128]{1,0:T(8,128)S(1)}, f32[1048,128]{1,0:T(8,128)S(1)}, u32[]{:S(2)}, u32[]{:S(2)}) collective-permute-start(f32[1048,128]{1,0:T(8,128)S(1)} %get-tuple-element.83), channel_id=1, source_target_pairs={{0,1},{1,0},{2,3},{3,2},{4,5},{5,4},{6,7},{7,6},{8,9},{9,8},{10,11... | collective-permute-start | bytes 1609736 | tf_op jit(solution)/shard_map/ppermute | solution.py:233
  39.5 5.8 %collective-permute-start.10 = (f32[280,128]{1,0:T(8,128)S(1)}, f32[280,128]{1,0:T(8,128)S(1)}, u32[]{:S(2)}, u32[]{:S(2)}) collective-permute-start(f32[280,128]{1,0:T(8,128)S(1)} %get-tuple-element.84), channel_id=1, source_target_pairs={{0,2},{1,3},{2,0},{3,1},{4,6},{5,7},{6,4},{7,5},{8,10},{9,11},{10,... | collective-permute-start | bytes 430088 | tf_op jit(solution)/shard_map/ppermute | solution.py:233
  39.9 5.4 %collective-permute-start.11 = (f32[280,128]{1,0:T(8,128)S(1)}, f32[280,128]{1,0:T(8,128)S(1)}, u32[]{:S(2)}, u32[]{:S(2)}) collective-permute-start(f32[280,128]{1,0:T(8,128)S(1)} %get-tuple-element.85), channel_id=1, source_target_pairs={{0,4},{1,5},{2,6},{3,7},{4,0},{5,1},{6,2},{7,3},{8,12},{9,13},{10,... | collective-permute-start | bytes 430088 | tf_op jit(solution)/shard_map/ppermute | solution.py:233
  41.2 7.2 %collective-permute-start.12 = (f32[280,128]{1,0:T(8,128)S(1)}, f32[280,128]{1,0:T(8,128)S(1)}, u32[]{:S(2)}, u32[]{:S(2)}) collective-permute-start(f32[280,128]{1,0:T(8,128)S(1)} %get-tuple-element.86.rest_0_), channel_id=1, source_target_pairs={{0,6},{1,7},{2,4},{3,5},{4,2},{5,3},{6,0},{7,1},{8,14},{9,15},{10,... | collective-permute-start | bytes 430088 | tf_op jit(solution)/shard_map/ppermute | solution.py:233
  48.6 9.1 %collective-permute-start.13 = (f32[280,128]{1,0:T(8,128)S(1)}, f32[280,128]{1,0:T(8,128)S(1)}, u32[]{:S(2)}, u32[]{:S(2)}) collective-permute-start(f32[280,128]{1,0:T(8,128)S(1)} %pad_maximum_fusion.11.rest_0_), channel_id=1, source_target_pairs={{0,8},{1,9},{2,10},{3,11},{4,12},{5,13},{6,14},{7,15},{8,0},{9,1},... | collective-permute-start | bytes 430088 | tf_op jit(solution)/shard_map/ppermute | solution.py:233
  57.8 3.9 %collective-permute-start.14 = (f32[256,128]{1,0:T(8,128)S(1)}, f32[256,128]{1,0:T(8,128)S(1)}, u32[]{:S(2)}, u32[]{:S(2)}) collective-permute-start(f32[256,128]{1,0:T(8,128)S(1)} %get-tuple-element.94), channel_id=1, source_target_pairs={{0,2},{1,3},{2,0},{3,1},{4,6},{5,7},{6,4},{7,5},{8,10},{9,11},{10,... | collective-permute-start | bytes 393224 | tf_op jit(solution)/shard_map/ppermute | solution.py:233
  58.3 3.8 %collective-permute-start.15 = (f32[256,128]{1,0:T(8,128)S(1)}, f32[256,128]{1,0:T(8,128)S(1)}, u32[]{:S(2)}, u32[]{:S(2)}) collective-permute-start(f32[256,128]{1,0:T(8,128)S(1)} %get-tuple-element.95), channel_id=1, source_target_pairs={{0,4},{1,5},{2,6},{3,7},{4,0},{5,1},{6,2},{7,3},{8,12},{9,13},{10,... | collective-permute-start | bytes 393224 | tf_op jit(solution)/shard_map/ppermute | solution.py:233
  59.5 5.4 %collective-permute-start.16 = (f32[256,128]{1,0:T(8,128)S(1)}, f32[256,128]{1,0:T(8,128)S(1)}, u32[]{:S(2)}, u32[]{:S(2)}) collective-permute-start(f32[256,128]{1,0:T(8,128)S(1)} %get-tuple-element.96), channel_id=1, source_target_pairs={{0,6},{1,7},{2,4},{3,5},{4,2},{5,3},{6,0},{7,1},{8,14},{9,15},{10,... | collective-permute-start | bytes 393224 | tf_op jit(solution)/shard_map/ppermute | solution.py:233
  65.1 4.9 %collective-permute-start.17 = (f32[1024,128]{1,0:T(8,128)S(1)}, f32[1024,128]{1,0:T(8,128)S(1)}, u32[]{:S(2)}, u32[]{:S(2)}) collective-permute-start(f32[1024,128]{1,0:T(8,128)S(1)} %get-tuple-element.135), channel_id=1, source_target_pairs={{0,1},{1,0},{2,3},{3,2},{4,5},{5,4},{6,7},{7,6},{8,9},{9,8},{10,11... | collective-permute-start | bytes 1572872 | tf_op jit(solution)/shard_map/ppermute | solution.py:233

commit v6 on v5

--- a/solution.py
+++ b/solution.py
@@ -129,15 +129,7 @@
     return jnp.concatenate(parts, axis=1)
 
 
-def local_kernel(
-    q_hbm, g_hbm, gain_hbm, k_ref, v_ref, start_ref, _,
-    out_ref, q_ref, g_ref, gain_ref, q_sems, g_sems, gain_sem, *, other,
-):
-    copies = fetch(other, [q_hbm], [q_ref], q_sems)
-    grad_copies = fetch(other, [g_hbm], [g_ref], g_sems)
-    gain_copy = pltpu.make_async_copy(gain_hbm, gain_ref, gain_sem)
-    gain_copy.start()
-    mask = sight(start_ref, False)
+def attend(q_ref, k_ref, v_ref, copies, mask, put_out):
     pairs = len(copies)
     for begin in range(0, pairs, TOGETHER):
         together = range(begin, min(begin + TOGETHER, pairs))
@@ -146,45 +138,80 @@
         for pair in together:
             c = head(pair)
             scores = dot(q_ref[:, c], k_ref[:, c], 1, 1).astype(BF16) * mask
-            out_ref[:, c] = dot(scores, v_ref[:, c], 1, 0)
+            put_out(c, dot(scores, v_ref[:, c], 1, 0))
+
+
+def local_kernel(
+    q_hbm, g_hbm, gain_hbm, k_ref, v_ref, start_ref, _,
+    out_ref, q_ref, g_ref, gain_ref, q_sems, g_sems, gain_sem,
+):
+    copies = fetch(0, [q_hbm], [q_ref], q_sems)
+    grad_copies = fetch(0, [g_hbm], [g_ref], g_sems)
+    gain_copy = pltpu.make_async_copy(gain_hbm, gain_ref, gain_sem)
+    gain_copy.start()
+
+    def put_out(c, local):
+        out_ref[:, c] = local
+
+    attend(q_ref, k_ref, v_ref, copies, sight(start_ref, False), put_out)
     for (copy,) in grad_copies:
         copy.wait()
     gain_copy.wait()
 
 
-def middle_kernel(q_ref, g_ref, gain_ref, local_ref, carry_ref, use_ref, *rest, other):
-    if other:
-        flag_ref, sums_ref, d_ref, state_ref = rest
-    else:
-        d_ref, state_ref, sums_ref = rest
+def other_local_kernel(
+    q_hbm, g_hbm, k_ref, v_ref, start_ref, use_ref, _,
+    out_ref, q_ref, g_ref, q_sems, g_sems,
+):
+    copies = fetch(1, [q_hbm], [q_ref], q_sems)
+    grad_copies = fetch(1, [g_hbm], [g_ref], g_sems)
+    rows = q_ref.shape[0]
+    use = use_ref[...]
+
+    def put_out(c, local):
+        out_ref[:rows, c] = local
+        out_ref[rows : 2 * rows, c] = (q_ref[:, c] * use).astype(F32)
+
+    attend(q_ref, k_ref, v_ref, copies, sight(start_ref, False), put_out)
+    for (copy,) in grad_copies:
+        copy.wait()
+    for pair in range(len(copies)):
+        out_ref[2 * rows :, head(pair)] = g_ref[:, head(pair)].astype(F32)
+
+
+def through_norm(local, used, grad, gain, carry):
+    attended = local + dot(used, carry.astype(BF16), 1, 0)
+    d_norm = grad * gain
+    square = jnp.mean(attended * attended, axis=1, keepdims=True)
+    centre = jnp.mean(d_norm * attended, axis=1, keepdims=True)
+    inverse = lax.rsqrt(square + EPS)
+    total = jnp.sum(grad * (attended * inverse), axis=0, keepdims=True)
+    d_att = ((d_norm - attended * (centre * inverse * inverse)) * inverse).astype(BF16)
+    return d_att, dot(used, d_att, 0, 0), total
+
+
+def middle_kernel(
+    q_ref, g_ref, gain_ref, local_ref, other_ref, mine_ref, theirs_ref, use_ref,
+    d_ref, other_d_ref, state_ref, other_state_ref, sums_ref,
+):
+    rows = q_ref.shape[0]
     pairs = q_ref.shape[1] // E
-    use = use_ref[...]
-    core = lax.axis_index("ctx") % 2
     for pair in range(pairs):
-        c = head(pair)
-        used = q_ref[:, c] * use
-        carry = carry_ref[place(pair, pairs), :].astype(BF16)
-        attended = local_ref[:, c] + dot(used, carry, 1, 0)
-        grad = g_ref[:, c].astype(F32)
-        d_norm = grad * gain_ref[:, owner_column(pair, other)]
-        square = jnp.mean(attended * attended, axis=1, keepdims=True)
-        centre = jnp.mean(d_norm * attended, axis=1, keepdims=True)
-        inverse = lax.rsqrt(square + EPS)
-        gained = grad * (attended * inverse)
-        d_att = ((d_norm - attended * (centre * inverse * inverse)) * inverse).astype(BF16)
+        c, where = head(pair), place(pair, pairs)
+        gain = gain_ref[:, owner_column(pair, 0)]
+        d_att, state, total = through_norm(
+            local_ref[:, c], q_ref[:, c] * use_ref[...], g_ref[:, c].astype(F32), gain,
+            mine_ref[where, :],
+        )
         d_ref[:, c] = d_att
-        state_ref[place(pair, pairs), :] = dot(used, d_att, 0, 0)
-        total = jnp.sum(gained, axis=0, keepdims=True)
-        if other:
-            both = jnp.concatenate(
-                crossed(core == 0, total, sums_ref[pair : pair + 1, :])
-            )
-            begin = pairs * E + FLAG + 2 * pair
-            state_ref[begin : begin + 2, :] = both
-        else:
-            sums_ref[pair : pair + 1, :] = total
-    if other:
-        state_ref[pairs * E : pairs * E + FLAG, :] = flag_ref[...]
+        state_ref[where, :] = state
+        d_att, state, other_total = through_norm(
+            other_ref[:rows, c], other_ref[rows : 2 * rows, c].astype(BF16),
+            other_ref[2 * rows :, c], gain, theirs_ref[where, :],
+        )
+        other_d_ref[:, c] = d_att.astype(F32)
+        other_state_ref[where, :] = state
+        sums_ref[pair : pair + 1, :] = total + other_total
 
 
 def spread_kernel(
@@ -199,7 +226,7 @@
     for pair in range(pairs):
         c = head(pair)
         carry = carry_ref[place(pair, pairs), :].astype(BF16)
-        query, key, value, d_att = q_ref[:, c], k_ref[:, c], v_ref[:, c], d_ref[:, c]
+        query, key, value, d_att = q_ref[:, c], k_ref[:, c], v_ref[:, c], d_ref[:, c].astype(BF16)
         dscores = dot(d_att, value, 1, 1).astype(BF16) * mask
         from_carry = dot(d_att * use, carry, 1, 1)
         qg_ref[:, c] = (dot(dscores, key, 1, 0) + from_carry).astype(BF16)
@@ -249,9 +276,9 @@
     return [a, b, c, d]
 
 
-def scan(keep, send, bits, backward, early):
+def scan(own, partner, own_flag, partner_flag, extra, bits, backward, summed):
     count = lax.axis_size("ctx")
-    rows = keep.shape[0]
+    rows = own.shape[0]
     part = rows // SQUARE
 
     def last(distance):
@@ -262,15 +289,13 @@
     def packed(block, flag, extra):
         return jnp.concatenate([block, jnp.broadcast_to(flag, (FLAG, E)), extra])
 
-    (got,) = yield [(send, 1)]
-    core_flag, late_flag = crossed(last(1), send[rows : rows + 1], got[rows : rows + 1])
-    extra = send[rows + FLAG :] + got[rows + FLAG :]
-    first_core = jnp.where(last(1), got[:rows], keep)
+    core_flag, late_flag = crossed(last(1), own_flag, partner_flag)
+    first_core = jnp.where(last(1), partner, own)
     flag = jnp.maximum(core_flag, late_flag)
 
     def both_cores(number):
         where = slice(number * part, (number + 1) * part)
-        early, late = crossed(last(1), keep[where], got[where])
+        early, late = crossed(last(1), own[where], partner[where])
         return late + (1.0 - late_flag) * early
 
     gots = yield [
@@ -296,15 +321,13 @@
         flag, total = (jnp.where(last(distance), b, a) for a, b in zip(after, ahead))
         distance *= 2
 
+    summed(extra)
     results = [before[1]] + [combine(before, run)[1] for run in runs]
     results = permuted(results, last(2), last(4))
     gots = yield [(results[number], 2 * number) for number in range(1, SQUARE)]
     before = jnp.concatenate([results[0], *gots])
     after = first_core + (1.0 - core_flag) * before
-    mine, theirs = crossed(last(1), before, after)
-    early(mine)
-    (got,) = yield [(theirs, 1)]
-    return got, extra
+    return crossed(last(1), before, after)
 
 
 def run(chain, work):
@@ -354,7 +377,8 @@
     grad = held(tokens, width, BF16, ANY)
     row = held(tokens, E, BF16)
     staging = pltpu.VMEM((tokens, half), BF16)
-    keys, values, local, carried, middle, spread = {}, {}, {}, {}, {}, {}
+    keys, values, query, local, carried, d_att, spread = {}, {}, {}, {}, {}, {}, {}
+    norm_inputs, middle = [], []
     send, keys[1], values[1], start, end, use, tail, flag, bits = call(
         send_state_kernel,
         [ANY] * 3,
@@ -369,28 +393,27 @@
         [copies(pairs, 2)],
     )(key_vectors, value_vectors, tail)
 
-    def local_of(other, token):
-        local[other] = call(
+    def other_local_of(token):
+        pack, other_query = call(
+            other_local_kernel,
+            [ANY] * 2 + [VMEM] * 4 + [ANY],
+            [held(3 * tokens, half), narrow],
+            [pltpu.VMEM((tokens, half), BF16), copies(pairs, 1), copies(pairs, 1)],
+        )(queries, out_grad, keys[1], values[1], start, use, token)
+        query[1] = other_query
+        middle[:] = [pack]
+        return other_query
+
+    def local_of(token):
+        local[0], query[0], *rest = call(
             local_kernel,
             [ANY] * 3 + [VMEM] * 3 + [ANY],
             [single, narrow, narrow, held(1, width)],
             [copies(pairs, 1), copies(pairs, 1), copies()],
-            other=other,
-        )(queries, out_grad, gains, keys[other], values[other], start, token)
-        return local[other][0]
-
-    def middle_of(other, carry):
-        carried[other] = carry
-        state = held(rows + FLAG + 2 * pairs, E) if other else held(rows, E)
-        middle[other] = call(
-            middle_kernel,
-            [VMEM] * (8 if other else 6),
-            [narrow, state] if other else [narrow, state, held(pairs, E)],
-            other=other,
-        )(
-            *local[other][1:], local[other][0], carry, use,
-            *([flag, middle[0][2]] if other else []),
-        )
+        )(queries, out_grad, gains, keys[0], values[0], start, token)
+        norm_inputs[:] = rest
+        local[1] = swap(lax.optimization_barrier((middle[0], token))[0], 1)
+        return local[0], local[1]
 
     def spread_of(other, token):
         done = spread[0][:1] if other else []
@@ -402,12 +425,24 @@
             {9: 0} if done else {},
             other=other,
         )(
-            local[other][1], keys[other], values[other], middle[other][0], carried[other],
+            query[other], keys[other], values[other], d_att[other], carried[other],
             use, start, end, token, *done,
         )
         return spread[other][1]
 
-    grads = []
+    def first_spread_of(token):
+        done = spread_of(0, token)
+        d_other, theirs = lax.optimization_barrier((middle, done))[0]
+        d_att[1], carried[1] = swap(d_other, 1), swap(theirs, 1)
+        return done
+
+    def last_spread_of(token):
+        done = spread_of(1, token)
+        sums = lax.optimization_barrier((gain_sums[0], done))[0]
+        gain_sums.append(swap(sums, 1))
+        return done, gain_sums[1]
+
+    grads, gain_sums = [], []
 
     def final_of(other, later):
         grads[:] = call(
@@ -420,20 +455,38 @@
         )(keys[other], values[other], *spread[other][1:], later, tail, *grads)
 
     def chain():
-        got, _ = yield from scan(keep, send, bits, False, functools.partial(middle_of, 0))
-        middle_of(1, got)
-        states = middle[0][1], middle[1][1]
-        got, total = yield from scan(*states, bits, True, functools.partial(final_of, 0))
+        (got,) = yield [(send, 1)]
+        own_flag, other_flag = flag[:1], got[rows : rows + 1]
+        nothing = jnp.zeros((0, E), F32)
+        mine, theirs = yield from scan(
+            keep, got[:rows], own_flag, other_flag, nothing, bits, False, lambda _: None
+        )
+        carried[0] = mine
+        d_att[0], other_d, state, other_state, sums = call(
+            middle_kernel,
+            [VMEM] * 8,
+            [narrow, single, held(rows, E), held(rows, E), held(pairs, E)],
+        )(query[0], *norm_inputs, local[0], local[1], mine, theirs, use)
+        middle[:] = other_d, theirs
+        mine, theirs = yield from scan(
+            state, other_state, own_flag, other_flag, sums, bits, True, gain_sums.append
+        )
+        final_of(0, mine)
+        (got,) = yield [(theirs, 1)]
         final_of(1, got)
-        return total
-
-    steps = levels + 1
-    work = {}
-    for begin, part in ((0, local_of), (steps, spread_of)):
-        work[begin + 1] = functools.partial(part, 0)
-        work[begin + steps - 3] = functools.partial(part, 1)
-    total = run(chain(), work)
-    gain_grad = total.reshape(width) / math.sqrt(tokens * lax.axis_size("ctx"))
+
+    doubling = levels - 3
+    back = 3 + doubling
+    work = {
+        1: other_local_of,
+        1 + doubling: local_of,
+        back: first_spread_of,
+        back + doubling: lambda _: (d_att[1], carried[1]),
+        back + doubling + 1: last_spread_of,
+    }
+    run(chain(), work)
+    gain_sums = jnp.stack(crossed(bits[:1] > 0.5, *gain_sums), axis=1)
+    gain_grad = gain_sums.reshape(width) / math.sqrt(tokens * lax.axis_size("ctx"))
     return spread[1][0], *grads, gain_grad
 
 

time: 71.7 us -> 69.7 us (0.972)
  waiting for transfers between devices: 26.1 us -> 19.1 us
  starting transfers between devices: 23.2 us -> 28.1 us
    ppermute x18 -> x20, waiting for transfers between devices: 26.1 us -> 19.1 us  [swap(): return lax.ppermute(block, 'ctx', [(i, i ^ distance) for i in range(count)])]
    ppermute x18 -> x20, starting transfers between devices: 23.2 us -> 28.1 us  [swap(): return lax.ppermute(block, 'ctx', [(i, i ^ distance) for i in range(count)])]
    pallas_call x2, Pallas kernels: 2.42 us -> 4.93 us  [the longest x1 2.66 us: other_local_of(): call(other_local_kernel, [ANY] * 2 + [VMEM] * 4 + [ANY], [held(3 * tokens...]
    pallas_call x2 -> x1, Pallas kernels: 4.71 us -> 2.36 us  [local_of(): call(local_kernel, [ANY] * 3 + [VMEM] * 3 + [ANY], [single, narrow, narro...]
  transfers between devices with their start and end apart: 18 -> 20, of which waited for: 15 -> 9; matrix products, arithmetic and copies ran while one was open for 1% -> 2% of each run, Pallas kernels for 21% -> 21%
where the time goes in v6:
time: 69.7 us; the launch traced here: 69.3 us
  starting transfers between devices  28.1 us (40%)
  Pallas kernels  19.6 us (28%)
  waiting for transfers between devices  19.1 us (27%)
  other arithmetic  0.96 us (1%)
  between operations  0.91 us (1%)
    ppermute x20, starting transfers between devices, swap(): return lax.ppermute(block, 'ctx', [(i, i ^ distance) for i in range(count)])  28.1 us
    ppermute x20, waiting for transfers between devices, swap(): return lax.ppermute(block, 'ctx', [(i, i ^ distance) for i in range(count)])  19.1 us
    pallas_call x2, Pallas kernels, spread_of(): call(spread_kernel, [VMEM] * 8 + [ANY] * (1 + len(done)), [grad, single,...  6.13 us
    pallas_call x2, Pallas kernels, final_of(): call(final_kernel, [VMEM] * 6 + [ANY] * len(grads), [grad, grad], [stagin...  2.66 us
    pallas_call x1, Pallas kernels, other_local_of(): call(other_local_kernel, [ANY] * 2 + [VMEM] * 4 + [ANY], [held(3 * tokens...  2.66 us
    pallas_call x1, Pallas kernels, local_of(): call(local_kernel, [ANY] * 3 + [VMEM] * 3 + [ANY], [single, narrow, narro...  2.36 us
    pallas_call x1, Pallas kernels, chain(): call(middle_kernel, [VMEM] * 8, [narrow, single, held(rows, E), held(rows...  2.28 us
    pallas_call x1, Pallas kernels, shards(): call(send_state_kernel, [ANY] * 3, [held(rows + FLAG, E), narrow, narrow,...  1.79 us
  transfers between devices with their start and end apart: 20, of which 9 were waited for; matrix products, arithmetic and copies ran while one was open for 2% of the time, Pallas kernels for 21%

profile of v6, /device:TPU:1, one launch (start us, length us, event | category | flops | bytes accessed | tf_op | source)
XLA Modules:
  0.0 69.3 jit_solution(10095994472505366238)
XLA Ops:
  0.6 1.8 %shard_map.93 = (f32[1032,128]{1,0:T(8,128)S(1)}, bf16[256,1024]{1,0:T(8,128)(2,1)S(1)}, bf16[256,1024]{1,0:T(8,128)(2,1)S(1)}, s32[256,128]{1,0:T(8,128)S(1)}, ...) custom-call(s32[2,2]{1,0:T(2,128)} %bounds_hbm.1, ...), custom_call_target="tpu_custom_call" | custom-call | tf_op jit(solution)/shard_map/pallas_call | solution.py:382
  2.6 1.8 %shard_map.94 = (f32[1024,128]{1,0:T(8,128)S(1)}, bf16[256,1024]{1,0:T(8,128)(2,1)S(1)}, bf16[256,1024]{1,0:T(8,128)(2,1)S(1)}) custom-call(bf16[256,2048]{1,0:T(8,128)(2,1)} %k_hbm.3, bf16[256,2048]{1,0:T(8,128)(2,1)} %v_hbm.3, bf16[256,128]{1,0:T(8,128)(2,1)S(1)} %get-tuple-element.61.tail_ref), custom_call_target="tpu_custom_call" | custom-call | tf_op jit(solution)/shard_map/pallas_call | solution.py:389
  4.6 2.7 %collective-permute-start.1 = (f32[264,128]{1,0:T(8,128)S(1)}, f32[264,128]{1,0:T(8,128)S(1)}, u32[]{:S(2)}, u32[]{:S(2)}) collective-permute-start(f32[264,128]{1,0:T(8,128)S(1)} %get-tuple-element.69), channel_id=1, source_target_pairs={{0,2},{1,3},{2,0},{3,1},{4,6},{5,7},{6,4},{7,5},{8,10},{9,11},{10,... | collective-permute-start | bytes 405512 | tf_op jit(solution)/shard_map/ppermute | solution.py:260
  7.3 1.3 %collective-permute-start.2 = (f32[264,128]{1,0:T(8,128)S(1)}, f32[264,128]{1,0:T(8,128)S(1)}, u32[]{:S(2)}, u32[]{:S(2)}) collective-permute-start(f32[264,128]{1,0:T(8,128)S(1)} %get-tuple-element.70), channel_id=1, source_target_pairs={{0,4},{1,5},{2,6},{3,7},{4,0},{5,1},{6,2},{7,3},{8,12},{9,13},{10,... | collective-permute-start | bytes 405512 | tf_op jit(solution)/shard_map/ppermute | solution.py:260
  8.6 2.7 %shard_map.95 = (f32[768,1024]{1,0:T(8,128)S(1)}, bf16[256,1024]{1,0:T(8,128)(2,1)S(1)}) custom-call(bf16[256,2048]{1,0:T(8,128)(2,1)} %q_hbm.3, bf16[256,2048]{1,0:T(8,128)(2,1)} %g_hbm.3, bf16[256,1024]{1,0:T(8,128)(2,1)S(1)} %get-tuple-element.56.k_ref, bf16[256,1024]{1,0:T(8,128)(2,1)S(1)} %get-tuple-element.57.v_ref, ...), custom_call_target="tpu_custom_call" | custom-call | tf_op jit(solution)/shard_map/pallas_call | solution.py:397
  11.3 0.8 %collective-permute-done.2 = f32[264,128]{1,0:T(8,128)S(1)} collective-permute-done((f32[264,128]{1,0:T(8,128)S(1)}, f32[264,128]{1,0:T(8,128)S(1)}, u32[]{:S(2)}, u32[]{:S(2)}) %collective-permute-start.2) | collective-permute-done | bytes 135200 | tf_op jit(solution)/shard_map/ppermute | solution.py:260
  12.1 2.8 %collective-permute-done.3 = f32[264,128]{1,0:T(8,128)S(1)} collective-permute-done((f32[264,128]{1,0:T(8,128)S(1)}, f32[264,128]{1,0:T(8,128)S(1)}, u32[]{:S(2)}, u32[]{:S(2)}) %collective-permute-start.3) | collective-permute-done | bytes 135200 | tf_op jit(solution)/shard_map/ppermute | solution.py:260
  15.0 1.1 %collective-permute-start.4 = (f32[768,1024]{1,0:T(8,128)S(1)}, f32[768,1024]{1,0:T(8,128)S(1)}, u32[]{:S(2)}, u32[]{:S(2)}) collective-permute-start(f32[768,1024]{1,0:T(8,128)S(1)} %get-tuple-element.77), channel_id=1, source_target_pairs={{0,1},{1,0},{2,3},{3,2},{4,5},{5,4},{6,7},{7,6},{8,9},{9,8},{10,11... | collective-permute-start | bytes 9437192 | tf_op jit(solution)/shard_map/ppermute | solution.py:260
  16.2 2.5 %collective-permute-start.5 = (f32[264,128]{1,0:T(8,128)S(1)}, f32[264,128]{1,0:T(8,128)S(1)}, u32[]{:S(2)}, u32[]{:S(2)}) collective-permute-start(f32[264,128]{1,0:T(8,128)S(1)} %pad_maximum_fusion.12._), channel_id=1, source_target_pairs={{0,8},{1,9},{2,10},{3,11},{4,12},{5,13},{6,14},{7,15},{8,0},{9,1},... | collective-permute-start | bytes 405512 | tf_op jit(solution)/shard_map/ppermute | solution.py:260
  18.7 2.4 %shard_map.96 = (f32[256,1024]{1,0:T(8,128)S(1)}, bf16[256,1024]{1,0:T(8,128)(2,1)S(1)}, bf16[256,1024]{1,0:T(8,128)(2,1)S(1)}, f32[1,2048]{1,0:T(1,128)S(1)}) custom-call(bf16[256,2048]{1,0:T(8,128)(2,1)} %q_hbm.3, bf16[256,2048]{1,0:T(8,128)(2,1)} %g_hbm.3, f32[1,2048]{1,0:T(1,128)} %bitcast.60, bf16[256,1024]{1,0:T(8,128)(2,1)S(1)} %get-tuple-element.67.k_ref, ...), custom_call_target="tpu_custom_call" | custom-call | tf_op jit(solution)/shard_map/pallas_call | solution.py:408
  21.0 4.3 %collective-permute-done.5 = f32[264,128]{1,0:T(8,128)S(1)} collective-permute-done((f32[264,128]{1,0:T(8,128)S(1)}, f32[264,128]{1,0:T(8,128)S(1)}, u32[]{:S(2)}, u32[]{:S(2)}) %collective-permute-start.5) | collective-permute-done | bytes 135200 | tf_op jit(solution)/shard_map/ppermute | solution.py:260
  25.5 1.3 %collective-permute-start.6 = (f32[256,128]{1,0:T(8,128)S(1)}, f32[256,128]{1,0:T(8,128)S(1)}, u32[]{:S(2)}, u32[]{:S(2)}) collective-permute-start(f32[256,128]{1,0:T(8,128)S(1)} %get-tuple-element.78), channel_id=1, source_target_pairs={{0,2},{1,3},{2,0},{3,1},{4,6},{5,7},{6,4},{7,5},{8,10},{9,11},{10,... | collective-permute-start | bytes 393224 | tf_op jit(solution)/shard_map/ppermute | solution.py:260
  26.7 0.8 %collective-permute-start.7 = (f32[256,128]{1,0:T(8,128)S(1)}, f32[256,128]{1,0:T(8,128)S(1)}, u32[]{:S(2)}, u32[]{:S(2)}) collective-permute-start(f32[256,128]{1,0:T(8,128)S(1)} %get-tuple-element.79), channel_id=1, source_target_pairs={{0,4},{1,5},{2,6},{3,7},{4,0},{5,1},{6,2},{7,3},{8,12},{9,13},{10,... | collective-permute-start | bytes 393224 | tf_op jit(solution)/shard_map/ppermute | solution.py:260
  28.2 1.6 %collective-permute-done.6 = f32[256,128]{1,0:T(8,128)S(1)} collective-permute-done((f32[256,128]{1,0:T(8,128)S(1)}, f32[256,128]{1,0:T(8,128)S(1)}, u32[]{:S(2)}, u32[]{:S(2)}) %collective-permute-start.6) | collective-permute-done | bytes 131104 | tf_op jit(solution)/shard_map/ppermute | solution.py:260
  29.8 1.1 %collective-permute-done.7 = f32[256,128]{1,0:T(8,128)S(1)} collective-permute-done((f32[256,128]{1,0:T(8,128)S(1)}, f32[256,128]{1,0:T(8,128)S(1)}, u32[]{:S(2)}, u32[]{:S(2)}) %collective-permute-start.7) | collective-permute-done | bytes 131104 | tf_op jit(solution)/shard_map/ppermute | solution.py:260
  30.9 3.1 %collective-permute-done.8 = f32[256,128]{1,0:T(8,128)S(1)} collective-permute-done((f32[256,128]{1,0:T(8,128)S(1)}, f32[256,128]{1,0:T(8,128)S(1)}, u32[]{:S(2)}, u32[]{:S(2)}) %collective-permute-start.8) | collective-permute-done | bytes 131104 | tf_op jit(solution)/shard_map/ppermute | solution.py:260
  34.1 2.3 %shard_map.97 = (bf16[256,1024]{1,0:T(8,128)(2,1)S(1)}, f32[256,1024]{1,0:T(8,128)S(1)}, f32[1024,128]{1,0:T(8,128)S(1)}, f32[1024,128]{1,0:T(8,128)S(1)}, f32[8,128]{1,0:T(8,128)S(1)}) custom-call(bf16[256,1024]{1,0:T(8,128)(2,1)S(1)} %get-tuple-element.72.q_ref, bf16[256,1024]{1,0:T(8,128)(2,1)S(1)} %get-tuple-element.73.g_ref, ...), custom_call_target="tpu_custom_call" | custom-call | tf_op jit(solution)/shard_map/pallas_call | solution.py:465
  36.5 0.7 %collective-permute-start.11 = (f32[272,128]{1,0:T(8,128)S(1)}, f32[272,128]{1,0:T(8,128)S(1)}, u32[]{:S(2)}, u32[]{:S(2)}) collective-permute-start(f32[272,128]{1,0:T(8,128)S(1)} %get-tuple-element.91), channel_id=1, source_target_pairs={{0,4},{1,5},{2,6},{3,7},{4,0},{5,1},{6,2},{7,3},{8,12},{9,13},{10,... | collective-permute-start | bytes 417800 | tf_op jit(solution)/shard_map/ppermute | solution.py:260
  37.2 1.0 %collective-permute-start.12 = (f32[272,128]{1,0:T(8,128)S(1)}, f32[272,128]{1,0:T(8,128)S(1)}, u32[]{:S(2)}, u32[]{:S(2)}) collective-permute-start(f32[272,128]{1,0:T(8,128)S(1)} %get-tuple-element.87.rest_0_), channel_id=1, source_target_pairs={{0,6},{1,7},{2,4},{3,5},{4,2},{5,3},{6,0},{7,1},{8,14},{9,15},{10,... | collective-permute-start | bytes 417800 | tf_op jit(solution)/shard_map/ppermute | solution.py:260
  38.2 1.0 %collective-permute-start.13 = (f32[272,128]{1,0:T(8,128)S(1)}, f32[272,128]{1,0:T(8,128)S(1)}, u32[]{:S(2)}, u32[]{:S(2)}) collective-permute-start(f32[272,128]{1,0:T(8,128)S(1)} %get-tuple-element.92), channel_id=1, source_target_pairs={{0,2},{1,3},{2,0},{3,1},{4,6},{5,7},{6,4},{7,5},{8,10},{9,11},{10,... | collective-permute-start | bytes 417800 | tf_op jit(solution)/shard_map/ppermute | solution.py:260
  39.2 3.1 %shard_map.98 = (bf16[256,2048]{1,0:T(8,128)(2,1)}, f32[256,1024]{1,0:T(8,128)S(1)}, f32[256,1024]{1,0:T(8,128)S(1)}) custom-call(bf16[256,1024]{1,0:T(8,128)(2,1)S(1)} %get-tuple-element.72.q_ref, bf16[256,1024]{1,0:T(8,128)(2,1)S(1)} %get-tuple-element.67.k_ref, bf16[256,1024]{1,0:T(8,128)(2,1)S(1)} %get-tuple-element.68.v_ref, ...), custom_call_target="tpu_custom_call" | custom-call | tf_op jit(solution)/shard_map/pallas_call | solution.py:420
  42.3 2.5 %collective-permute-start.9 = (f32[256,1024]{1,0:T(8,128)S(1)}, f32[256,1024]{1,0:T(8,128)S(1)}, u32[]{:S(2)}, u32[]{:S(2)}) collective-permute-start(f32[256,1024]{1,0:T(8,128)S(1)} %get-tuple-element.89), channel_id=1, source_target_pairs={{0,1},{1,0},{2,3},{3,2},{4,5},{5,4},{6,7},{7,6},{8,9},{9,8},{10,11... | collective-permute-start | bytes 3145736 | tf_op jit(solution)/shard_map/ppermute | solution.py:260
  44.9 4.5 %collective-permute-start.14 = (f32[272,128]{1,0:T(8,128)S(1)}, f32[272,128]{1,0:T(8,128)S(1)}, u32[]{:S(2)}, u32[]{:S(2)}) collective-permute-start(f32[272,128]{1,0:T(8,128)S(1)} %pad_maximum_fusion.11), channel_id=1, source_target_pairs={{0,8},{1,9},{2,10},{3,11},{4,12},{5,13},{6,14},{7,15},{8,0},{9,1},... | collective-permute-start | bytes 417800 | tf_op jit(solution)/shard_map/ppermute | solution.py:260
  49.4 1.8 %collective-permute-start.10 = (f32[1024,128]{1,0:T(8,128)S(1)}, f32[1024,128]{1,0:T(8,128)S(1)}, u32[]{:S(2)}, u32[]{:S(2)}) collective-permute-start(f32[1024,128]{1,0:T(8,128)S(1)} %get-tuple-element.90.theirs_ref), channel_id=1, source_target_pairs={{0,1},{1,0},{2,3},{3,2},{4,5},{5,4},{6,7},{7,6},{8,9},{9,8},{10,11... | collective-permute-start | bytes 1572872 | tf_op jit(solution)/shard_map/ppermute | solution.py:260
  51.2 4.6 %collective-permute-done.14 = f32[272,128]{1,0:T(8,128)S(1)} collective-permute-done((f32[272,128]{1,0:T(8,128)S(1)}, f32[272,128]{1,0:T(8,128)S(1)}, u32[]{:S(2)}, u32[]{:S(2)}) %collective-permute-start.14) | collective-permute-done | bytes 139296 | tf_op jit(solution)/shard_map/ppermute | solution.py:260
  56.6 2.0 %collective-permute-start.17 = (f32[256,128]{1,0:T(8,128)S(1)}, f32[256,128]{1,0:T(8,128)S(1)}, u32[]{:S(2)}, u32[]{:S(2)}) collective-permute-start(f32[256,128]{1,0:T(8,128)S(1)} %get-tuple-element.94.rest_0_), channel_id=1, source_target_pairs={{0,6},{1,7},{2,4},{3,5},{4,2},{5,3},{6,0},{7,1},{8,14},{9,15},{10,... | collective-permute-start | bytes 393224 | tf_op jit(solution)/shard_map/ppermute | solution.py:260
  58.6 3.1 %shard_map.99 = (bf16[256,2048]{1,0:T(8,128)(2,1)}, f32[256,1024]{1,0:T(8,128)S(1)}, f32[256,1024]{1,0:T(8,128)S(1)}) custom-call(bf16[256,1024]{1,0:T(8,128)(2,1)S(1)} %get-tuple-element.66.q_ref, bf16[256,1024]{1,0:T(8,128)(2,1)S(1)} %get-tuple-element.56.k_ref, bf16[256,1024]{1,0:T(8,128)(2,1)S(1)} %get-tuple-element.57.v_ref, ...), custom_call_target="tpu_custom_call", output_to_operand_aliasing={{0}: (9, {})} | custom-call | tf_op jit(solution)/shard_map/pallas_call | solution.py:420
  61.6 2.2 %collective-permute-start.18 = (f32[8,128]{1,0:T(8,128)S(1)}, f32[8,128]{1,0:T(8,128)S(1)}, u32[]{:S(2)}, u32[]{:S(2)}) collective-permute-start(f32[8,128]{1,0:T(8,128)S(1)} %slice_add_fusion), channel_id=1, source_target_pairs={{0,1},{1,0},{2,3},{3,2},{4,5},{5,4},{6,7},{7,6},{8,9},{9,8},{10,11... | collective-permute-start | bytes 12296 | tf_op jit(solution)/shard_map/ppermute | solution.py:260
  64.0 0.7 %collective-permute-done.18 = f32[8,128]{1,0:T(8,128)S(1)} collective-permute-done((f32[8,128]{1,0:T(8,128)S(1)}, f32[8,128]{1,0:T(8,128)S(1)}, u32[]{:S(2)}, u32[]{:S(2)}) %collective-permute-start.18) | collective-permute-done | bytes 4128 | tf_op jit(solution)/shard_map/ppermute | solution.py:260
  64.7 1.3 %collective-permute-start.19 = (f32[1024,128]{1,0:T(8,128)S(1)}, f32[1024,128]{1,0:T(8,128)S(1)}, u32[]{:S(2)}, u32[]{:S(2)}) collective-permute-start(f32[1024,128]{1,0:T(8,128)S(1)} %get-tuple-element.102), channel_id=1, source_target_pairs={{0,1},{1,0},{2,3},{3,2},{4,5},{5,4},{6,7},{7,6},{8,9},{9,8},{10,11... | collective-permute-start | bytes 1572872 | tf_op jit(solution)/shard_map/ppermute | solution.py:260
  66.6 1.3 %shard_map.100 = (bf16[256,2048]{1,0:T(8,128)(2,1)}, bf16[256,2048]{1,0:T(8,128)(2,1)}) custom-call(bf16[256,1024]{1,0:T(8,128)(2,1)S(1)} %get-tuple-element.67.k_ref, bf16[256,1024]{1,0:T(8,128)(2,1)S(1)} %get-tuple-element.68.v_ref, f32[256,1024]{1,0:T(8,128)S(1)} %get-tuple-element.88.kp_ref, f32[256,1024]{1,0:T(8,128)S(1)} %get-tuple-element.103.vp_ref, ...), custom_call_target="tpu_custom_call" | custom-call | tf_op jit(solution)/shard_map/pallas_call | solution.py:448
  68.0 1.3 %shard_map.101 = (bf16[256,2048]{1,0:T(8,128)(2,1)}, bf16[256,2048]{1,0:T(8,128)(2,1)}) custom-call(bf16[256,1024]{1,0:T(8,128)(2,1)S(1)} %get-tuple-element.56.k_ref, bf16[256,1024]{1,0:T(8,128)(2,1)S(1)} %get-tuple-element.57.v_ref, f32[256,1024]{1,0:T(8,128)S(1)} %get-tuple-element.97.kp_ref, ...), custom_call_target="tpu_custom_call", output_to_operand_aliasing={{0}: (6, {}), {1}: (7, {})} | custom-call | tf_op jit(solution)/shard_map/pallas_call | solution.py:448
  (48 shorter events, 3.2 us)
Async XLA Ops:
  2.4 2.0 %collective-permute-start = (f32[1032,128]{1,0:T(8,128)S(1)}, f32[1032,128]{1,0:T(8,128)S(1)}, u32[]{:S(2)}, u32[]{:S(2)}) collective-permute-start(f32[1032,128]{1,0:T(8,128)S(1)} %get-tuple-element.63), channel_id=1, source_target_pairs={{0,1},{1,0},{2,3},{3,2},{4,5},{5,4},{6,7},{7,6},{8,9},{9,8},{10,11... | collective-permute-start | bytes 1585160 | tf_op jit(solution)/shard_map/ppermute | solution.py:260
  4.6 6.7 %collective-permute-start.1 = (f32[264,128]{1,0:T(8,128)S(1)}, f32[264,128]{1,0:T(8,128)S(1)}, u32[]{:S(2)}, u32[]{:S(2)}) collective-permute-start(f32[264,128]{1,0:T(8,128)S(1)} %get-tuple-element.69), channel_id=1, source_target_pairs={{0,2},{1,3},{2,0},{3,1},{4,6},{5,7},{6,4},{7,5},{8,10},{9,11},{10,... | collective-permute-start | bytes 405512 | tf_op jit(solution)/shard_map/ppermute | solution.py:260
  7.3 4.8 %collective-permute-start.2 = (f32[264,128]{1,0:T(8,128)S(1)}, f32[264,128]{1,0:T(8,128)S(1)}, u32[]{:S(2)}, u32[]{:S(2)}) collective-permute-start(f32[264,128]{1,0:T(8,128)S(1)} %get-tuple-element.70), channel_id=1, source_target_pairs={{0,4},{1,5},{2,6},{3,7},{4,0},{5,1},{6,2},{7,3},{8,12},{9,13},{10,... | collective-permute-start | bytes 405512 | tf_op jit(solution)/shard_map/ppermute | solution.py:260
  8.6 6.3 %collective-permute-start.3 = (f32[264,128]{1,0:T(8,128)S(1)}, f32[264,128]{1,0:T(8,128)S(1)}, u32[]{:S(2)}, u32[]{:S(2)}) collective-permute-start(f32[264,128]{1,0:T(8,128)S(1)} %get-tuple-element.65._), channel_id=1, source_target_pairs={{0,6},{1,7},{2,4},{3,5},{4,2},{5,3},{6,0},{7,1},{8,14},{9,15},{10,... | collective-permute-start | bytes 405512 | tf_op jit(solution)/shard_map/ppermute | solution.py:260
  15.0 10.4 %collective-permute-start.4 = (f32[768,1024]{1,0:T(8,128)S(1)}, f32[768,1024]{1,0:T(8,128)S(1)}, u32[]{:S(2)}, u32[]{:S(2)}) collective-permute-start(f32[768,1024]{1,0:T(8,128)S(1)} %get-tuple-element.77), channel_id=1, source_target_pairs={{0,1},{1,0},{2,3},{3,2},{4,5},{5,4},{6,7},{7,6},{8,9},{9,8},{10,11... | collective-permute-start | bytes 9437192 | tf_op jit(solution)/shard_map/ppermute | solution.py:260
  16.2 9.1 %collective-permute-start.5 = (f32[264,128]{1,0:T(8,128)S(1)}, f32[264,128]{1,0:T(8,128)S(1)}, u32[]{:S(2)}, u32[]{:S(2)}) collective-permute-start(f32[264,128]{1,0:T(8,128)S(1)} %pad_maximum_fusion.12._), channel_id=1, source_target_pairs={{0,8},{1,9},{2,10},{3,11},{4,12},{5,13},{6,14},{7,15},{8,0},{9,1},... | collective-permute-start | bytes 405512 | tf_op jit(solution)/shard_map/ppermute | solution.py:260
  25.5 4.3 %collective-permute-start.6 = (f32[256,128]{1,0:T(8,128)S(1)}, f32[256,128]{1,0:T(8,128)S(1)}, u32[]{:S(2)}, u32[]{:S(2)}) collective-permute-start(f32[256,128]{1,0:T(8,128)S(1)} %get-tuple-element.78), channel_id=1, source_target_pairs={{0,2},{1,3},{2,0},{3,1},{4,6},{5,7},{6,4},{7,5},{8,10},{9,11},{10,... | collective-permute-start | bytes 393224 | tf_op jit(solution)/shard_map/ppermute | solution.py:260
  26.7 4.1 %collective-permute-start.7 = (f32[256,128]{1,0:T(8,128)S(1)}, f32[256,128]{1,0:T(8,128)S(1)}, u32[]{:S(2)}, u32[]{:S(2)}) collective-permute-start(f32[256,128]{1,0:T(8,128)S(1)} %get-tuple-element.79), channel_id=1, source_target_pairs={{0,4},{1,5},{2,6},{3,7},{4,0},{5,1},{6,2},{7,3},{8,12},{9,13},{10,... | collective-permute-start | bytes 393224 | tf_op jit(solution)/shard_map/ppermute | solution.py:260
  27.5 6.4 %collective-permute-start.8 = (f32[256,128]{1,0:T(8,128)S(1)}, f32[256,128]{1,0:T(8,128)S(1)}, u32[]{:S(2)}, u32[]{:S(2)}) collective-permute-start(f32[256,128]{1,0:T(8,128)S(1)} %get-tuple-element.80), channel_id=1, source_target_pairs={{0,6},{1,7},{2,4},{3,5},{4,2},{5,3},{6,0},{7,1},{8,14},{9,15},{10,... | collective-permute-start | bytes 393224 | tf_op jit(solution)/shard_map/ppermute | solution.py:260
  36.5 8.3 %collective-permute-start.11 = (f32[272,128]{1,0:T(8,128)S(1)}, f32[272,128]{1,0:T(8,128)S(1)}, u32[]{:S(2)}, u32[]{:S(2)}) collective-permute-start(f32[272,128]{1,0:T(8,128)S(1)} %get-tuple-element.91), channel_id=1, source_target_pairs={{0,4},{1,5},{2,6},{3,7},{4,0},{5,1},{6,2},{7,3},{8,12},{9,13},{10,... | collective-permute-start | bytes 417800 | tf_op jit(solution)/shard_map/ppermute | solution.py:260
  37.2 7.5 %collective-permute-start.12 = (f32[272,128]{1,0:T(8,128)S(1)}, f32[272,128]{1,0:T(8,128)S(1)}, u32[]{:S(2)}, u32[]{:S(2)}) collective-permute-start(f32[272,128]{1,0:T(8,128)S(1)} %get-tuple-element.87.rest_0_), channel_id=1, source_target_pairs={{0,6},{1,7},{2,4},{3,5},{4,2},{5,3},{6,0},{7,1},{8,14},{9,15},{10,... | collective-permute-start | bytes 417800 | tf_op jit(solution)/shard_map/ppermute | solution.py:260
  38.2 6.6 %collective-permute-start.13 = (f32[272,128]{1,0:T(8,128)S(1)}, f32[272,128]{1,0:T(8,128)S(1)}, u32[]{:S(2)}, u32[]{:S(2)}) collective-permute-start(f32[272,128]{1,0:T(8,128)S(1)} %get-tuple-element.92), channel_id=1, source_target_pairs={{0,2},{1,3},{2,0},{3,1},{4,6},{5,7},{6,4},{7,5},{8,10},{9,11},{10,... | collective-permute-start | bytes 417800 | tf_op jit(solution)/shard_map/ppermute | solution.py:260
  42.3 13.6 %collective-permute-start.9 = (f32[256,1024]{1,0:T(8,128)S(1)}, f32[256,1024]{1,0:T(8,128)S(1)}, u32[]{:S(2)}, u32[]{:S(2)}) collective-permute-start(f32[256,1024]{1,0:T(8,128)S(1)} %get-tuple-element.89), channel_id=1, source_target_pairs={{0,1},{1,0},{2,3},{3,2},{4,5},{5,4},{6,7},{7,6},{8,9},{9,8},{10,11... | collective-permute-start | bytes 3145736 | tf_op jit(solution)/shard_map/ppermute | solution.py:260
  44.9 10.8 %collective-permute-start.14 = (f32[272,128]{1,0:T(8,128)S(1)}, f32[272,128]{1,0:T(8,128)S(1)}, u32[]{:S(2)}, u32[]{:S(2)}) collective-permute-start(f32[272,128]{1,0:T(8,128)S(1)} %pad_maximum_fusion.11), channel_id=1, source_target_pairs={{0,8},{1,9},{2,10},{3,11},{4,12},{5,13},{6,14},{7,15},{8,0},{9,1},... | collective-permute-start | bytes 417800 | tf_op jit(solution)/shard_map/ppermute | solution.py:260
  49.4 6.4 %collective-permute-start.10 = (f32[1024,128]{1,0:T(8,128)S(1)}, f32[1024,128]{1,0:T(8,128)S(1)}, u32[]{:S(2)}, u32[]{:S(2)}) collective-permute-start(f32[1024,128]{1,0:T(8,128)S(1)} %get-tuple-element.90.theirs_ref), channel_id=1, source_target_pairs={{0,1},{1,0},{2,3},{3,2},{4,5},{5,4},{6,7},{7,6},{8,9},{9,8},{10,11... | collective-permute-start | bytes 1572872 | tf_op jit(solution)/shard_map/ppermute | solution.py:260
  55.9 8.0 %collective-permute-start.15 = (f32[256,128]{1,0:T(8,128)S(1)}, f32[256,128]{1,0:T(8,128)S(1)}, u32[]{:S(2)}, u32[]{:S(2)}) collective-permute-start(f32[256,128]{1,0:T(8,128)S(1)} %get-tuple-element.99), channel_id=1, source_target_pairs={{0,2},{1,3},{2,0},{3,1},{4,6},{5,7},{6,4},{7,5},{8,10},{9,11},{10,... | collective-permute-start | bytes 393224 | tf_op jit(solution)/shard_map/ppermute | solution.py:260
  55.9 7.9 %collective-permute-start.16 = (f32[256,128]{1,0:T(8,128)S(1)}, f32[256,128]{1,0:T(8,128)S(1)}, u32[]{:S(2)}, u32[]{:S(2)}) collective-permute-start(f32[256,128]{1,0:T(8,128)S(1)} %get-tuple-element.100), channel_id=1, source_target_pairs={{0,4},{1,5},{2,6},{3,7},{4,0},{5,1},{6,2},{7,3},{8,12},{9,13},{10,... | collective-permute-start | bytes 393224 | tf_op jit(solution)/shard_map/ppermute | solution.py:260
  56.6 7.3 %collective-permute-start.17 = (f32[256,128]{1,0:T(8,128)S(1)}, f32[256,128]{1,0:T(8,128)S(1)}, u32[]{:S(2)}, u32[]{:S(2)}) collective-permute-start(f32[256,128]{1,0:T(8,128)S(1)} %get-tuple-element.94.rest_0_), channel_id=1, source_target_pairs={{0,6},{1,7},{2,4},{3,5},{4,2},{5,3},{6,0},{7,1},{8,14},{9,15},{10,... | collective-permute-start | bytes 393224 | tf_op jit(solution)/shard_map/ppermute | solution.py:260
  61.6 3.0 %collective-permute-start.18 = (f32[8,128]{1,0:T(8,128)S(1)}, f32[8,128]{1,0:T(8,128)S(1)}, u32[]{:S(2)}, u32[]{:S(2)}) collective-permute-start(f32[8,128]{1,0:T(8,128)S(1)} %slice_add_fusion), channel_id=1, source_target_pairs={{0,1},{1,0},{2,3},{3,2},{4,5},{5,4},{6,7},{7,6},{8,9},{9,8},{10,11... | collective-permute-start | bytes 12296 | tf_op jit(solution)/shard_map/ppermute | solution.py:260
  64.7 3.3 %collective-permute-start.19 = (f32[1024,128]{1,0:T(8,128)S(1)}, f32[1024,128]{1,0:T(8,128)S(1)}, u32[]{:S(2)}, u32[]{:S(2)}) collective-permute-start(f32[1024,128]{1,0:T(8,128)S(1)} %get-tuple-element.102), channel_id=1, source_target_pairs={{0,1},{1,0},{2,3},{3,2},{4,5},{5,4},{6,7},{7,6},{8,9},{9,8},{10,11... | collective-permute-start | bytes 1572872 | tf_op jit(solution)/shard_map/ppermute | solution.py:260

commit v7 on v6

--- a/solution.py
+++ b/solution.py
@@ -404,6 +404,10 @@
         middle[:] = [pack]
         return other_query
 
+    def exchange(block):
+        local[1] = swap(lax.optimization_barrier((middle[0], block))[0], 1)
+        return ()
+
     def local_of(token):
         local[0], query[0], *rest = call(
             local_kernel,
@@ -412,8 +416,7 @@
             [copies(pairs, 1), copies(pairs, 1), copies()],
         )(queries, out_grad, gains, keys[0], values[0], start, token)
         norm_inputs[:] = rest
-        local[1] = swap(lax.optimization_barrier((middle[0], token))[0], 1)
-        return local[0], local[1]
+        return local[0]
 
     def spread_of(other, token):
         done = spread[0][:1] if other else []
@@ -480,6 +483,7 @@
     work = {
         1: other_local_of,
         1 + doubling: local_of,
+        2 + doubling: exchange,
         back: first_spread_of,
         back + doubling: lambda _: (d_att[1], carried[1]),
         back + doubling + 1: last_spread_of,

time: 69.7 us -> 69.3 us (level)
  starting transfers between devices: 28.1 us -> 26.1 us
  waiting for transfers between devices: 19.1 us -> 20.7 us
    ppermute x20, starting transfers between devices: 28.1 us -> 26.1 us  [swap(): return lax.ppermute(block, 'ctx', [(i, i ^ distance) for i in range(count)])]
    ppermute x20, waiting for transfers between devices: 19.1 us -> 20.7 us  [swap(): return lax.ppermute(block, 'ctx', [(i, i ^ distance) for i in range(count)])]
  transfers between devices with their start and end apart: 20 -> 20, of which waited for: 9 -> 10; matrix products, arithmetic and copies ran while one was open for 2% -> 2% of each run, Pallas kernels for 21% -> 21%
where the time goes in v7:
time: 69.3 us; the launch traced here: 68.9 us
  starting transfers between devices  26.1 us (38%)
  waiting for transfers between devices  20.7 us (30%)
  Pallas kernels  19.6 us (28%)
  other arithmetic  0.96 us (1%)
  between operations  0.89 us (1%)
    ppermute x20, starting transfers between devices, swap(): return lax.ppermute(block, 'ctx', [(i, i ^ distance) for i in range(count)])  26.1 us
    ppermute x20, waiting for transfers between devices, swap(): return lax.ppermute(block, 'ctx', [(i, i ^ distance) for i in range(count)])  20.7 us
    pallas_call x2, Pallas kernels, spread_of(): call(spread_kernel, [VMEM] * 8 + [ANY] * (1 + len(done)), [grad, single,...  6.13 us
    pallas_call x2, Pallas kernels, final_of(): call(final_kernel, [VMEM] * 6 + [ANY] * len(grads), [grad, grad], [stagin...  2.66 us
    pallas_call x1, Pallas kernels, other_local_of(): call(other_local_kernel, [ANY] * 2 + [VMEM] * 4 + [ANY], [held(3 * tokens...  2.66 us
    pallas_call x1, Pallas kernels, local_of(): call(local_kernel, [ANY] * 3 + [VMEM] * 3 + [ANY], [single, narrow, narro...  2.36 us
    pallas_call x1, Pallas kernels, chain(): call(middle_kernel, [VMEM] * 8, [narrow, single, held(rows, E), held(rows...  2.28 us
    pallas_call x1, Pallas kernels, shards(): call(send_state_kernel, [ANY] * 3, [held(rows + FLAG, E), narrow, narrow,...  1.79 us
  transfers between devices with their start and end apart: 20, of which 10 were waited for; matrix products, arithmetic and copies ran while one was open for 2% of the time, Pallas kernels for 21%

profile of v7, /device:TPU:1, one launch (start us, length us, event | category | flops | bytes accessed | tf_op | source)
XLA Modules:
  0.0 68.9 jit_solution(16199890826481264852)
XLA Ops:
  0.6 1.8 %shard_map.93 = (f32[1032,128]{1,0:T(8,128)S(1)}, bf16[256,1024]{1,0:T(8,128)(2,1)S(1)}, bf16[256,1024]{1,0:T(8,128)(2,1)S(1)}, s32[256,128]{1,0:T(8,128)S(1)}, ...) custom-call(s32[2,2]{1,0:T(2,128)} %bounds_hbm.1, ...), custom_call_target="tpu_custom_call" | custom-call | tf_op jit(solution)/shard_map/pallas_call | solution.py:382
  2.6 1.8 %shard_map.94 = (f32[1024,128]{1,0:T(8,128)S(1)}, bf16[256,1024]{1,0:T(8,128)(2,1)S(1)}, bf16[256,1024]{1,0:T(8,128)(2,1)S(1)}) custom-call(bf16[256,2048]{1,0:T(8,128)(2,1)} %k_hbm.3, bf16[256,2048]{1,0:T(8,128)(2,1)} %v_hbm.3, bf16[256,128]{1,0:T(8,128)(2,1)S(1)} %get-tuple-element.61.tail_ref), custom_call_target="tpu_custom_call" | custom-call | tf_op jit(solution)/shard_map/pallas_call | solution.py:389
  4.6 2.7 %collective-permute-start.1 = (f32[264,128]{1,0:T(8,128)S(1)}, f32[264,128]{1,0:T(8,128)S(1)}, u32[]{:S(2)}, u32[]{:S(2)}) collective-permute-start(f32[264,128]{1,0:T(8,128)S(1)} %get-tuple-element.69), channel_id=1, source_target_pairs={{0,2},{1,3},{2,0},{3,1},{4,6},{5,7},{6,4},{7,5},{8,10},{9,11},{10,... | collective-permute-start | bytes 405512 | tf_op jit(solution)/shard_map/ppermute | solution.py:260
  7.3 1.3 %collective-permute-start.2 = (f32[264,128]{1,0:T(8,128)S(1)}, f32[264,128]{1,0:T(8,128)S(1)}, u32[]{:S(2)}, u32[]{:S(2)}) collective-permute-start(f32[264,128]{1,0:T(8,128)S(1)} %get-tuple-element.70), channel_id=1, source_target_pairs={{0,4},{1,5},{2,6},{3,7},{4,0},{5,1},{6,2},{7,3},{8,12},{9,13},{10,... | collective-permute-start | bytes 405512 | tf_op jit(solution)/shard_map/ppermute | solution.py:260
  8.6 2.7 %shard_map.95 = (f32[768,1024]{1,0:T(8,128)S(1)}, bf16[256,1024]{1,0:T(8,128)(2,1)S(1)}) custom-call(bf16[256,2048]{1,0:T(8,128)(2,1)} %q_hbm.3, bf16[256,2048]{1,0:T(8,128)(2,1)} %g_hbm.3, bf16[256,1024]{1,0:T(8,128)(2,1)S(1)} %get-tuple-element.56.k_ref, bf16[256,1024]{1,0:T(8,128)(2,1)S(1)} %get-tuple-element.57.v_ref, ...), custom_call_target="tpu_custom_call" | custom-call | tf_op jit(solution)/shard_map/pallas_call | solution.py:397
  11.3 0.8 %collective-permute-done.2 = f32[264,128]{1,0:T(8,128)S(1)} collective-permute-done((f32[264,128]{1,0:T(8,128)S(1)}, f32[264,128]{1,0:T(8,128)S(1)}, u32[]{:S(2)}, u32[]{:S(2)}) %collective-permute-start.2) | collective-permute-done | bytes 135200 | tf_op jit(solution)/shard_map/ppermute | solution.py:260
  12.1 2.8 %collective-permute-done.3 = f32[264,128]{1,0:T(8,128)S(1)} collective-permute-done((f32[264,128]{1,0:T(8,128)S(1)}, f32[264,128]{1,0:T(8,128)S(1)}, u32[]{:S(2)}, u32[]{:S(2)}) %collective-permute-start.3) | collective-permute-done | bytes 135200 | tf_op jit(solution)/shard_map/ppermute | solution.py:260
  15.0 2.6 %collective-permute-start.4 = (f32[264,128]{1,0:T(8,128)S(1)}, f32[264,128]{1,0:T(8,128)S(1)}, u32[]{:S(2)}, u32[]{:S(2)}) collective-permute-start(f32[264,128]{1,0:T(8,128)S(1)} %pad_maximum_fusion.12._), channel_id=1, source_target_pairs={{0,8},{1,9},{2,10},{3,11},{4,12},{5,13},{6,14},{7,15},{8,0},{9,1},... | collective-permute-start | bytes 405512 | tf_op jit(solution)/shard_map/ppermute | solution.py:260
  17.7 2.4 %shard_map.96 = (f32[256,1024]{1,0:T(8,128)S(1)}, bf16[256,1024]{1,0:T(8,128)(2,1)S(1)}, bf16[256,1024]{1,0:T(8,128)(2,1)S(1)}, f32[1,2048]{1,0:T(1,128)S(1)}) custom-call(bf16[256,2048]{1,0:T(8,128)(2,1)} %q_hbm.3, bf16[256,2048]{1,0:T(8,128)(2,1)} %g_hbm.3, f32[1,2048]{1,0:T(1,128)} %bitcast.60, bf16[256,1024]{1,0:T(8,128)(2,1)S(1)} %get-tuple-element.67.k_ref, ...), custom_call_target="tpu_custom_call" | custom-call | tf_op jit(solution)/shard_map/pallas_call | solution.py:412
  20.0 3.7 %collective-permute-done.4 = f32[264,128]{1,0:T(8,128)S(1)} collective-permute-done((f32[264,128]{1,0:T(8,128)S(1)}, f32[264,128]{1,0:T(8,128)S(1)}, u32[]{:S(2)}, u32[]{:S(2)}) %collective-permute-start.4) | collective-permute-done | bytes 135200 | tf_op jit(solution)/shard_map/ppermute | solution.py:260
  23.8 1.5 %collective-permute-start.5 = (f32[768,1024]{1,0:T(8,128)S(1)}, f32[768,1024]{1,0:T(8,128)S(1)}, u32[]{:S(2)}, u32[]{:S(2)}) collective-permute-start(f32[768,1024]{1,0:T(8,128)S(1)} %get-tuple-element.78), channel_id=1, source_target_pairs={{0,1},{1,0},{2,3},{3,2},{4,5},{5,4},{6,7},{7,6},{8,9},{9,8},{10,11... | collective-permute-start | bytes 9437192 | tf_op jit(solution)/shard_map/ppermute | solution.py:260
  25.3 1.1 %collective-permute-start.6 = (f32[256,128]{1,0:T(8,128)S(1)}, f32[256,128]{1,0:T(8,128)S(1)}, u32[]{:S(2)}, u32[]{:S(2)}) collective-permute-start(f32[256,128]{1,0:T(8,128)S(1)} %get-tuple-element.79), channel_id=1, source_target_pairs={{0,2},{1,3},{2,0},{3,1},{4,6},{5,7},{6,4},{7,5},{8,10},{9,11},{10,... | collective-permute-start | bytes 393224 | tf_op jit(solution)/shard_map/ppermute | solution.py:260
  26.8 1.2 %collective-permute-start.8 = (f32[256,128]{1,0:T(8,128)S(1)}, f32[256,128]{1,0:T(8,128)S(1)}, u32[]{:S(2)}, u32[]{:S(2)}) collective-permute-start(f32[256,128]{1,0:T(8,128)S(1)} %get-tuple-element.77), channel_id=1, source_target_pairs={{0,6},{1,7},{2,4},{3,5},{4,2},{5,3},{6,0},{7,1},{8,14},{9,15},{10,... | collective-permute-start | bytes 393224 | tf_op jit(solution)/shard_map/ppermute | solution.py:260
  28.0 2.4 %collective-permute-done.6 = f32[256,128]{1,0:T(8,128)S(1)} collective-permute-done((f32[256,128]{1,0:T(8,128)S(1)}, f32[256,128]{1,0:T(8,128)S(1)}, u32[]{:S(2)}, u32[]{:S(2)}) %collective-permute-start.6) | collective-permute-done | bytes 131104 | tf_op jit(solution)/shard_map/ppermute | solution.py:260
  30.4 0.8 %collective-permute-done.7 = f32[256,128]{1,0:T(8,128)S(1)} collective-permute-done((f32[256,128]{1,0:T(8,128)S(1)}, f32[256,128]{1,0:T(8,128)S(1)}, u32[]{:S(2)}, u32[]{:S(2)}) %collective-permute-start.7) | collective-permute-done | bytes 131104 | tf_op jit(solution)/shard_map/ppermute | solution.py:260
  31.1 2.9 %collective-permute-done.8 = f32[256,128]{1,0:T(8,128)S(1)} collective-permute-done((f32[256,128]{1,0:T(8,128)S(1)}, f32[256,128]{1,0:T(8,128)S(1)}, u32[]{:S(2)}, u32[]{:S(2)}) %collective-permute-start.8) | collective-permute-done | bytes 131104 | tf_op jit(solution)/shard_map/ppermute | solution.py:260
  34.2 2.3 %shard_map.97 = (bf16[256,1024]{1,0:T(8,128)(2,1)S(1)}, f32[256,1024]{1,0:T(8,128)S(1)}, f32[1024,128]{1,0:T(8,128)S(1)}, f32[1024,128]{1,0:T(8,128)S(1)}, f32[8,128]{1,0:T(8,128)S(1)}) custom-call(bf16[256,1024]{1,0:T(8,128)(2,1)S(1)} %get-tuple-element.72.q_ref, bf16[256,1024]{1,0:T(8,128)(2,1)S(1)} %get-tuple-element.73.g_ref, ...), custom_call_target="tpu_custom_call" | custom-call | tf_op jit(solution)/shard_map/pallas_call | solution.py:468
  37.0 1.9 %collective-permute-start.12 = (f32[272,128]{1,0:T(8,128)S(1)}, f32[272,128]{1,0:T(8,128)S(1)}, u32[]{:S(2)}, u32[]{:S(2)}) collective-permute-start(f32[272,128]{1,0:T(8,128)S(1)} %get-tuple-element.87.rest_0_), channel_id=1, source_target_pairs={{0,6},{1,7},{2,4},{3,5},{4,2},{5,3},{6,0},{7,1},{8,14},{9,15},{10,... | collective-permute-start | bytes 417800 | tf_op jit(solution)/shard_map/ppermute | solution.py:260
  39.3 3.1 %shard_map.98 = (bf16[256,2048]{1,0:T(8,128)(2,1)}, f32[256,1024]{1,0:T(8,128)S(1)}, f32[256,1024]{1,0:T(8,128)S(1)}) custom-call(bf16[256,1024]{1,0:T(8,128)(2,1)S(1)} %get-tuple-element.72.q_ref, bf16[256,1024]{1,0:T(8,128)(2,1)S(1)} %get-tuple-element.67.k_ref, bf16[256,1024]{1,0:T(8,128)(2,1)S(1)} %get-tuple-element.68.v_ref, ...), custom_call_target="tpu_custom_call" | custom-call | tf_op jit(solution)/shard_map/pallas_call | solution.py:423
  42.4 2.1 %collective-permute-start.9 = (f32[256,1024]{1,0:T(8,128)S(1)}, f32[256,1024]{1,0:T(8,128)S(1)}, u32[]{:S(2)}, u32[]{:S(2)}) collective-permute-start(f32[256,1024]{1,0:T(8,128)S(1)} %get-tuple-element.89), channel_id=1, source_target_pairs={{0,1},{1,0},{2,3},{3,2},{4,5},{5,4},{6,7},{7,6},{8,9},{9,8},{10,11... | collective-permute-start | bytes 3145736 | tf_op jit(solution)/shard_map/ppermute | solution.py:260
  44.5 2.0 %collective-permute-done.13 = f32[272,128]{1,0:T(8,128)S(1)} collective-permute-done((f32[272,128]{1,0:T(8,128)S(1)}, f32[272,128]{1,0:T(8,128)S(1)}, u32[]{:S(2)}, u32[]{:S(2)}) %collective-permute-start.13) | collective-permute-done | bytes 139296 | tf_op jit(solution)/shard_map/ppermute | solution.py:260
  46.7 2.4 %collective-permute-start.14 = (f32[272,128]{1,0:T(8,128)S(1)}, f32[272,128]{1,0:T(8,128)S(1)}, u32[]{:S(2)}, u32[]{:S(2)}) collective-permute-start(f32[272,128]{1,0:T(8,128)S(1)} %pad_maximum_fusion.11), channel_id=1, source_target_pairs={{0,8},{1,9},{2,10},{3,11},{4,12},{5,13},{6,14},{7,15},{8,0},{9,1},... | collective-permute-start | bytes 417800 | tf_op jit(solution)/shard_map/ppermute | solution.py:260
  49.1 1.8 %collective-permute-start.10 = (f32[1024,128]{1,0:T(8,128)S(1)}, f32[1024,128]{1,0:T(8,128)S(1)}, u32[]{:S(2)}, u32[]{:S(2)}) collective-permute-start(f32[1024,128]{1,0:T(8,128)S(1)} %get-tuple-element.90.theirs_ref), channel_id=1, source_target_pairs={{0,1},{1,0},{2,3},{3,2},{4,5},{5,4},{6,7},{7,6},{8,9},{9,8},{10,11... | collective-permute-start | bytes 1572872 | tf_op jit(solution)/shard_map/ppermute | solution.py:260
  50.8 4.5 %collective-permute-done.14 = f32[272,128]{1,0:T(8,128)S(1)} collective-permute-done((f32[272,128]{1,0:T(8,128)S(1)}, f32[272,128]{1,0:T(8,128)S(1)}, u32[]{:S(2)}, u32[]{:S(2)}) %collective-permute-start.14) | collective-permute-done | bytes 139296 | tf_op jit(solution)/shard_map/ppermute | solution.py:260
  56.5 1.7 %collective-permute-start.17 = (f32[256,128]{1,0:T(8,128)S(1)}, f32[256,128]{1,0:T(8,128)S(1)}, u32[]{:S(2)}, u32[]{:S(2)}) collective-permute-start(f32[256,128]{1,0:T(8,128)S(1)} %get-tuple-element.94.rest_0_), channel_id=1, source_target_pairs={{0,6},{1,7},{2,4},{3,5},{4,2},{5,3},{6,0},{7,1},{8,14},{9,15},{10,... | collective-permute-start | bytes 393224 | tf_op jit(solution)/shard_map/ppermute | solution.py:260
  58.2 3.1 %shard_map.99 = (bf16[256,2048]{1,0:T(8,128)(2,1)}, f32[256,1024]{1,0:T(8,128)S(1)}, f32[256,1024]{1,0:T(8,128)S(1)}) custom-call(bf16[256,1024]{1,0:T(8,128)(2,1)S(1)} %get-tuple-element.66.q_ref, bf16[256,1024]{1,0:T(8,128)(2,1)S(1)} %get-tuple-element.56.k_ref, bf16[256,1024]{1,0:T(8,128)(2,1)S(1)} %get-tuple-element.57.v_ref, ...), custom_call_target="tpu_custom_call", output_to_operand_aliasing={{0}: (9, {})} | custom-call | tf_op jit(solution)/shard_map/pallas_call | solution.py:423
  61.2 2.3 %collective-permute-start.18 = (f32[8,128]{1,0:T(8,128)S(1)}, f32[8,128]{1,0:T(8,128)S(1)}, u32[]{:S(2)}, u32[]{:S(2)}) collective-permute-start(f32[8,128]{1,0:T(8,128)S(1)} %slice_add_fusion), channel_id=1, source_target_pairs={{0,1},{1,0},{2,3},{3,2},{4,5},{5,4},{6,7},{7,6},{8,9},{9,8},{10,11... | collective-permute-start | bytes 12296 | tf_op jit(solution)/shard_map/ppermute | solution.py:260
  63.7 0.7 %collective-permute-done.18 = f32[8,128]{1,0:T(8,128)S(1)} collective-permute-done((f32[8,128]{1,0:T(8,128)S(1)}, f32[8,128]{1,0:T(8,128)S(1)}, u32[]{:S(2)}, u32[]{:S(2)}) %collective-permute-start.18) | collective-permute-done | bytes 4128 | tf_op jit(solution)/shard_map/ppermute | solution.py:260
  64.4 1.2 %collective-permute-start.19 = (f32[1024,128]{1,0:T(8,128)S(1)}, f32[1024,128]{1,0:T(8,128)S(1)}, u32[]{:S(2)}, u32[]{:S(2)}) collective-permute-start(f32[1024,128]{1,0:T(8,128)S(1)} %get-tuple-element.102), channel_id=1, source_target_pairs={{0,1},{1,0},{2,3},{3,2},{4,5},{5,4},{6,7},{7,6},{8,9},{9,8},{10,11... | collective-permute-start | bytes 1572872 | tf_op jit(solution)/shard_map/ppermute | solution.py:260
  65.6 0.6 copy.13
  66.2 1.3 %shard_map.100 = (bf16[256,2048]{1,0:T(8,128)(2,1)}, bf16[256,2048]{1,0:T(8,128)(2,1)}) custom-call(bf16[256,1024]{1,0:T(8,128)(2,1)S(1)} %get-tuple-element.67.k_ref, bf16[256,1024]{1,0:T(8,128)(2,1)S(1)} %get-tuple-element.68.v_ref, f32[256,1024]{1,0:T(8,128)S(1)} %get-tuple-element.88.kp_ref, f32[256,1024]{1,0:T(8,128)S(1)} %get-tuple-element.103.vp_ref, ...), custom_call_target="tpu_custom_call" | custom-call | tf_op jit(solution)/shard_map/pallas_call | solution.py:451
  67.6 1.3 %shard_map.101 = (bf16[256,2048]{1,0:T(8,128)(2,1)}, bf16[256,2048]{1,0:T(8,128)(2,1)}) custom-call(bf16[256,1024]{1,0:T(8,128)(2,1)S(1)} %get-tuple-element.56.k_ref, bf16[256,1024]{1,0:T(8,128)(2,1)S(1)} %get-tuple-element.57.v_ref, f32[256,1024]{1,0:T(8,128)S(1)} %get-tuple-element.97.kp_ref, ...), custom_call_target="tpu_custom_call", output_to_operand_aliasing={{0}: (6, {}), {1}: (7, {})} | custom-call | tf_op jit(solution)/shard_map/pallas_call | solution.py:451
  (48 shorter events, 3.4 us)
Async XLA Ops:
  2.4 2.0 %collective-permute-start = (f32[1032,128]{1,0:T(8,128)S(1)}, f32[1032,128]{1,0:T(8,128)S(1)}, u32[]{:S(2)}, u32[]{:S(2)}) collective-permute-start(f32[1032,128]{1,0:T(8,128)S(1)} %get-tuple-element.63), channel_id=1, source_target_pairs={{0,1},{1,0},{2,3},{3,2},{4,5},{5,4},{6,7},{7,6},{8,9},{9,8},{10,11... | collective-permute-start | bytes 1585160 | tf_op jit(solution)/shard_map/ppermute | solution.py:260
  4.6 6.7 %collective-permute-start.1 = (f32[264,128]{1,0:T(8,128)S(1)}, f32[264,128]{1,0:T(8,128)S(1)}, u32[]{:S(2)}, u32[]{:S(2)}) collective-permute-start(f32[264,128]{1,0:T(8,128)S(1)} %get-tuple-element.69), channel_id=1, source_target_pairs={{0,2},{1,3},{2,0},{3,1},{4,6},{5,7},{6,4},{7,5},{8,10},{9,11},{10,... | collective-permute-start | bytes 405512 | tf_op jit(solution)/shard_map/ppermute | solution.py:260
  7.3 4.8 %collective-permute-start.2 = (f32[264,128]{1,0:T(8,128)S(1)}, f32[264,128]{1,0:T(8,128)S(1)}, u32[]{:S(2)}, u32[]{:S(2)}) collective-permute-start(f32[264,128]{1,0:T(8,128)S(1)} %get-tuple-element.70), channel_id=1, source_target_pairs={{0,4},{1,5},{2,6},{3,7},{4,0},{5,1},{6,2},{7,3},{8,12},{9,13},{10,... | collective-permute-start | bytes 405512 | tf_op jit(solution)/shard_map/ppermute | solution.py:260
  8.6 6.3 %collective-permute-start.3 = (f32[264,128]{1,0:T(8,128)S(1)}, f32[264,128]{1,0:T(8,128)S(1)}, u32[]{:S(2)}, u32[]{:S(2)}) collective-permute-start(f32[264,128]{1,0:T(8,128)S(1)} %get-tuple-element.65._), channel_id=1, source_target_pairs={{0,6},{1,7},{2,4},{3,5},{4,2},{5,3},{6,0},{7,1},{8,14},{9,15},{10,... | collective-permute-start | bytes 405512 | tf_op jit(solution)/shard_map/ppermute | solution.py:260
  15.0 8.7 %collective-permute-start.4 = (f32[264,128]{1,0:T(8,128)S(1)}, f32[264,128]{1,0:T(8,128)S(1)}, u32[]{:S(2)}, u32[]{:S(2)}) collective-permute-start(f32[264,128]{1,0:T(8,128)S(1)} %pad_maximum_fusion.12._), channel_id=1, source_target_pairs={{0,8},{1,9},{2,10},{3,11},{4,12},{5,13},{6,14},{7,15},{8,0},{9,1},... | collective-permute-start | bytes 405512 | tf_op jit(solution)/shard_map/ppermute | solution.py:260
  23.8 10.3 %collective-permute-start.5 = (f32[768,1024]{1,0:T(8,128)S(1)}, f32[768,1024]{1,0:T(8,128)S(1)}, u32[]{:S(2)}, u32[]{:S(2)}) collective-permute-start(f32[768,1024]{1,0:T(8,128)S(1)} %get-tuple-element.78), channel_id=1, source_target_pairs={{0,1},{1,0},{2,3},{3,2},{4,5},{5,4},{6,7},{7,6},{8,9},{9,8},{10,11... | collective-permute-start | bytes 9437192 | tf_op jit(solution)/shard_map/ppermute | solution.py:260
  25.3 5.1 %collective-permute-start.6 = (f32[256,128]{1,0:T(8,128)S(1)}, f32[256,128]{1,0:T(8,128)S(1)}, u32[]{:S(2)}, u32[]{:S(2)}) collective-permute-start(f32[256,128]{1,0:T(8,128)S(1)} %get-tuple-element.79), channel_id=1, source_target_pairs={{0,2},{1,3},{2,0},{3,1},{4,6},{5,7},{6,4},{7,5},{8,10},{9,11},{10,... | collective-permute-start | bytes 393224 | tf_op jit(solution)/shard_map/ppermute | solution.py:260
  26.4 4.7 %collective-permute-start.7 = (f32[256,128]{1,0:T(8,128)S(1)}, f32[256,128]{1,0:T(8,128)S(1)}, u32[]{:S(2)}, u32[]{:S(2)}) collective-permute-start(f32[256,128]{1,0:T(8,128)S(1)} %get-tuple-element.80), channel_id=1, source_target_pairs={{0,4},{1,5},{2,6},{3,7},{4,0},{5,1},{6,2},{7,3},{8,12},{9,13},{10,... | collective-permute-start | bytes 393224 | tf_op jit(solution)/shard_map/ppermute | solution.py:260
  26.8 7.3 %collective-permute-start.8 = (f32[256,128]{1,0:T(8,128)S(1)}, f32[256,128]{1,0:T(8,128)S(1)}, u32[]{:S(2)}, u32[]{:S(2)}) collective-permute-start(f32[256,128]{1,0:T(8,128)S(1)} %get-tuple-element.77), channel_id=1, source_target_pairs={{0,6},{1,7},{2,4},{3,5},{4,2},{5,3},{6,0},{7,1},{8,14},{9,15},{10,... | collective-permute-start | bytes 393224 | tf_op jit(solution)/shard_map/ppermute | solution.py:260
  36.6 7.9 %collective-permute-start.11 = (f32[272,128]{1,0:T(8,128)S(1)}, f32[272,128]{1,0:T(8,128)S(1)}, u32[]{:S(2)}, u32[]{:S(2)}) collective-permute-start(f32[272,128]{1,0:T(8,128)S(1)} %get-tuple-element.91), channel_id=1, source_target_pairs={{0,4},{1,5},{2,6},{3,7},{4,0},{5,1},{6,2},{7,3},{8,12},{9,13},{10,... | collective-permute-start | bytes 417800 | tf_op jit(solution)/shard_map/ppermute | solution.py:260
  37.0 7.5 %collective-permute-start.12 = (f32[272,128]{1,0:T(8,128)S(1)}, f32[272,128]{1,0:T(8,128)S(1)}, u32[]{:S(2)}, u32[]{:S(2)}) collective-permute-start(f32[272,128]{1,0:T(8,128)S(1)} %get-tuple-element.87.rest_0_), channel_id=1, source_target_pairs={{0,6},{1,7},{2,4},{3,5},{4,2},{5,3},{6,0},{7,1},{8,14},{9,15},{10,... | collective-permute-start | bytes 417800 | tf_op jit(solution)/shard_map/ppermute | solution.py:260
  38.9 7.6 %collective-permute-start.13 = (f32[272,128]{1,0:T(8,128)S(1)}, f32[272,128]{1,0:T(8,128)S(1)}, u32[]{:S(2)}, u32[]{:S(2)}) collective-permute-start(f32[272,128]{1,0:T(8,128)S(1)} %get-tuple-element.92), channel_id=1, source_target_pairs={{0,2},{1,3},{2,0},{3,1},{4,6},{5,7},{6,4},{7,5},{8,10},{9,11},{10,... | collective-permute-start | bytes 417800 | tf_op jit(solution)/shard_map/ppermute | solution.py:260
  42.4 13.1 %collective-permute-start.9 = (f32[256,1024]{1,0:T(8,128)S(1)}, f32[256,1024]{1,0:T(8,128)S(1)}, u32[]{:S(2)}, u32[]{:S(2)}) collective-permute-start(f32[256,1024]{1,0:T(8,128)S(1)} %get-tuple-element.89), channel_id=1, source_target_pairs={{0,1},{1,0},{2,3},{3,2},{4,5},{5,4},{6,7},{7,6},{8,9},{9,8},{10,11... | collective-permute-start | bytes 3145736 | tf_op jit(solution)/shard_map/ppermute | solution.py:260
  46.7 8.6 %collective-permute-start.14 = (f32[272,128]{1,0:T(8,128)S(1)}, f32[272,128]{1,0:T(8,128)S(1)}, u32[]{:S(2)}, u32[]{:S(2)}) collective-permute-start(f32[272,128]{1,0:T(8,128)S(1)} %pad_maximum_fusion.11), channel_id=1, source_target_pairs={{0,8},{1,9},{2,10},{3,11},{4,12},{5,13},{6,14},{7,15},{8,0},{9,1},... | collective-permute-start | bytes 417800 | tf_op jit(solution)/shard_map/ppermute | solution.py:260
  49.1 6.3 %collective-permute-start.10 = (f32[1024,128]{1,0:T(8,128)S(1)}, f32[1024,128]{1,0:T(8,128)S(1)}, u32[]{:S(2)}, u32[]{:S(2)}) collective-permute-start(f32[1024,128]{1,0:T(8,128)S(1)} %get-tuple-element.90.theirs_ref), channel_id=1, source_target_pairs={{0,1},{1,0},{2,3},{3,2},{4,5},{5,4},{6,7},{7,6},{8,9},{9,8},{10,11... | collective-permute-start | bytes 1572872 | tf_op jit(solution)/shard_map/ppermute | solution.py:260
  55.5 8.1 %collective-permute-start.15 = (f32[256,128]{1,0:T(8,128)S(1)}, f32[256,128]{1,0:T(8,128)S(1)}, u32[]{:S(2)}, u32[]{:S(2)}) collective-permute-start(f32[256,128]{1,0:T(8,128)S(1)} %get-tuple-element.99), channel_id=1, source_target_pairs={{0,2},{1,3},{2,0},{3,1},{4,6},{5,7},{6,4},{7,5},{8,10},{9,11},{10,... | collective-permute-start | bytes 393224 | tf_op jit(solution)/shard_map/ppermute | solution.py:260
  55.9 7.6 %collective-permute-start.16 = (f32[256,128]{1,0:T(8,128)S(1)}, f32[256,128]{1,0:T(8,128)S(1)}, u32[]{:S(2)}, u32[]{:S(2)}) collective-permute-start(f32[256,128]{1,0:T(8,128)S(1)} %get-tuple-element.100), channel_id=1, source_target_pairs={{0,4},{1,5},{2,6},{3,7},{4,0},{5,1},{6,2},{7,3},{8,12},{9,13},{10,... | collective-permute-start | bytes 393224 | tf_op jit(solution)/shard_map/ppermute | solution.py:260
  56.5 7.1 %collective-permute-start.17 = (f32[256,128]{1,0:T(8,128)S(1)}, f32[256,128]{1,0:T(8,128)S(1)}, u32[]{:S(2)}, u32[]{:S(2)}) collective-permute-start(f32[256,128]{1,0:T(8,128)S(1)} %get-tuple-element.94.rest_0_), channel_id=1, source_target_pairs={{0,6},{1,7},{2,4},{3,5},{4,2},{5,3},{6,0},{7,1},{8,14},{9,15},{10,... | collective-permute-start | bytes 393224 | tf_op jit(solution)/shard_map/ppermute | solution.py:260
  61.2 3.1 %collective-permute-start.18 = (f32[8,128]{1,0:T(8,128)S(1)}, f32[8,128]{1,0:T(8,128)S(1)}, u32[]{:S(2)}, u32[]{:S(2)}) collective-permute-start(f32[8,128]{1,0:T(8,128)S(1)} %slice_add_fusion), channel_id=1, source_target_pairs={{0,1},{1,0},{2,3},{3,2},{4,5},{5,4},{6,7},{7,6},{8,9},{9,8},{10,11... | collective-permute-start | bytes 12296 | tf_op jit(solution)/shard_map/ppermute | solution.py:260
  64.4 3.2 %collective-permute-start.19 = (f32[1024,128]{1,0:T(8,128)S(1)}, f32[1024,128]{1,0:T(8,128)S(1)}, u32[]{:S(2)}, u32[]{:S(2)}) collective-permute-start(f32[1024,128]{1,0:T(8,128)S(1)} %get-tuple-element.102), channel_id=1, source_target_pairs={{0,1},{1,0},{2,3},{3,2},{4,5},{5,4},{6,7},{7,6},{8,9},{9,8},{10,11... | collective-permute-start | bytes 1572872 | tf_op jit(solution)/shard_map/ppermute | solution.py:260

commit v8 on v7

--- a/solution.py
+++ b/solution.py
@@ -182,11 +182,12 @@
 def through_norm(local, used, grad, gain, carry):
     attended = local + dot(used, carry.astype(BF16), 1, 0)
     d_norm = grad * gain
-    square = jnp.mean(attended * attended, axis=1, keepdims=True)
-    centre = jnp.mean(d_norm * attended, axis=1, keepdims=True)
-    inverse = lax.rsqrt(square + EPS)
-    total = jnp.sum(grad * (attended * inverse), axis=0, keepdims=True)
-    d_att = ((d_norm - attended * (centre * inverse * inverse)) * inverse).astype(BF16)
+    square = jnp.sum(attended * attended, axis=1, keepdims=True)
+    along = jnp.sum(d_norm * attended, axis=1, keepdims=True)
+    inverse = lax.rsqrt(square * (1.0 / E) + EPS)
+    normed = attended * inverse
+    total = jnp.sum(grad * normed, axis=0, keepdims=True)
+    d_att = ((d_norm - normed * (along * inverse * (1.0 / E))) * inverse).astype(BF16)
     return d_att, dot(used, d_att, 0, 0), total
 
 

time: 69.3 us -> 69.1 us (level)
  no operation moved by 1% of the time
where the time goes in v8:
time: 69.1 us; the launch traced here: 68.7 us
  starting transfers between devices  26.1 us (38%)
  waiting for transfers between devices  20.7 us (30%)
  Pallas kernels  19.5 us (28%)
  other arithmetic  0.96 us (1%)
  between operations  0.89 us (1%)
    ppermute x20, starting transfers between devices, swap(): return lax.ppermute(block, 'ctx', [(i, i ^ distance) for i in range(count)])  26.1 us
    ppermute x20, waiting for transfers between devices, swap(): return lax.ppermute(block, 'ctx', [(i, i ^ distance) for i in range(count)])  20.7 us
    pallas_call x2, Pallas kernels, spread_of(): call(spread_kernel, [VMEM] * 8 + [ANY] * (1 + len(done)), [grad, single,...  6.14 us
    pallas_call x2, Pallas kernels, final_of(): call(final_kernel, [VMEM] * 6 + [ANY] * len(grads), [grad, grad], [stagin...  2.66 us
    pallas_call x1, Pallas kernels, other_local_of(): call(other_local_kernel, [ANY] * 2 + [VMEM] * 4 + [ANY], [held(3 * tokens...  2.66 us
    pallas_call x1, Pallas kernels, local_of(): call(local_kernel, [ANY] * 3 + [VMEM] * 3 + [ANY], [single, narrow, narro...  2.36 us
    pallas_call x1, Pallas kernels, chain(): call(middle_kernel, [VMEM] * 8, [narrow, single, held(rows, E), held(rows...  2.13 us
    pallas_call x1, Pallas kernels, shards(): call(send_state_kernel, [ANY] * 3, [held(rows + FLAG, E), narrow, narrow,...  1.79 us
  transfers between devices with their start and end apart: 20, of which 10 were waited for; matrix products, arithmetic and copies ran while one was open for 2% of the time, Pallas kernels for 21%

profile of v8, /device:TPU:1, one launch (start us, length us, event | category | flops | bytes accessed | tf_op | source)
XLA Modules:
  0.0 68.7 jit_solution(9055676333624752379)
XLA Ops:
  0.6 1.8 %shard_map.93 = (f32[1032,128]{1,0:T(8,128)S(1)}, bf16[256,1024]{1,0:T(8,128)(2,1)S(1)}, bf16[256,1024]{1,0:T(8,128)(2,1)S(1)}, s32[256,128]{1,0:T(8,128)S(1)}, ...) custom-call(s32[2,2]{1,0:T(2,128)} %bounds_hbm.1, ...), custom_call_target="tpu_custom_call" | custom-call | tf_op jit(solution)/shard_map/pallas_call | solution.py:383
  2.6 1.8 %shard_map.94 = (f32[1024,128]{1,0:T(8,128)S(1)}, bf16[256,1024]{1,0:T(8,128)(2,1)S(1)}, bf16[256,1024]{1,0:T(8,128)(2,1)S(1)}) custom-call(bf16[256,2048]{1,0:T(8,128)(2,1)} %k_hbm.3, bf16[256,2048]{1,0:T(8,128)(2,1)} %v_hbm.3, bf16[256,128]{1,0:T(8,128)(2,1)S(1)} %get-tuple-element.61.tail_ref), custom_call_target="tpu_custom_call" | custom-call | tf_op jit(solution)/shard_map/pallas_call | solution.py:390
  4.6 2.7 %collective-permute-start.1 = (f32[264,128]{1,0:T(8,128)S(1)}, f32[264,128]{1,0:T(8,128)S(1)}, u32[]{:S(2)}, u32[]{:S(2)}) collective-permute-start(f32[264,128]{1,0:T(8,128)S(1)} %get-tuple-element.69), channel_id=1, source_target_pairs={{0,2},{1,3},{2,0},{3,1},{4,6},{5,7},{6,4},{7,5},{8,10},{9,11},{10,... | collective-permute-start | bytes 405512 | tf_op jit(solution)/shard_map/ppermute | solution.py:261
  7.3 1.3 %collective-permute-start.2 = (f32[264,128]{1,0:T(8,128)S(1)}, f32[264,128]{1,0:T(8,128)S(1)}, u32[]{:S(2)}, u32[]{:S(2)}) collective-permute-start(f32[264,128]{1,0:T(8,128)S(1)} %get-tuple-element.70), channel_id=1, source_target_pairs={{0,4},{1,5},{2,6},{3,7},{4,0},{5,1},{6,2},{7,3},{8,12},{9,13},{10,... | collective-permute-start | bytes 405512 | tf_op jit(solution)/shard_map/ppermute | solution.py:261
  8.6 2.7 %shard_map.95 = (f32[768,1024]{1,0:T(8,128)S(1)}, bf16[256,1024]{1,0:T(8,128)(2,1)S(1)}) custom-call(bf16[256,2048]{1,0:T(8,128)(2,1)} %q_hbm.3, bf16[256,2048]{1,0:T(8,128)(2,1)} %g_hbm.3, bf16[256,1024]{1,0:T(8,128)(2,1)S(1)} %get-tuple-element.56.k_ref, bf16[256,1024]{1,0:T(8,128)(2,1)S(1)} %get-tuple-element.57.v_ref, ...), custom_call_target="tpu_custom_call" | custom-call | tf_op jit(solution)/shard_map/pallas_call | solution.py:398
  11.3 0.8 %collective-permute-done.2 = f32[264,128]{1,0:T(8,128)S(1)} collective-permute-done((f32[264,128]{1,0:T(8,128)S(1)}, f32[264,128]{1,0:T(8,128)S(1)}, u32[]{:S(2)}, u32[]{:S(2)}) %collective-permute-start.2) | collective-permute-done | bytes 135200 | tf_op jit(solution)/shard_map/ppermute | solution.py:261
  12.1 2.8 %collective-permute-done.3 = f32[264,128]{1,0:T(8,128)S(1)} collective-permute-done((f32[264,128]{1,0:T(8,128)S(1)}, f32[264,128]{1,0:T(8,128)S(1)}, u32[]{:S(2)}, u32[]{:S(2)}) %collective-permute-start.3) | collective-permute-done | bytes 135200 | tf_op jit(solution)/shard_map/ppermute | solution.py:261
  15.0 2.6 %collective-permute-start.4 = (f32[264,128]{1,0:T(8,128)S(1)}, f32[264,128]{1,0:T(8,128)S(1)}, u32[]{:S(2)}, u32[]{:S(2)}) collective-permute-start(f32[264,128]{1,0:T(8,128)S(1)} %pad_maximum_fusion.12._), channel_id=1, source_target_pairs={{0,8},{1,9},{2,10},{3,11},{4,12},{5,13},{6,14},{7,15},{8,0},{9,1},... | collective-permute-start | bytes 405512 | tf_op jit(solution)/shard_map/ppermute | solution.py:261
  17.7 2.4 %shard_map.96 = (f32[256,1024]{1,0:T(8,128)S(1)}, bf16[256,1024]{1,0:T(8,128)(2,1)S(1)}, bf16[256,1024]{1,0:T(8,128)(2,1)S(1)}, f32[1,2048]{1,0:T(1,128)S(1)}) custom-call(bf16[256,2048]{1,0:T(8,128)(2,1)} %q_hbm.3, bf16[256,2048]{1,0:T(8,128)(2,1)} %g_hbm.3, f32[1,2048]{1,0:T(1,128)} %bitcast.60, bf16[256,1024]{1,0:T(8,128)(2,1)S(1)} %get-tuple-element.67.k_ref, ...), custom_call_target="tpu_custom_call" | custom-call | tf_op jit(solution)/shard_map/pallas_call | solution.py:413
  20.0 3.7 %collective-permute-done.4 = f32[264,128]{1,0:T(8,128)S(1)} collective-permute-done((f32[264,128]{1,0:T(8,128)S(1)}, f32[264,128]{1,0:T(8,128)S(1)}, u32[]{:S(2)}, u32[]{:S(2)}) %collective-permute-start.4) | collective-permute-done | bytes 135200 | tf_op jit(solution)/shard_map/ppermute | solution.py:261
  23.8 1.5 %collective-permute-start.5 = (f32[768,1024]{1,0:T(8,128)S(1)}, f32[768,1024]{1,0:T(8,128)S(1)}, u32[]{:S(2)}, u32[]{:S(2)}) collective-permute-start(f32[768,1024]{1,0:T(8,128)S(1)} %get-tuple-element.78), channel_id=1, source_target_pairs={{0,1},{1,0},{2,3},{3,2},{4,5},{5,4},{6,7},{7,6},{8,9},{9,8},{10,11... | collective-permute-start | bytes 9437192 | tf_op jit(solution)/shard_map/ppermute | solution.py:261
  25.3 1.1 %collective-permute-start.6 = (f32[256,128]{1,0:T(8,128)S(1)}, f32[256,128]{1,0:T(8,128)S(1)}, u32[]{:S(2)}, u32[]{:S(2)}) collective-permute-start(f32[256,128]{1,0:T(8,128)S(1)} %get-tuple-element.79), channel_id=1, source_target_pairs={{0,2},{1,3},{2,0},{3,1},{4,6},{5,7},{6,4},{7,5},{8,10},{9,11},{10,... | collective-permute-start | bytes 393224 | tf_op jit(solution)/shard_map/ppermute | solution.py:261
  26.8 1.2 %collective-permute-start.8 = (f32[256,128]{1,0:T(8,128)S(1)}, f32[256,128]{1,0:T(8,128)S(1)}, u32[]{:S(2)}, u32[]{:S(2)}) collective-permute-start(f32[256,128]{1,0:T(8,128)S(1)} %get-tuple-element.77), channel_id=1, source_target_pairs={{0,6},{1,7},{2,4},{3,5},{4,2},{5,3},{6,0},{7,1},{8,14},{9,15},{10,... | collective-permute-start | bytes 393224 | tf_op jit(solution)/shard_map/ppermute | solution.py:261
  28.0 2.4 %collective-permute-done.6 = f32[256,128]{1,0:T(8,128)S(1)} collective-permute-done((f32[256,128]{1,0:T(8,128)S(1)}, f32[256,128]{1,0:T(8,128)S(1)}, u32[]{:S(2)}, u32[]{:S(2)}) %collective-permute-start.6) | collective-permute-done | bytes 131104 | tf_op jit(solution)/shard_map/ppermute | solution.py:261
  30.4 0.8 %collective-permute-done.7 = f32[256,128]{1,0:T(8,128)S(1)} collective-permute-done((f32[256,128]{1,0:T(8,128)S(1)}, f32[256,128]{1,0:T(8,128)S(1)}, u32[]{:S(2)}, u32[]{:S(2)}) %collective-permute-start.7) | collective-permute-done | bytes 131104 | tf_op jit(solution)/shard_map/ppermute | solution.py:261
  31.1 2.9 %collective-permute-done.8 = f32[256,128]{1,0:T(8,128)S(1)} collective-permute-done((f32[256,128]{1,0:T(8,128)S(1)}, f32[256,128]{1,0:T(8,128)S(1)}, u32[]{:S(2)}, u32[]{:S(2)}) %collective-permute-start.8) | collective-permute-done | bytes 131104 | tf_op jit(solution)/shard_map/ppermute | solution.py:261
  34.2 2.1 %shard_map.97 = (bf16[256,1024]{1,0:T(8,128)(2,1)S(1)}, f32[256,1024]{1,0:T(8,128)S(1)}, f32[1024,128]{1,0:T(8,128)S(1)}, f32[1024,128]{1,0:T(8,128)S(1)}, f32[8,128]{1,0:T(8,128)S(1)}) custom-call(bf16[256,1024]{1,0:T(8,128)(2,1)S(1)} %get-tuple-element.72.q_ref, bf16[256,1024]{1,0:T(8,128)(2,1)S(1)} %get-tuple-element.73.g_ref, ...), custom_call_target="tpu_custom_call" | custom-call | tf_op jit(solution)/shard_map/pallas_call | solution.py:469
  36.8 1.9 %collective-permute-start.12 = (f32[272,128]{1,0:T(8,128)S(1)}, f32[272,128]{1,0:T(8,128)S(1)}, u32[]{:S(2)}, u32[]{:S(2)}) collective-permute-start(f32[272,128]{1,0:T(8,128)S(1)} %get-tuple-element.87.rest_0_), channel_id=1, source_target_pairs={{0,6},{1,7},{2,4},{3,5},{4,2},{5,3},{6,0},{7,1},{8,14},{9,15},{10,... | collective-permute-start | bytes 417800 | tf_op jit(solution)/shard_map/ppermute | solution.py:261
  39.1 3.1 %shard_map.98 = (bf16[256,2048]{1,0:T(8,128)(2,1)}, f32[256,1024]{1,0:T(8,128)S(1)}, f32[256,1024]{1,0:T(8,128)S(1)}) custom-call(bf16[256,1024]{1,0:T(8,128)(2,1)S(1)} %get-tuple-element.72.q_ref, bf16[256,1024]{1,0:T(8,128)(2,1)S(1)} %get-tuple-element.67.k_ref, bf16[256,1024]{1,0:T(8,128)(2,1)S(1)} %get-tuple-element.68.v_ref, ...), custom_call_target="tpu_custom_call" | custom-call | tf_op jit(solution)/shard_map/pallas_call | solution.py:424
  42.2 2.1 %collective-permute-start.9 = (f32[256,1024]{1,0:T(8,128)S(1)}, f32[256,1024]{1,0:T(8,128)S(1)}, u32[]{:S(2)}, u32[]{:S(2)}) collective-permute-start(f32[256,1024]{1,0:T(8,128)S(1)} %get-tuple-element.89), channel_id=1, source_target_pairs={{0,1},{1,0},{2,3},{3,2},{4,5},{5,4},{6,7},{7,6},{8,9},{9,8},{10,11... | collective-permute-start | bytes 3145736 | tf_op jit(solution)/shard_map/ppermute | solution.py:261
  44.3 2.0 %collective-permute-done.13 = f32[272,128]{1,0:T(8,128)S(1)} collective-permute-done((f32[272,128]{1,0:T(8,128)S(1)}, f32[272,128]{1,0:T(8,128)S(1)}, u32[]{:S(2)}, u32[]{:S(2)}) %collective-permute-start.13) | collective-permute-done | bytes 139296 | tf_op jit(solution)/shard_map/ppermute | solution.py:261
  46.5 2.4 %collective-permute-start.14 = (f32[272,128]{1,0:T(8,128)S(1)}, f32[272,128]{1,0:T(8,128)S(1)}, u32[]{:S(2)}, u32[]{:S(2)}) collective-permute-start(f32[272,128]{1,0:T(8,128)S(1)} %pad_maximum_fusion.11), channel_id=1, source_target_pairs={{0,8},{1,9},{2,10},{3,11},{4,12},{5,13},{6,14},{7,15},{8,0},{9,1},... | collective-permute-start | bytes 417800 | tf_op jit(solution)/shard_map/ppermute | solution.py:261
  48.9 1.8 %collective-permute-start.10 = (f32[1024,128]{1,0:T(8,128)S(1)}, f32[1024,128]{1,0:T(8,128)S(1)}, u32[]{:S(2)}, u32[]{:S(2)}) collective-permute-start(f32[1024,128]{1,0:T(8,128)S(1)} %get-tuple-element.90.theirs_ref), channel_id=1, source_target_pairs={{0,1},{1,0},{2,3},{3,2},{4,5},{5,4},{6,7},{7,6},{8,9},{9,8},{10,11... | collective-permute-start | bytes 1572872 | tf_op jit(solution)/shard_map/ppermute | solution.py:261
  50.7 4.5 %collective-permute-done.14 = f32[272,128]{1,0:T(8,128)S(1)} collective-permute-done((f32[272,128]{1,0:T(8,128)S(1)}, f32[272,128]{1,0:T(8,128)S(1)}, u32[]{:S(2)}, u32[]{:S(2)}) %collective-permute-start.14) | collective-permute-done | bytes 139296 | tf_op jit(solution)/shard_map/ppermute | solution.py:261
  56.3 1.7 %collective-permute-start.17 = (f32[256,128]{1,0:T(8,128)S(1)}, f32[256,128]{1,0:T(8,128)S(1)}, u32[]{:S(2)}, u32[]{:S(2)}) collective-permute-start(f32[256,128]{1,0:T(8,128)S(1)} %get-tuple-element.94.rest_0_), channel_id=1, source_target_pairs={{0,6},{1,7},{2,4},{3,5},{4,2},{5,3},{6,0},{7,1},{8,14},{9,15},{10,... | collective-permute-start | bytes 393224 | tf_op jit(solution)/shard_map/ppermute | solution.py:261
  58.0 3.1 %shard_map.99 = (bf16[256,2048]{1,0:T(8,128)(2,1)}, f32[256,1024]{1,0:T(8,128)S(1)}, f32[256,1024]{1,0:T(8,128)S(1)}) custom-call(bf16[256,1024]{1,0:T(8,128)(2,1)S(1)} %get-tuple-element.66.q_ref, bf16[256,1024]{1,0:T(8,128)(2,1)S(1)} %get-tuple-element.56.k_ref, bf16[256,1024]{1,0:T(8,128)(2,1)S(1)} %get-tuple-element.57.v_ref, ...), custom_call_target="tpu_custom_call", output_to_operand_aliasing={{0}: (9, {})} | custom-call | tf_op jit(solution)/shard_map/pallas_call | solution.py:424
  61.1 2.3 %collective-permute-start.18 = (f32[8,128]{1,0:T(8,128)S(1)}, f32[8,128]{1,0:T(8,128)S(1)}, u32[]{:S(2)}, u32[]{:S(2)}) collective-permute-start(f32[8,128]{1,0:T(8,128)S(1)} %slice_add_fusion), channel_id=1, source_target_pairs={{0,1},{1,0},{2,3},{3,2},{4,5},{5,4},{6,7},{7,6},{8,9},{9,8},{10,11... | collective-permute-start | bytes 12296 | tf_op jit(solution)/shard_map/ppermute | solution.py:261
  63.5 0.7 %collective-permute-done.18 = f32[8,128]{1,0:T(8,128)S(1)} collective-permute-done((f32[8,128]{1,0:T(8,128)S(1)}, f32[8,128]{1,0:T(8,128)S(1)}, u32[]{:S(2)}, u32[]{:S(2)}) %collective-permute-start.18) | collective-permute-done | bytes 4128 | tf_op jit(solution)/shard_map/ppermute | solution.py:261
  64.2 1.2 %collective-permute-start.19 = (f32[1024,128]{1,0:T(8,128)S(1)}, f32[1024,128]{1,0:T(8,128)S(1)}, u32[]{:S(2)}, u32[]{:S(2)}) collective-permute-start(f32[1024,128]{1,0:T(8,128)S(1)} %get-tuple-element.102), channel_id=1, source_target_pairs={{0,1},{1,0},{2,3},{3,2},{4,5},{5,4},{6,7},{7,6},{8,9},{9,8},{10,11... | collective-permute-start | bytes 1572872 | tf_op jit(solution)/shard_map/ppermute | solution.py:261
  65.5 0.6 copy.13
  66.1 1.3 %shard_map.100 = (bf16[256,2048]{1,0:T(8,128)(2,1)}, bf16[256,2048]{1,0:T(8,128)(2,1)}) custom-call(bf16[256,1024]{1,0:T(8,128)(2,1)S(1)} %get-tuple-element.67.k_ref, bf16[256,1024]{1,0:T(8,128)(2,1)S(1)} %get-tuple-element.68.v_ref, f32[256,1024]{1,0:T(8,128)S(1)} %get-tuple-element.88.kp_ref, f32[256,1024]{1,0:T(8,128)S(1)} %get-tuple-element.103.vp_ref, ...), custom_call_target="tpu_custom_call" | custom-call | tf_op jit(solution)/shard_map/pallas_call | solution.py:452
  67.4 1.3 %shard_map.101 = (bf16[256,2048]{1,0:T(8,128)(2,1)}, bf16[256,2048]{1,0:T(8,128)(2,1)}) custom-call(bf16[256,1024]{1,0:T(8,128)(2,1)S(1)} %get-tuple-element.56.k_ref, bf16[256,1024]{1,0:T(8,128)(2,1)S(1)} %get-tuple-element.57.v_ref, f32[256,1024]{1,0:T(8,128)S(1)} %get-tuple-element.97.kp_ref, ...), custom_call_target="tpu_custom_call", output_to_operand_aliasing={{0}: (6, {}), {1}: (7, {})} | custom-call | tf_op jit(solution)/shard_map/pallas_call | solution.py:452
  (48 shorter events, 3.4 us)
Async XLA Ops:
  2.4 2.0 %collective-permute-start = (f32[1032,128]{1,0:T(8,128)S(1)}, f32[1032,128]{1,0:T(8,128)S(1)}, u32[]{:S(2)}, u32[]{:S(2)}) collective-permute-start(f32[1032,128]{1,0:T(8,128)S(1)} %get-tuple-element.63), channel_id=1, source_target_pairs={{0,1},{1,0},{2,3},{3,2},{4,5},{5,4},{6,7},{7,6},{8,9},{9,8},{10,11... | collective-permute-start | bytes 1585160 | tf_op jit(solution)/shard_map/ppermute | solution.py:261
  4.6 6.7 %collective-permute-start.1 = (f32[264,128]{1,0:T(8,128)S(1)}, f32[264,128]{1,0:T(8,128)S(1)}, u32[]{:S(2)}, u32[]{:S(2)}) collective-permute-start(f32[264,128]{1,0:T(8,128)S(1)} %get-tuple-element.69), channel_id=1, source_target_pairs={{0,2},{1,3},{2,0},{3,1},{4,6},{5,7},{6,4},{7,5},{8,10},{9,11},{10,... | collective-permute-start | bytes 405512 | tf_op jit(solution)/shard_map/ppermute | solution.py:261
  7.3 4.8 %collective-permute-start.2 = (f32[264,128]{1,0:T(8,128)S(1)}, f32[264,128]{1,0:T(8,128)S(1)}, u32[]{:S(2)}, u32[]{:S(2)}) collective-permute-start(f32[264,128]{1,0:T(8,128)S(1)} %get-tuple-element.70), channel_id=1, source_target_pairs={{0,4},{1,5},{2,6},{3,7},{4,0},{5,1},{6,2},{7,3},{8,12},{9,13},{10,... | collective-permute-start | bytes 405512 | tf_op jit(solution)/shard_map/ppermute | solution.py:261
  8.6 6.3 %collective-permute-start.3 = (f32[264,128]{1,0:T(8,128)S(1)}, f32[264,128]{1,0:T(8,128)S(1)}, u32[]{:S(2)}, u32[]{:S(2)}) collective-permute-start(f32[264,128]{1,0:T(8,128)S(1)} %get-tuple-element.65._), channel_id=1, source_target_pairs={{0,6},{1,7},{2,4},{3,5},{4,2},{5,3},{6,0},{7,1},{8,14},{9,15},{10,... | collective-permute-start | bytes 405512 | tf_op jit(solution)/shard_map/ppermute | solution.py:261
  15.0 8.7 %collective-permute-start.4 = (f32[264,128]{1,0:T(8,128)S(1)}, f32[264,128]{1,0:T(8,128)S(1)}, u32[]{:S(2)}, u32[]{:S(2)}) collective-permute-start(f32[264,128]{1,0:T(8,128)S(1)} %pad_maximum_fusion.12._), channel_id=1, source_target_pairs={{0,8},{1,9},{2,10},{3,11},{4,12},{5,13},{6,14},{7,15},{8,0},{9,1},... | collective-permute-start | bytes 405512 | tf_op jit(solution)/shard_map/ppermute | solution.py:261
  23.8 10.3 %collective-permute-start.5 = (f32[768,1024]{1,0:T(8,128)S(1)}, f32[768,1024]{1,0:T(8,128)S(1)}, u32[]{:S(2)}, u32[]{:S(2)}) collective-permute-start(f32[768,1024]{1,0:T(8,128)S(1)} %get-tuple-element.78), channel_id=1, source_target_pairs={{0,1},{1,0},{2,3},{3,2},{4,5},{5,4},{6,7},{7,6},{8,9},{9,8},{10,11... | collective-permute-start | bytes 9437192 | tf_op jit(solution)/shard_map/ppermute | solution.py:261
  25.3 5.1 %collective-permute-start.6 = (f32[256,128]{1,0:T(8,128)S(1)}, f32[256,128]{1,0:T(8,128)S(1)}, u32[]{:S(2)}, u32[]{:S(2)}) collective-permute-start(f32[256,128]{1,0:T(8,128)S(1)} %get-tuple-element.79), channel_id=1, source_target_pairs={{0,2},{1,3},{2,0},{3,1},{4,6},{5,7},{6,4},{7,5},{8,10},{9,11},{10,... | collective-permute-start | bytes 393224 | tf_op jit(solution)/shard_map/ppermute | solution.py:261
  26.4 4.7 %collective-permute-start.7 = (f32[256,128]{1,0:T(8,128)S(1)}, f32[256,128]{1,0:T(8,128)S(1)}, u32[]{:S(2)}, u32[]{:S(2)}) collective-permute-start(f32[256,128]{1,0:T(8,128)S(1)} %get-tuple-element.80), channel_id=1, source_target_pairs={{0,4},{1,5},{2,6},{3,7},{4,0},{5,1},{6,2},{7,3},{8,12},{9,13},{10,... | collective-permute-start | bytes 393224 | tf_op jit(solution)/shard_map/ppermute | solution.py:261
  26.8 7.3 %collective-permute-start.8 = (f32[256,128]{1,0:T(8,128)S(1)}, f32[256,128]{1,0:T(8,128)S(1)}, u32[]{:S(2)}, u32[]{:S(2)}) collective-permute-start(f32[256,128]{1,0:T(8,128)S(1)} %get-tuple-element.77), channel_id=1, source_target_pairs={{0,6},{1,7},{2,4},{3,5},{4,2},{5,3},{6,0},{7,1},{8,14},{9,15},{10,... | collective-permute-start | bytes 393224 | tf_op jit(solution)/shard_map/ppermute | solution.py:261
  36.4 7.9 %collective-permute-start.11 = (f32[272,128]{1,0:T(8,128)S(1)}, f32[272,128]{1,0:T(8,128)S(1)}, u32[]{:S(2)}, u32[]{:S(2)}) collective-permute-start(f32[272,128]{1,0:T(8,128)S(1)} %get-tuple-element.91), channel_id=1, source_target_pairs={{0,4},{1,5},{2,6},{3,7},{4,0},{5,1},{6,2},{7,3},{8,12},{9,13},{10,... | collective-permute-start | bytes 417800 | tf_op jit(solution)/shard_map/ppermute | solution.py:261
  36.8 7.5 %collective-permute-start.12 = (f32[272,128]{1,0:T(8,128)S(1)}, f32[272,128]{1,0:T(8,128)S(1)}, u32[]{:S(2)}, u32[]{:S(2)}) collective-permute-start(f32[272,128]{1,0:T(8,128)S(1)} %get-tuple-element.87.rest_0_), channel_id=1, source_target_pairs={{0,6},{1,7},{2,4},{3,5},{4,2},{5,3},{6,0},{7,1},{8,14},{9,15},{10,... | collective-permute-start | bytes 417800 | tf_op jit(solution)/shard_map/ppermute | solution.py:261
  38.8 7.6 %collective-permute-start.13 = (f32[272,128]{1,0:T(8,128)S(1)}, f32[272,128]{1,0:T(8,128)S(1)}, u32[]{:S(2)}, u32[]{:S(2)}) collective-permute-start(f32[272,128]{1,0:T(8,128)S(1)} %get-tuple-element.92), channel_id=1, source_target_pairs={{0,2},{1,3},{2,0},{3,1},{4,6},{5,7},{6,4},{7,5},{8,10},{9,11},{10,... | collective-permute-start | bytes 417800 | tf_op jit(solution)/shard_map/ppermute | solution.py:261
  42.2 13.0 %collective-permute-start.9 = (f32[256,1024]{1,0:T(8,128)S(1)}, f32[256,1024]{1,0:T(8,128)S(1)}, u32[]{:S(2)}, u32[]{:S(2)}) collective-permute-start(f32[256,1024]{1,0:T(8,128)S(1)} %get-tuple-element.89), channel_id=1, source_target_pairs={{0,1},{1,0},{2,3},{3,2},{4,5},{5,4},{6,7},{7,6},{8,9},{9,8},{10,11... | collective-permute-start | bytes 3145736 | tf_op jit(solution)/shard_map/ppermute | solution.py:261
  46.5 8.6 %collective-permute-start.14 = (f32[272,128]{1,0:T(8,128)S(1)}, f32[272,128]{1,0:T(8,128)S(1)}, u32[]{:S(2)}, u32[]{:S(2)}) collective-permute-start(f32[272,128]{1,0:T(8,128)S(1)} %pad_maximum_fusion.11), channel_id=1, source_target_pairs={{0,8},{1,9},{2,10},{3,11},{4,12},{5,13},{6,14},{7,15},{8,0},{9,1},... | collective-permute-start | bytes 417800 | tf_op jit(solution)/shard_map/ppermute | solution.py:261
  48.9 6.3 %collective-permute-start.10 = (f32[1024,128]{1,0:T(8,128)S(1)}, f32[1024,128]{1,0:T(8,128)S(1)}, u32[]{:S(2)}, u32[]{:S(2)}) collective-permute-start(f32[1024,128]{1,0:T(8,128)S(1)} %get-tuple-element.90.theirs_ref), channel_id=1, source_target_pairs={{0,1},{1,0},{2,3},{3,2},{4,5},{5,4},{6,7},{7,6},{8,9},{9,8},{10,11... | collective-permute-start | bytes 1572872 | tf_op jit(solution)/shard_map/ppermute | solution.py:261
  55.3 8.1 %collective-permute-start.15 = (f32[256,128]{1,0:T(8,128)S(1)}, f32[256,128]{1,0:T(8,128)S(1)}, u32[]{:S(2)}, u32[]{:S(2)}) collective-permute-start(f32[256,128]{1,0:T(8,128)S(1)} %get-tuple-element.99), channel_id=1, source_target_pairs={{0,2},{1,3},{2,0},{3,1},{4,6},{5,7},{6,4},{7,5},{8,10},{9,11},{10,... | collective-permute-start | bytes 393224 | tf_op jit(solution)/shard_map/ppermute | solution.py:261
  55.8 7.6 %collective-permute-start.16 = (f32[256,128]{1,0:T(8,128)S(1)}, f32[256,128]{1,0:T(8,128)S(1)}, u32[]{:S(2)}, u32[]{:S(2)}) collective-permute-start(f32[256,128]{1,0:T(8,128)S(1)} %get-tuple-element.100), channel_id=1, source_target_pairs={{0,4},{1,5},{2,6},{3,7},{4,0},{5,1},{6,2},{7,3},{8,12},{9,13},{10,... | collective-permute-start | bytes 393224 | tf_op jit(solution)/shard_map/ppermute | solution.py:261
  56.3 7.1 %collective-permute-start.17 = (f32[256,128]{1,0:T(8,128)S(1)}, f32[256,128]{1,0:T(8,128)S(1)}, u32[]{:S(2)}, u32[]{:S(2)}) collective-permute-start(f32[256,128]{1,0:T(8,128)S(1)} %get-tuple-element.94.rest_0_), channel_id=1, source_target_pairs={{0,6},{1,7},{2,4},{3,5},{4,2},{5,3},{6,0},{7,1},{8,14},{9,15},{10,... | collective-permute-start | bytes 393224 | tf_op jit(solution)/shard_map/ppermute | solution.py:261
  61.1 3.1 %collective-permute-start.18 = (f32[8,128]{1,0:T(8,128)S(1)}, f32[8,128]{1,0:T(8,128)S(1)}, u32[]{:S(2)}, u32[]{:S(2)}) collective-permute-start(f32[8,128]{1,0:T(8,128)S(1)} %slice_add_fusion), channel_id=1, source_target_pairs={{0,1},{1,0},{2,3},{3,2},{4,5},{5,4},{6,7},{7,6},{8,9},{9,8},{10,11... | collective-permute-start | bytes 12296 | tf_op jit(solution)/shard_map/ppermute | solution.py:261
  64.2 3.2 %collective-permute-start.19 = (f32[1024,128]{1,0:T(8,128)S(1)}, f32[1024,128]{1,0:T(8,128)S(1)}, u32[]{:S(2)}, u32[]{:S(2)}) collective-permute-start(f32[1024,128]{1,0:T(8,128)S(1)} %get-tuple-element.102), channel_id=1, source_target_pairs={{0,1},{1,0},{2,3},{3,2},{4,5},{5,4},{6,7},{7,6},{8,9},{9,8},{10,11... | collective-permute-start | bytes 1572872 | tf_op jit(solution)/shard_map/ppermute | solution.py:261
